TPU v7x, 32 devices: a whole 2x2x4 slice. The times are simulated.
32 devices in a mesh: dp: 2 (over core), seq: 16 (over z, y, x).
Axes of the slice: x: 2, y: 2, z: 4, core: 2. Of those that a mesh axis runs over, the one named last changes fastest.
Arguments:
- siblings: int32 [2, 32, 16], P('dp', 'seq'), may hold values from 0 to 31, all different within a row
- queries: bfloat16 [2, 32, 512, 2560], P('dp', 'seq'), may hold values from -6 to 6
- grad_out: bfloat16 [2, 32, 512, 2560], P('dp', 'seq'), may hold values from -6 to 6
- keys_in: bfloat16 [2, 32, 16, 512], P('dp', 'seq'), may hold values from -4 to 4
- input_values: bfloat16 [2, 32, 16, 512], P('dp', 'seq'), may hold values from -6 to 6
- summary: bfloat16 [2, 32, 16, 5120], P('dp', 'seq'), may hold values from -6 to 6
Outputs:
- query_gradient: bfloat16 [2, 32, 512, 2560], P('dp', 'seq')
- kv_weight_grad: float32 [5120, 1024], P(('dp', 'seq'))
Inputs may be any that keep to these rules, and one draw needn't show every extreme that they name: `siblings`: the 16 entries of one completion's list are distinct completions of the same prompt.
All inputs are finite; a program needn't handle non-finite values.
Results may differ from a plain program's by a relative error of at most 0.012.
Values may be sent and summed in bfloat16 or wider, within the bound.
No kernel may reach another device: no remote copies, remote signals or barrier semaphores. Data moves between devices by JAX's collectives and lax.ppermute only.
A program may use at most 192 MiB of HBM per device.

v0:
```python
import math

import jax
import jax.numpy as jnp
from jax import lax
from jax.sharding import PartitionSpec as P

HEAD_SIZE = 128


def group_grads(query_tile_block, incoming_gradient, key_tile_block, value_tile_block, scaling):
    scores = (
        jnp.einsum(
            "ctrd,cld->crtl", query_tile_block, key_tile_block, preferred_element_type=jnp.float32
        )
        * scaling
    )
    largest = jnp.max(scores, axis=-1, keepdims=True)
    exponent = jnp.exp(scores - largest)
    probability = exponent / jnp.sum(exponent, axis=-1, keepdims=True)
    prob_half = probability.astype(jnp.bfloat16)
    attended = jnp.einsum(
        "crtl,cld->ctrd", prob_half, value_tile_block, preferred_element_type=jnp.float32
    )
    token_delta = jnp.sum(incoming_gradient * attended, axis=-1)
    row_delta = jnp.transpose(token_delta, (0, 2, 1))[..., None]
    prob_grad = jnp.einsum(
        "ctrd,cld->crtl", incoming_gradient, value_tile_block, preferred_element_type=jnp.float32
    )
    score_half = (probability * (prob_grad - row_delta)).astype(jnp.bfloat16)
    query_gradient = (
        jnp.einsum("crtl,cld->ctrd", score_half, key_tile_block, preferred_element_type=jnp.float32)
        * scaling
    )
    key_gradient = (
        jnp.einsum(
            "crtl,ctrd->cld", score_half, query_tile_block, preferred_element_type=jnp.float32
        )
        * scaling
    )
    value_gradient = jnp.einsum(
        "crtl,ctrd->cld", prob_half, incoming_gradient, preferred_element_type=jnp.float32
    )
    return (query_gradient, key_gradient, value_gradient)


def per_device(siblings, queries, grad_out, keys_in, input_values, summary):
    keys_all, values_all = (
        lax.all_gather(keys_in, "seq", axis=1, tiled=True),
        lax.all_gather(input_values, "seq", axis=1, tiled=True),
    )
    sibling = siblings[0]
    own_count, row_length = (queries.shape[1], queries.shape[2])
    everyone = keys_all.shape[1]
    neighbours, positions, key_value_width = (sibling.shape[1], keys_in.shape[2], keys_in.shape[3])
    kv_heads = key_value_width // HEAD_SIZE
    group_span = queries.shape[3] // kv_heads
    group_size = group_span // HEAD_SIZE
    scaling = 1.0 / math.sqrt(HEAD_SIZE)
    key_rows = keys_all[0][sibling].reshape(own_count, neighbours * positions, key_value_width)
    value_rows = values_all[0][sibling].reshape(own_count, neighbours * positions, key_value_width)
    query_parts, key_parts, value_parts = ([], [], [])
    for kv_head in range(kv_heads):
        query_tile_block = queries[
            0, :, :, kv_head * group_span : (kv_head + 1) * group_span
        ].reshape(own_count, row_length, group_size, HEAD_SIZE)
        incoming_gradient = grad_out[
            0, :, :, kv_head * group_span : (kv_head + 1) * group_span
        ].reshape(own_count, row_length, group_size, HEAD_SIZE)
        key_tile_block = key_rows[:, :, kv_head * HEAD_SIZE : (kv_head + 1) * HEAD_SIZE]
        value_tile_block = value_rows[:, :, kv_head * HEAD_SIZE : (kv_head + 1) * HEAD_SIZE]
        query_gradient, key_gradient, value_gradient = group_grads(
            query_tile_block, incoming_gradient, key_tile_block, value_tile_block, scaling
        )
        query_parts.append(query_gradient.reshape(own_count, row_length, group_span))
        key_parts.append(key_gradient)
        value_parts.append(value_gradient)
    query_out = jnp.concatenate(query_parts, axis=-1).astype(jnp.bfloat16)
    key_gradient = jnp.concatenate(key_parts, axis=-1).reshape(
        own_count * neighbours, positions * key_value_width
    )
    value_gradient = jnp.concatenate(value_parts, axis=-1).reshape(
        own_count * neighbours, positions * key_value_width
    )
    targets = sibling.reshape(-1)
    placing = (targets[:, None] == jnp.arange(everyone, dtype=jnp.int32)[None, :]).astype(
        jnp.float32
    )
    key_buffer = jnp.dot(placing.T, key_gradient, precision=lax.Precision.HIGHEST)
    value_buffer = jnp.dot(placing.T, value_gradient, precision=lax.Precision.HIGHEST)
    owner_keys, owner_values = (
        lax.psum_scatter(key_buffer, "seq", scatter_dimension=0, tiled=True),
        lax.psum_scatter(value_buffer, "seq", scatter_dimension=0, tiled=True),
    )
    grads_half = jnp.concatenate(
        [
            owner_keys.astype(jnp.bfloat16).reshape(own_count * positions, key_value_width),
            owner_values.astype(jnp.bfloat16).reshape(own_count * positions, key_value_width),
        ],
        axis=1,
    )
    hidden = summary[0].reshape(own_count * positions, summary.shape[3])
    column_share = lax.all_to_all(hidden, ("dp", "seq"), split_axis=1, concat_axis=0, tiled=True)
    weight_grad = jnp.einsum(
        "sd,sk->dk",
        column_share,
        lax.all_gather(grads_half, ("dp", "seq"), axis=0, tiled=True),
        preferred_element_type=jnp.float32,
    )
    return (query_out[None], weight_grad)


def solution(mesh):
    placed = (
        P("dp", "seq", None),
        P("dp", "seq", None, None),
        P("dp", "seq", None, None),
        P("dp", "seq", None, None),
        P("dp", "seq", None, None),
        P("dp", "seq", None, None),
    )
    return jax.shard_map(
        per_device,
        mesh=mesh,
        in_specs=placed,
        out_specs=(P("dp", "seq", None, None), P(("dp", "seq"), None)),
        check_vma=False,
    )
```

profile of v0, /device:TPU:0, one launch (start us, length us, event | category | flops | bytes accessed | tf_op | source)
XLA Modules:
  0.0 357.1 jit_solution(10787800439655643126)
XLA Ops:
  7.2 0.8 eq.15
  8.0 0.7 compare_select_fusion
  8.8 45.6 %all_gather.9 = bf16[1,32,16,512]{3,2,0,1:T(8,128)(2,1)S(1)} all-gather(bf16[1,2,16,512]{3,2,0,1:T(8,128)(2,1)} %bitcast.358), channel_id=1, replica_groups=mesh['dp'=2,'seq'=16] {'seq'}, dimensions={1}, use_global_device_ids=true | all-gather | bytes 557056 | tf_op jit(solution)/shard_map/all_gather | solution.py:49
  54.3 38.8 %all_gather.10 = bf16[1,32,16,512]{3,2,0,1:T(8,128)(2,1)S(1)} all-gather(bf16[1,2,16,512]{3,2,0,1:T(8,128)(2,1)} %bitcast.359), channel_id=1, replica_groups=mesh['dp'=2,'seq'=16] {'seq'}, dimensions={1}, use_global_device_ids=true | all-gather | bytes 557056 | tf_op jit(solution)/shard_map/all_gather | solution.py:50
  93.7 1.4 gather_fusion.1
  95.1 4.5 %fusion.68 = (bf16[1,2,512,640]{3,2,1,0:T(8,128)(2,1)}, bf16[1,2,512,640]{3,2,1,0:T(8,128)(2,1)}, bf16[1,2,512,640]{3,2,1,0:T(8,128)(2,1)S(1)}, bf16[1,2,512,640]{3,2,1,0:T(8,128)(2,1)S(1)}) fusion(bf16[1,2,512,2560]{3,2,1,0:T(8,128)(2,1)} %param.7), kind=kLoop, calls=%fused_computation.108 | loop fusion | bytes 10485760 | tf_op jit(solution)/shard_map/slice | solution.py:64
  99.6 1.5 copy.210
  101.1 1.5 copy.214
  102.6 4.6 %fusion.69 = (bf16[1,2,512,640]{3,2,1,0:T(8,128)(2,1)}, bf16[1,2,512,640]{3,2,1,0:T(8,128)(2,1)}, bf16[1,2,512,640]{3,2,1,0:T(8,128)(2,1)S(1)}, bf16[1,2,512,640]{3,2,1,0:T(8,128)(2,1)}) fusion(bf16[1,2,512,2560]{3,2,1,0:T(8,128)(2,1)} %param.8), kind=kLoop, calls=%fused_computation.109 | loop fusion | bytes 10485760 | tf_op jit(solution)/shard_map/slice | solution.py:67
  107.2 0.6 copy.211
  107.8 1.6 copy.215
  109.4 5.4 %fusion.70 = (f32[2,5,512]{2,1,0:T(8,128)S(1)}, f32[2,5,512,256]{2,3,1,0:T(8,128)}) fusion(bf16[2,512,5,128]{1,3,2,0:T(8,128)(2,1)} %bitcast.320, bf16[2,256,512]{2,1,0:T(8,128)(2,1)S(1)} %bitcast.336), kind=kOutput, calls=%fused_computation.110 | convolution fusion | flops 339476736 | bytes 6705152 | tf_op jit(solution)/shard_map/sub | solution.py:19
  114.8 3.2 fusion.43
  118.1 1.0 convolution_bitcast_fusion.1
  119.0 1.5 fusion.32
  120.6 5.4 %fusion.72 = (f32[2,5,512]{2,1,0:T(8,128)S(1)}, f32[2,5,512,256]{2,3,1,0:T(8,128)}) fusion(bf16[2,512,5,128]{1,3,2,0:T(8,128)(2,1)} %bitcast.318, bf16[2,256,512]{2,1,0:T(8,128)(2,1)S(1)} %bitcast.337), kind=kOutput, calls=%fused_computation.112 | convolution fusion | flops 339476736 | bytes 6705152 | tf_op jit(solution)/shard_map/sub | solution.py:19
  126.0 3.2 fusion.41
  129.2 2.1 fusion.34
  131.4 1.7 convolution_bitcast_fusion.3
  133.1 2.5 copy.212
  135.5 2.4 copy.213
  137.9 5.4 %fusion.71 = (f32[2,5,512]{2,1,0:T(8,128)S(1)}, f32[2,5,512,256]{2,3,1,0:T(8,128)}) fusion(bf16[2,512,5,128]{1,3,2,0:T(8,128)(2,1)} %bitcast.324, bf16[2,256,512]{2,1,0:T(8,128)(2,1)S(1)} %bitcast.338), kind=kOutput, calls=%fused_computation.111 | convolution fusion | flops 339476736 | bytes 6705152 | tf_op jit(solution)/shard_map/sub | solution.py:19
  143.4 3.3 fusion.42
  146.7 2.1 fusion.33
  148.8 1.7 convolution_bitcast_fusion.2
  150.5 2.4 copy.208
  152.9 2.4 copy.209
  155.4 5.4 %fusion.73 = (f32[2,5,512]{2,1,0:T(8,128)S(1)}, f32[2,5,512,256]{2,3,1,0:T(8,128)}) fusion(bf16[2,512,5,128]{1,3,2,0:T(8,128)(2,1)} %bitcast.322, bf16[2,256,512]{2,1,0:T(8,128)(2,1)S(1)} %bitcast.339), kind=kOutput, calls=%fused_computation.113 | convolution fusion | flops 339476736 | bytes 6705152 | tf_op jit(solution)/shard_map/sub | solution.py:19
  160.7 3.4 fusion.40
  164.2 1.2 fusion.35
  165.4 1.0 convolution_bitcast_fusion.4
  166.4 0.9 fusion.5
  167.3 0.6 copy-done.13
  168.0 1.7 fusion.44
  169.7 0.9 fusion.13
  170.6 1.0 copy-done.12
  171.6 1.7 fusion.46
  173.2 0.7 copy-done.3
  173.9 0.8 fusion.9
  175.2 1.7 fusion.45
  177.5 1.7 fusion.60
  179.2 3.5 fusion.17
  182.7 1.5 copy-done.10
  184.2 1.0 fusion.47
  186.0 1.7 fusion.61
  188.9 98.3 %all-reduce.4 = (bf16[32,8192]{1,0:T(8,128)(2,1)}, bf16[32,8192]{1,0:T(8,128)(2,1)}) all-reduce(f32[32,8192]{1,0:T(8,128)} %fusion.60, f32[32,8192]{1,0:T(8,128)} %fusion.61), channel_id=3, replica_groups=mesh['dp'=2,'seq'=16] {'seq'}, use_global_device_ids=true, to_apply=%region_13.0.clone | all-reduce | flops 524288 | bytes 3145728
  287.2 1.0 dynamic-slice_convert_fusion
  288.2 0.6 reshape.139
  288.9 1.4 pad_maximum_fusion.3
  290.3 1.4 all_to_all.14
  291.7 2.1 copy.143
  293.9 3.5 all-to-all-start
  297.4 1.6 multiply_convert_fusion
  299.0 0.6 copy-done.7
  299.6 1.7 multiply_convert_fusion.2
  301.8 1.7 multiply_convert_fusion.1
  304.0 1.7 multiply_convert_fusion.3
  305.7 0.7 copy.132
  306.4 1.7 copy.130
  308.1 2.4 copy.131
  310.6 2.4 copy.129
  313.0 4.6 %pad_maximum_fusion = bf16[1,2,512,2560]{3,2,1,0:T(8,128)(2,1)} fusion(bf16[1,2,512,640]{3,2,1,0:T(8,128)(2,1)S(1)} %copy.132, bf16[1,2,512,640]{3,2,1,0:T(8,128)(2,1)} %copy.131, bf16[1,2,512,640]{3,2,1,0:T(8,128)(2,1)S(1)} %copy.130, bf16[1,2,512,640]{3,2,1,0:T(8,128)(2,1)} %copy.129), kind=kLoop, calls=%fused_computation.6 | loop fusion | flops 20971520 | bytes 10485760 | tf_op jit(solution)/shard_map/concatenate | solution.py:78
  317.6 29.6 %all-gather.2.cloned.1.call-done = bf16[1024,1024]{1,0:T(8,128)(2,1)} async-done(((bf16[32,1024]{1,0:T(8,128)(2,1)}), bf16[1024,1024]{1,0:T(8,128)(2,1)}) %all-gather.2.cloned.1.call-update) | async-done | bytes 2097168 | tf_op jit(solution)/shard_map/all_gather | solution.py:107
  347.2 3.1 convolution_bitcast_fusion
  (88 shorter events, 4.3 us)
Async XLA Ops:
  7.2 340.0 %all-gather.2.cloned.1.call-start = ((), (), s32[]{:S(2)}) async-start(), calls=%async_computation.1 | async-start | bytes 2162688 | tf_op jit(solution)/shard_map/all_gather | solution.py:107
  93.7 61.7 %copy-start.17 = (bf16[32,16,512]{2,1,0:T(8,128)(2,1)}, bf16[32,16,512]{2,1,0:T(8,128)(2,1)S(1)}, u32[]{:S(2)}) copy-start(bf16[32,16,512]{2,1,0:T(8,128)(2,1)S(1)} %gather_fusion) | copy-start | bytes 1572868
  143.4 3.3 copy-start.28
  143.4 3.4 copy-start.2
  160.7 3.4 copy-start
  160.7 3.4 copy-start.19
  160.7 5.6 %slice-start = ((s8[5242880]{0:T(1024)(128)(4,1)}), s8[4194304]{0:T(1024)(128)(4,1)S(1)}, s32[]{:S(2)}) async-start(s8[5242880]{0:T(1024)(128)(4,1)} %bitcast.330), calls=%async_computation.2 | async-start | bytes 8388608
  164.2 2.2 slice-start.1
  165.4 4.3 %slice-start.2 = ((s8[5242880]{0:T(1024)(128)(4,1)}), s8[4194304]{0:T(1024)(128)(4,1)S(1)}, s32[]{:S(2)}) async-start(s8[5242880]{0:T(1024)(128)(4,1)} %bitcast.332), calls=%async_computation.4 | async-start | bytes 8388608
  166.4 1.6 copy-start.13
  166.4 3.2 slice-start.3
  166.4 3.2 copy-start.26
  167.9 1.7 copy-start.4
  167.9 5.3 %slice-start.4 = ((s8[5242880]{0:T(1024)(128)(4,1)}), s8[4194304]{0:T(1024)(128)(4,1)S(1)}, s32[]{:S(2)}) async-start(s8[5242880]{0:T(1024)(128)(4,1)} %bitcast.334), calls=%async_computation.6 | async-start | bytes 8388608
  169.7 1.9 copy-start.12
  169.7 3.6 slice-start.5
  171.5 3.2 copy-start.6
  171.6 2.3 copy-start.3
  171.6 2.3 copy-start.29
  171.6 2.3 copy-start.30
  173.9 1.3 copy-start.15
  175.2 1.7 copy-start.8
  175.2 1.7 copy-start.20
  175.2 1.7 copy-start.21
  177.3 1.9 copy-start.1
  177.3 1.9 copy-start.27
  179.2 5.0 %copy-start.14 = (bf16[1,2,512,640]{2,3,1,0:T(8,128)(2,1)S(1)}, bf16[1,2,512,640]{2,3,1,0:T(8,128)(2,1)}, u32[]{:S(2)}) copy-start(bf16[1,2,512,640]{2,3,1,0:T(8,128)(2,1)} %copy.208) | copy-start | bytes 3932164
  182.7 1.5 copy-start.10
  184.2 1.0 copy-start.22
  184.2 1.0 copy-start.23
  184.2 1.1 copy-start.24
  185.7 1.9 copy-start.31
  185.9 104.3 %copy-start.25 = (bf16[1,2,16,5120]{3,2,1,0:T(8,128)(2,1)S(1)}, bf16[1,2,16,5120]{3,2,1,0:T(8,128)(2,1)}, u32[]{:S(2)}) copy-start(bf16[1,2,16,5120]{3,2,1,0:T(8,128)(2,1)} %param.11) | copy-start | bytes 983044
  188.8 108.5 %copy-start.5 = (bf16[2,5,512,256]{2,3,1,0:T(8,128)(2,1)S(1)}, bf16[2,5,512,256]{2,3,1,0:T(8,128)(2,1)}, u32[]{:S(2)}) copy-start(bf16[2,5,512,256]{2,3,1,0:T(8,128)(2,1)} %copy-done.4) | copy-start | bytes 7864324
  188.9 108.5 %copy-start.18 = (bf16[32,16,512]{2,1,0:T(8,128)(2,1)S(1)}, bf16[32,16,512]{2,1,0:T(8,128)(2,1)}, u32[]{:S(2)}) copy-start(bf16[32,16,512]{2,1,0:T(8,128)(2,1)} %copy-done.17) | copy-start | bytes 1572868
  293.9 23.7 %all-to-all-start = ((bf16[32,32,160]{2,0,1:T(8,128)(2,1)}), bf16[32,32,160]{2,0,1:T(8,128)(2,1)}, u32[]{:S(2)}, u32[]{:S(2)}) async-start(bf16[32,32,160]{2,0,1:T(8,128)(2,1)} %copy.143), calls=%async_computation | async-start | bytes 1048576 | tf_op jit(solution)/shard_map/all_to_all | solution.py:103
  297.4 2.2 copy-start.7
  299.6 2.2 copy-start.9
  301.8 2.2 copy-start.11
  304.0 1.7 copy-start.16
Sparse Core Ops, SparseCore 0:
  290.4 56.7 all-gather.1
where the time goes:
time: 358 us; the launch traced here: 357 us
  blocking collectives  183 us (51%)
  matrix products  58.9 us (16%)
  local copies, waits for them, and re-layouts  47.2 us (13%)
  waiting for transfers between devices  29.6 us (8%)
  other arithmetic  20 us (6%)
  between operations  15.2 us (4%)
    unnamed x1, blocking collectives  98.3 us
    all_gather x1, blocking collectives, per_device(): lax.all_gather(keys_in, 'seq', axis=1, tiled=True)  45.6 us
    all_gather x1, blocking collectives, per_device(): lax.all_gather(input_values, 'seq', axis=1, tiled=True)  38.8 us
    all_gather x1, waiting for transfers between devices, per_device(): lax.all_gather(grads_half, ('dp', 'seq'), axis=0, tiled=True)  29.6 us
    unnamed x85, local copies, waits for them, and re-layouts  21.7 us
    sub x4, matrix products, group_grads(): exponent = jnp.exp(scores - largest)  21.6 us
    convert_element_type x4, other arithmetic, group_grads(): prob_half = probability.astype(jnp.bfloat16)  13.2 us
    concatenate x4, local copies, waits for them, and re-layouts, per_device(): query_out = jnp.concatenate(query_parts, axis=-1).astype(jnp.bfloat16)  7.29 us
  transfers between devices with their start and end apart: 2, of which 1 were waited for; matrix products, arithmetic and copies ran while one was open for 6% of the time, Pallas kernels for 0%

commit v1 on v0

v1 whole, which is shorter than its diff:
```python
import math

import jax
import jax.numpy as jnp
from jax import lax
from jax.experimental import pallas as pl
from jax.experimental.pallas import tpu as pltpu
from jax.sharding import PartitionSpec as P

HEAD = 128
OUTER = 4
F32 = jnp.float32
BF16 = jnp.bfloat16


def dg(a, b, ca, cb):
    return lax.dot_general(a, b, (((ca,), (cb,)), ((), ())), preferred_element_type=F32)


def attention(idx, queries, grad_out, kv_parts):
    own, length, width = queries.shape
    inner = len(kv_parts)
    blocks, pos, kvw2 = kv_parts[0].shape
    kv_heads = kvw2 // (2 * HEAD)
    group = width // (kv_heads * HEAD)
    sib = idx.shape[1]
    rows = sib * pos
    scale = 1.0 / math.sqrt(HEAD)
    scale2 = scale * math.log2(math.e)

    def kern(idx_ref, q_ref, g_ref, *refs):
        kv_in = refs[:inner]
        dq_ref = refs[inner]
        outs = refs[inner + 1 : 2 * inner + 1]
        kv_s, k_s, v_s, acc = refs[2 * inner + 1 :]
        g = pl.program_id(0)
        c = pl.program_id(1)

        @pl.when((g == 0) & (c == 0))
        def _():
            for i in range(inner):
                kv_s[i * blocks : (i + 1) * blocks] = kv_in[i][...]

        k_at = pl.ds(pl.multiple_of(g * HEAD, HEAD), HEAD)
        v_at = pl.ds(pl.multiple_of((kv_heads + g) * HEAD, HEAD), HEAD)
        for j in range(sib):
            b = idx_ref[c, j]
            k_s[j * pos : (j + 1) * pos, :] = kv_s[b, :, k_at]
            v_s[j * pos : (j + 1) * pos, :] = kv_s[b, :, v_at]
        k = k_s[...]
        v = v_s[...]
        dk = dv = None
        for h in range(group):
            at = slice(h * HEAD, (h + 1) * HEAD)
            q = q_ref[0, :, at]
            go = g_ref[0, :, at]
            s = dg(k, q, 1, 1)
            m = jnp.max(s, axis=0, keepdims=True)
            e = jnp.exp2((s - m) * scale2)
            p = e * (1.0 / jnp.sum(e, axis=0, keepdims=True))
            ph = p.astype(BF16)
            dp = dg(v, go, 1, 1)
            delta = jnp.sum(ph.astype(F32) * dp, axis=0, keepdims=True)
            sh = (p * (dp - delta)).astype(BF16)
            dq_ref[0, :, at] = (dg(sh, k, 0, 0) * scale).astype(BF16)
            dkh = dg(sh, q, 1, 0)
            dvh = dg(ph, go, 1, 0)
            dk = dkh if dk is None else dk + dkh
            dv = dvh if dv is None else dv + dvh

        @pl.when(c == 0)
        def _():
            acc[...] = jnp.zeros_like(acc)

        for j in range(sib):
            b = idx_ref[c, j]
            acc[b, :, :HEAD] += dk[j * pos : (j + 1) * pos, :] * scale
            acc[b, :, HEAD:] += dv[j * pos : (j + 1) * pos, :]

        @pl.when(c == own - 1)
        def _():
            for i in range(inner):
                outs[i][...] = acc[i * blocks : (i + 1) * blocks].astype(BF16)

    q_spec = pl.BlockSpec((1, length, group * HEAD), lambda g, c, i: (c, 0, g))
    kv_spec = pl.BlockSpec(
        (blocks, pos, kvw2), lambda g, c, i: (0, 0, 0), pipeline_mode=pl.Buffered(1)
    )
    out_spec = pl.BlockSpec((blocks, pos, 2 * HEAD), lambda g, c, i: (0, 0, g))
    flops = 10 * own * length * group * kv_heads * rows * HEAD
    res = pl.pallas_call(
        kern,
        grid_spec=pltpu.PrefetchScalarGridSpec(
            num_scalar_prefetch=1,
            grid=(kv_heads, own),
            in_specs=[q_spec, q_spec] + [kv_spec] * inner,
            out_specs=[q_spec] + [out_spec] * inner,
            scratch_shapes=[
                pltpu.VMEM((inner * blocks, pos, kvw2), BF16),
                pltpu.VMEM((rows, HEAD), BF16),
                pltpu.VMEM((rows, HEAD), BF16),
                pltpu.VMEM((inner * blocks, pos, 2 * HEAD), F32),
            ],
        ),
        out_shape=[jax.ShapeDtypeStruct(queries.shape, BF16)]
        + [jax.ShapeDtypeStruct((blocks, pos, kvw2), BF16)] * inner,
        compiler_params=pltpu.CompilerParams(vmem_limit_bytes=48 << 20),
        cost_estimate=pl.CostEstimate(
            flops=flops, bytes_accessed=6 * queries.size, transcendentals=0
        ),
        name="attention",
    )(idx, queries, grad_out, *kv_parts)
    return res[0], res[1:]


def add_split(parts, pieces):
    shape = parts[0].shape
    each = shape[0] // pieces
    count = len(parts)

    def kern(*refs):
        for i in range(pieces):
            at = slice(i * each, (i + 1) * each)
            total = refs[0][at].astype(F32)
            for r in refs[1:count]:
                total = total + r[at].astype(F32)
            refs[count + i][...] = total.astype(BF16)

    return pl.pallas_call(
        kern,
        out_shape=[jax.ShapeDtypeStruct((each,) + shape[1:], BF16)] * pieces,
        cost_estimate=pl.CostEstimate(flops=0, bytes_accessed=2 * count * 2 * 65536, transcendentals=0),
        name="add_split",
    )(*parts)


def weight_parts(place, columns, grads, kv_heads):
    devices, dps, rows, width = columns.shape
    inner = len(grads)
    kvw2 = grads[0].shape[1]

    def kern(place_ref, c_ref, *refs):
        g_in = refs[:inner]
        outs = refs[inner : inner + dps]
        g_s, c_s = refs[inner + dps :]
        mine = place_ref[0]
        at = 0
        for i in range(inner):
            g_s[i * OUTER * rows : (i + 1) * OUTER * rows, :] = g_in[i][...]
        for k in range(dps):
            which = place_ref[1 + k]
            for i in range(inner):
                for o in range(OUTER):
                    at = (i * OUTER + o) * rows
                    c_s[at : at + rows, :] = c_ref[place_ref[1 + dps + i * OUTER + o], which]
            both = dg(c_s[...], g_s[...], 0, 0)
            for h in range(kv_heads):
                lo = 2 * h * HEAD
                outs[k][:, h * HEAD : (h + 1) * HEAD] = both[:, lo : lo + HEAD]
                outs[k][:, (kv_heads + h) * HEAD : (kv_heads + h + 1) * HEAD] = both[
                    :, lo + HEAD : lo + 2 * HEAD
                ]

    vmem = pl.BlockSpec(memory_space=pltpu.VMEM)
    return pl.pallas_call(
        kern,
        in_specs=[pl.BlockSpec(memory_space=pltpu.SMEM)] + [vmem] * (1 + inner),
        out_specs=[vmem] * dps,
        out_shape=[jax.ShapeDtypeStruct((width, kvw2), F32)] * dps,
        scratch_shapes=[
            pltpu.VMEM((devices * rows, kvw2), BF16),
            pltpu.VMEM((devices * rows, width), BF16),
        ],
        compiler_params=pltpu.CompilerParams(vmem_limit_bytes=32 << 20),
        name="weight_parts",
    )(place, columns, *grads)


def make_per_device(n_seq, n_dp):
    inner = n_seq // OUTER

    def swap(x, axis, count, by):
        return lax.ppermute(x, axis, [(i, i ^ by) for i in range(count)])

    def seq_swap(x, by):
        return swap(x, "seq", n_seq, by)

    def gather_all(x):
        near = [x] + [seq_swap(x, k * inner) for k in range(1, OUTER)]
        near = jnp.concatenate(near, axis=0)
        return [near] + [seq_swap(near, k) for k in range(1, inner)]

    def per_device(siblings, queries, grad_out, keys_in, input_values, summary):
        own, pos, kvw = keys_in.shape[1:]
        kv_heads = kvw // HEAD
        me = lax.axis_index("seq").astype(jnp.int32)
        me_dp = lax.axis_index("dp").astype(jnp.int32)

        kv = jnp.concatenate([keys_in[0], input_values[0]], axis=-1)
        kv_parts = gather_all(kv)

        sib = siblings[0]
        rel = jnp.bitwise_xor(sib // own, me)
        idx = ((rel % inner) * OUTER + rel // inner) * own + sib % own
        query_grad, terms = attention(idx, queries[0], grad_out[0], kv_parts)

        width = summary.shape[3] // (n_dp * n_seq)
        hidden = summary[0].reshape(own * pos, n_dp, n_seq, width)
        columns = lax.all_to_all(
            jnp.transpose(hidden, (2, 1, 0, 3)), "seq", split_axis=0, concat_axis=0, tiled=True
        )

        near = add_split([terms[0]] + [seq_swap(terms[k], k) for k in range(1, inner)], OUTER)
        mine = add_split(
            [near[0]] + [seq_swap(near[k], k * inner) for k in range(1, OUTER)], 1
        )[0]
        grads = gather_all(mine.reshape(own * pos, 2 * kvw))

        dps = jnp.bitwise_xor(jnp.arange(n_dp, dtype=jnp.int32), me_dp)
        order = jnp.array(
            [o * inner + i for i in range(inner) for o in range(OUTER)], dtype=jnp.int32
        )
        place = jnp.concatenate([me[None], dps, jnp.bitwise_xor(order, me)])
        parts = weight_parts(place, columns, grads, kv_heads)
        total = parts[0]
        for k in range(1, n_dp):
            total = total + swap(parts[k], "dp", n_dp, k)
        return query_grad[None], total

    return per_device


def solution(mesh):
    rows = P("dp", "seq", None, None)
    return jax.shard_map(
        make_per_device(mesh.shape["seq"], mesh.shape["dp"]),
        mesh=mesh,
        in_specs=(P("dp", "seq", None), rows, rows, rows, rows, rows),
        out_specs=(rows, P(("dp", "seq"), None)),
        check_vma=False,
    )
```

time: 358 us -> 119 us (0.33)
  blocking collectives: 183 us -> 0 us
  matrix products: 58.9 us -> 0 us
  local copies, waits for them, and re-layouts: 47.2 us -> 3.87 us
  Pallas kernels: 0 us -> 34.4 us
  starting transfers between devices: 3.55 us -> 29.8 us
  other arithmetic: 20 us -> 4.16 us
  waiting for transfers between devices: 29.6 us -> 45.4 us
  between operations: 15.2 us -> 0.72 us
    unnamed x1 -> x0, blocking collectives: 98.3 us -> none
    all_gather x2 -> x0, blocking collectives: 84.4 us -> none  [the longest x1 45.6 us: per_device(): lax.all_gather(keys_in, 'seq', axis=1, tiled=True)]
    ppermute x0 -> x19, waiting for transfers between devices: none -> 38.2 us  [swap(): return lax.ppermute(x, axis, [(i, i ^ by) for i in range(count)])]
    dot_general x23 -> x0, matrix products: 37.3 us -> none  [the longest x4 6.98 us: group_grads(): jnp.einsum('crtl,cld->ctrd', prob_half, value_tile_block, preferred_eleme...]
    pallas_call x0 -> x4, Pallas kernels: none -> 34.4 us  [the longest x1 29.8 us: attention(): pl.pallas_call(kern, grid_spec=pltpu.PrefetchScalarGridSpec(num_scalar_pr...]
    all_gather x1 -> x0, waiting for transfers between devices: 29.6 us -> none  [per_device(): lax.all_gather(grads_half, ('dp', 'seq'), axis=0, tiled=True)]
    ppermute x0 -> x19, starting transfers between devices: none -> 25.1 us  [swap(): return lax.ppermute(x, axis, [(i, i ^ by) for i in range(count)])]
    sub x4 -> x0, matrix products: 21.6 us -> none  [group_grads(): exponent = jnp.exp(scores - largest)]
  transfers between devices with their start and end apart: 2 -> 20, of which waited for: 1 -> 15; matrix products, arithmetic and copies ran while one was open for 6% -> 3% of each run, Pallas kernels for 0% -> 0%
where the time goes in v1:
time: 119 us; the launch traced here: 118 us
  waiting for transfers between devices  45.4 us (38%)
  Pallas kernels  34.4 us (29%)
  starting transfers between devices  29.8 us (25%)
  other arithmetic  4.16 us (3%)
  local copies, waits for them, and re-layouts  3.87 us (3%)
    ppermute x19, waiting for transfers between devices, swap(): return lax.ppermute(x, axis, [(i, i ^ by) for i in range(count)])  38.2 us
    pallas_call x1, Pallas kernels, attention(): pl.pallas_call(kern, grid_spec=pltpu.PrefetchScalarGridSpec(num_scalar_pr...  29.8 us
    ppermute x19, starting transfers between devices, swap(): return lax.ppermute(x, axis, [(i, i ^ by) for i in range(count)])  25.1 us
    all_to_all x1, waiting for transfers between devices, per_device(): lax.all_to_all(jnp.transpose(hidden, (2, 1, 0, 3)), 'seq', split_axis=0,...  7.24 us
    all_to_all x1, starting transfers between devices, per_device(): lax.all_to_all(jnp.transpose(hidden, (2, 1, 0, 3)), 'seq', split_axis=0,...  4.61 us
    pallas_call x2, Pallas kernels, add_split(): pl.pallas_call(kern, out_shape=[jax.ShapeDtypeStruct((each,) + shape[1:],...  3.53 us
  transfers between devices with their start and end apart: 20, of which 15 were waited for; matrix products, arithmetic and copies ran while one was open for 3% of the time, Pallas kernels for 0%

profile of v1, /device:TPU:0, one launch (start us, length us, event | category | flops | bytes accessed | tf_op | source)
XLA Modules:
  0.0 118.3 jit_solution(3969668052257701017)
XLA Ops:
  0.6 0.8 pad_maximum_fusion.2
  1.4 5.1 %collective-permute-start.2 = (bf16[2,16,1024]{2,1,0:T(8,128)(2,1)S(1)}, bf16[2,16,1024]{2,1,0:T(8,128)(2,1)S(1)}, u32[]{:S(2)}, u32[]{:S(2)}) collective-permute-start(bf16[2,16,1024]{2,1,0:T(8,128)(2,1)S(1)} %pad_maximum_fusion.2), channel_id=1, source_target_pairs={{0,12},{1,13},{2,14},{3,15},{4,8},{5,9},{6,10},{7,11},{8,4},{9,5},... | collective-permute-start | bytes 196616 | tf_op jit(solution)/shard_map/ppermute | solution.py:183
  6.5 0.0 collective-permute-start.1
  6.5 0.6 collective-permute-start
  7.1 1.9 %collective-permute-done.2 = bf16[2,16,1024]{2,1,0:T(8,128)(2,1)S(1)} collective-permute-done((bf16[2,16,1024]{2,1,0:T(8,128)(2,1)S(1)}, bf16[2,16,1024]{2,1,0:T(8,128)(2,1)S(1)}, u32[]{:S(2)}, u32[]{:S(2)}) %collective-permute-start.2) | collective-permute-done | bytes 65568 | tf_op jit(solution)/shard_map/ppermute | solution.py:183
  9.0 3.1 %collective-permute-done.1 = bf16[2,16,1024]{2,1,0:T(8,128)(2,1)S(1)} collective-permute-done((bf16[2,16,1024]{2,1,0:T(8,128)(2,1)S(1)}, bf16[2,16,1024]{2,1,0:T(8,128)(2,1)S(1)}, u32[]{:S(2)}, u32[]{:S(2)}) %collective-permute-start.1) | collective-permute-done | bytes 65568 | tf_op jit(solution)/shard_map/ppermute | solution.py:183
  12.1 0.0 collective-permute-done
  12.1 0.8 pad_maximum_fusion.refs_0_
  12.9 2.5 %collective-permute-start.5 = (bf16[8,16,1024]{2,1,0:T(8,128)(2,1)S(1)}, bf16[8,16,1024]{2,1,0:T(8,128)(2,1)S(1)}, u32[]{:S(2)}, u32[]{:S(2)}) collective-permute-start(bf16[8,16,1024]{2,1,0:T(8,128)(2,1)S(1)} %pad_maximum_fusion.refs_0_), channel_id=1, source_target_pairs={{0,3},{1,2},{2,1},{3,0},{4,7},{5,6},{6,5},{7,4},{8,11},{9,10},{10,... | collective-permute-start | bytes 786440 | tf_op jit(solution)/shard_map/ppermute | solution.py:183
  15.4 0.5 collective-permute-start.4
  15.9 0.5 collective-permute-start.3
  16.4 0.7 fusion.2.idx_ref
  17.1 5.9 %collective-permute-done.5.refs_3_ = bf16[8,16,1024]{2,1,0:T(8,128)(2,1)S(1)} collective-permute-done((bf16[8,16,1024]{2,1,0:T(8,128)(2,1)S(1)}, bf16[8,16,1024]{2,1,0:T(8,128)(2,1)S(1)}, u32[]{:S(2)}, u32[]{:S(2)}) %collective-permute-start.5) | collective-permute-done | bytes 262176 | tf_op jit(solution)/shard_map/ppermute | solution.py:183
  23.1 4.3 %collective-permute-done.4.refs_2_ = bf16[8,16,1024]{2,1,0:T(8,128)(2,1)S(1)} collective-permute-done((bf16[8,16,1024]{2,1,0:T(8,128)(2,1)S(1)}, bf16[8,16,1024]{2,1,0:T(8,128)(2,1)S(1)}, u32[]{:S(2)}, u32[]{:S(2)}) %collective-permute-start.4) | collective-permute-done | bytes 262176 | tf_op jit(solution)/shard_map/ppermute | solution.py:183
  27.4 0.2 collective-permute-done.3.refs_1_
  27.6 0.0 copy-start.1
  27.6 0.0 copy-start.8
  27.6 29.8 %attention.1 = (bf16[2,512,2560]{2,1,0:T(8,128)(2,1)}, bf16[8,16,1024]{2,1,0:T(8,128)(2,1)S(1)}, bf16[8,16,1024]{2,1,0:T(8,128)(2,1)S(1)}, bf16[8,16,1024]{2,1,0:T(8,128)(2,1)S(1)}, bf16[8,16,1024]{2,1,0:T(8,128)(2,1)S(1)}) custom-call(s32[2,16]{1,0:T(2,128)S(1)} %fusion.2.idx_ref, bf16[2,512,2560]{2,1,0:T(8,128)(2,1)} %bitcast.34, ...), custom_call_target="tpu_custom_call" | custom-call | flops 6710886400 | bytes 15728640 | tf_op jit(solution)/shard_map/attention/pallas_call | solution.py:91
  57.3 0.0 copy-start
  57.3 0.7 copy-done
  58.0 1.5 %collective-permute-start.6 = (bf16[8,16,1024]{2,1,0:T(8,128)(2,1)S(1)}, bf16[8,16,1024]{2,1,0:T(8,128)(2,1)S(1)}, u32[]{:S(2)}, u32[]{:S(2)}) collective-permute-start(bf16[8,16,1024]{2,1,0:T(8,128)(2,1)S(1)} %get-tuple-element.15), channel_id=1, source_target_pairs={{0,1},{1,0},{2,3},{3,2},{4,5},{5,4},{6,7},{7,6},{8,9},{9,8},{10,11... | collective-permute-start | bytes 786440 | tf_op jit(solution)/shard_map/ppermute | solution.py:183
  59.5 0.6 collective-permute-start.7
  60.1 1.4 %collective-permute-start.8 = (bf16[8,16,1024]{2,1,0:T(8,128)(2,1)S(1)}, bf16[8,16,1024]{2,1,0:T(8,128)(2,1)S(1)}, u32[]{:S(2)}, u32[]{:S(2)}) collective-permute-start(bf16[8,16,1024]{2,1,0:T(8,128)(2,1)S(1)} %get-tuple-element.17), channel_id=1, source_target_pairs={{0,3},{1,2},{2,1},{3,0},{4,7},{5,6},{6,5},{7,4},{8,11},{9,10},{10,... | collective-permute-start | bytes 786440 | tf_op jit(solution)/shard_map/ppermute | solution.py:183
  61.5 5.7 %collective-permute-done.6.refs_1_ = bf16[8,16,1024]{2,1,0:T(8,128)(2,1)S(1)} collective-permute-done((bf16[8,16,1024]{2,1,0:T(8,128)(2,1)S(1)}, bf16[8,16,1024]{2,1,0:T(8,128)(2,1)S(1)}, u32[]{:S(2)}, u32[]{:S(2)}) %collective-permute-start.6) | collective-permute-done | bytes 262176 | tf_op jit(solution)/shard_map/ppermute | solution.py:183
  67.2 5.8 %collective-permute-done.7.refs_2_ = bf16[8,16,1024]{2,1,0:T(8,128)(2,1)S(1)} collective-permute-done((bf16[8,16,1024]{2,1,0:T(8,128)(2,1)S(1)}, bf16[8,16,1024]{2,1,0:T(8,128)(2,1)S(1)}, u32[]{:S(2)}, u32[]{:S(2)}) %collective-permute-start.7) | collective-permute-done | bytes 262176 | tf_op jit(solution)/shard_map/ppermute | solution.py:183
  73.0 0.0 collective-permute-done.8.refs_3_
  73.0 0.0 copy-done.2
  73.0 0.7 copy-done.3
  73.7 0.1 copy-done.4
  73.8 1.9 %add_split.2 = (bf16[2,16,1024]{2,1,0:T(8,128)(2,1)}, bf16[2,16,1024]{2,1,0:T(8,128)(2,1)}, bf16[2,16,1024]{2,1,0:T(8,128)(2,1)}, bf16[2,16,1024]{2,1,0:T(8,128)(2,1)}) custom-call(bf16[8,16,1024]{2,1,0:T(8,128)(2,1)} %copy-done, bf16[8,16,1024]{2,1,0:T(8,128)(2,1)} %copy-done.2, bf16[8,16,1024]{2,1,0:T(8,128)(2,1)} %copy-done.3, bf16[8,16,1024]{2,1,0:T(8,128)(2,1)} %copy-done.4), custom_call_target="tpu_custom_call" | custom-call | bytes 1048576 | tf_op jit(solution)/shard_map/add_split/pallas_call | solution.py:129
  75.8 0.0 collective-permute-start.9
  75.8 2.0 %collective-permute-start.10 = (bf16[2,16,1024]{2,1,0:T(8,128)(2,1)}, bf16[2,16,1024]{2,1,0:T(8,128)(2,1)S(1)}, u32[]{:S(2)}, u32[]{:S(2)}) collective-permute-start(bf16[2,16,1024]{2,1,0:T(8,128)(2,1)} %get-tuple-element.20), channel_id=1, source_target_pairs={{0,8},{1,9},{2,10},{3,11},{4,12},{5,13},{6,14},{7,15},{8,0},{9,1},... | collective-permute-start | bytes 196616 | tf_op jit(solution)/shard_map/ppermute | solution.py:183
  77.8 2.3 %collective-permute-start.11 = (bf16[2,16,1024]{2,1,0:T(8,128)(2,1)}, bf16[2,16,1024]{2,1,0:T(8,128)(2,1)S(1)}, u32[]{:S(2)}, u32[]{:S(2)}) collective-permute-start(bf16[2,16,1024]{2,1,0:T(8,128)(2,1)} %get-tuple-element.21), channel_id=1, source_target_pairs={{0,12},{1,13},{2,14},{3,15},{4,8},{5,9},{6,10},{7,11},{8,4},{9,5},... | collective-permute-start | bytes 196616 | tf_op jit(solution)/shard_map/ppermute | solution.py:183
  80.2 0.1 collective-permute-done.9.refs_1_
  80.2 2.5 %collective-permute-done.10.refs_2_ = bf16[2,16,1024]{2,1,0:T(8,128)(2,1)S(1)} collective-permute-done((bf16[2,16,1024]{2,1,0:T(8,128)(2,1)}, bf16[2,16,1024]{2,1,0:T(8,128)(2,1)S(1)}, u32[]{:S(2)}, u32[]{:S(2)}) %collective-permute-start.10) | collective-permute-done | bytes 65568 | tf_op jit(solution)/shard_map/ppermute | solution.py:183
  82.7 1.4 %collective-permute-done.11.refs_3_ = bf16[2,16,1024]{2,1,0:T(8,128)(2,1)S(1)} collective-permute-done((bf16[2,16,1024]{2,1,0:T(8,128)(2,1)}, bf16[2,16,1024]{2,1,0:T(8,128)(2,1)S(1)}, u32[]{:S(2)}, u32[]{:S(2)}) %collective-permute-start.11) | collective-permute-done | bytes 65568 | tf_op jit(solution)/shard_map/ppermute | solution.py:183
  84.1 0.0 copy-done.5
  84.1 0.0 copy-done.6
  84.1 0.6 copy-done.7
  84.7 1.6 %add_split.3 = bf16[2,16,1024]{2,1,0:T(8,128)(2,1)} custom-call(bf16[2,16,1024]{2,1,0:T(8,128)(2,1)} %get-tuple-element.18.refs_0_, bf16[2,16,1024]{2,1,0:T(8,128)(2,1)} %copy-done.5, bf16[2,16,1024]{2,1,0:T(8,128)(2,1)} %copy-done.6, bf16[2,16,1024]{2,1,0:T(8,128)(2,1)} %copy-done.7), custom_call_target="tpu_custom_call" | custom-call | bytes 1048576 | tf_op jit(solution)/shard_map/add_split/pallas_call | solution.py:129
  86.3 2.3 %collective-permute-start.14 = (bf16[32,1024]{1,0:T(8,128)(2,1)}, bf16[32,1024]{1,0:T(8,128)(2,1)S(1)}, u32[]{:S(2)}, u32[]{:S(2)}) collective-permute-start(bf16[32,1024]{1,0:T(8,128)(2,1)} %bitcast.26), channel_id=1, source_target_pairs={{0,12},{1,13},{2,14},{3,15},{4,8},{5,9},{6,10},{7,11},{8,4},{9,5},... | collective-permute-start | bytes 196616 | tf_op jit(solution)/shard_map/ppermute | solution.py:183
  88.6 0.0 collective-permute-start.13
  88.7 2.1 %collective-permute-start.12 = (bf16[32,1024]{1,0:T(8,128)(2,1)}, bf16[32,1024]{1,0:T(8,128)(2,1)S(1)}, u32[]{:S(2)}, u32[]{:S(2)}) collective-permute-start(bf16[32,1024]{1,0:T(8,128)(2,1)} %bitcast.28), channel_id=1, source_target_pairs={{0,4},{1,5},{2,6},{3,7},{4,0},{5,1},{6,2},{7,3},{8,12},{9,13},{10,... | collective-permute-start | bytes 196616 | tf_op jit(solution)/shard_map/ppermute | solution.py:183
  90.7 0.0 copy-done.1
  90.7 0.6 reshape_squeeze.3
  91.4 1.1 copy.11
  92.5 4.6 %all-to-all-start = ((bf16[16,2,32,160]{3,2,1,0:T(8,128)(2,1)}), bf16[16,2,32,160]{3,2,1,0:T(8,128)(2,1)S(1)}, u32[]{:S(2)}, u32[]{:S(2)}) async-start(bf16[16,2,32,160]{3,2,1,0:T(8,128)(2,1)} %bitcast.25), calls=%async_computation | async-start | bytes 1048576 | tf_op jit(solution)/shard_map/all_to_all | solution.py:209
  97.1 0.0 collective-permute-done.14
  97.1 0.0 collective-permute-done.13
  97.1 0.0 collective-permute-done.12
  97.1 0.9 pad_maximum_fusion.1.refs_0_
  98.0 2.9 %collective-permute-start.17 = (bf16[128,1024]{1,0:T(8,128)(2,1)S(1)}, bf16[128,1024]{1,0:T(8,128)(2,1)S(1)}, u32[]{:S(2)}, u32[]{:S(2)}) collective-permute-start(bf16[128,1024]{1,0:T(8,128)(2,1)S(1)} %pad_maximum_fusion.1.refs_0_), channel_id=1, source_target_pairs={{0,3},{1,2},{2,1},{3,0},{4,7},{5,6},{6,5},{7,4},{8,11},{9,10},{10,... | collective-permute-start | bytes 786440 | tf_op jit(solution)/shard_map/ppermute | solution.py:183
  100.9 0.6 collective-permute-start.16
  101.4 0.1 collective-permute-start.15
  101.5 0.0 copy-done.8
  101.5 0.1 pad_add_fusion.place_ref
  101.6 7.2 %all-to-all-done.c_ref = bf16[16,2,32,160]{3,2,1,0:T(8,128)(2,1)S(1)} async-done(((bf16[16,2,32,160]{3,2,1,0:T(8,128)(2,1)}), bf16[16,2,32,160]{3,2,1,0:T(8,128)(2,1)S(1)}, u32[]{:S(2)}, u32[]{:S(2)}) %all-to-all-start) | async-done | bytes 327712 | tf_op jit(solution)/shard_map/all_to_all | solution.py:209
  108.9 2.5 %collective-permute-done.17.refs_3_ = bf16[128,1024]{1,0:T(8,128)(2,1)S(1)} collective-permute-done((bf16[128,1024]{1,0:T(8,128)(2,1)S(1)}, bf16[128,1024]{1,0:T(8,128)(2,1)S(1)}, u32[]{:S(2)}, u32[]{:S(2)}) %collective-permute-start.17) | collective-permute-done | bytes 262176 | tf_op jit(solution)/shard_map/ppermute | solution.py:183
  111.4 2.2 %collective-permute-done.16.refs_2_ = bf16[128,1024]{1,0:T(8,128)(2,1)S(1)} collective-permute-done((bf16[128,1024]{1,0:T(8,128)(2,1)S(1)}, bf16[128,1024]{1,0:T(8,128)(2,1)S(1)}, u32[]{:S(2)}, u32[]{:S(2)}) %collective-permute-start.16) | collective-permute-done | bytes 262176 | tf_op jit(solution)/shard_map/ppermute | solution.py:183
  113.5 0.6 collective-permute-done.15.refs_1_
  114.1 1.1 weight_parts.1
  115.2 0.1 collective-permute-start.18
  115.3 2.1 %collective-permute-done.18 = f32[160,1024]{1,0:T(8,128)S(1)} collective-permute-done((f32[160,1024]{1,0:T(8,128)S(1)}, f32[160,1024]{1,0:T(8,128)S(1)}, u32[]{:S(2)}, u32[]{:S(2)}) %collective-permute-start.18) | collective-permute-done | bytes 655392 | tf_op jit(solution)/shard_map/ppermute | solution.py:183
  117.4 0.9 add.25
  (8 shorter events, 0.0 us)
Async XLA Ops:
  1.4 7.6 %collective-permute-start.2 = (bf16[2,16,1024]{2,1,0:T(8,128)(2,1)S(1)}, bf16[2,16,1024]{2,1,0:T(8,128)(2,1)S(1)}, u32[]{:S(2)}, u32[]{:S(2)}) collective-permute-start(bf16[2,16,1024]{2,1,0:T(8,128)(2,1)S(1)} %pad_maximum_fusion.2), channel_id=1, source_target_pairs={{0,12},{1,13},{2,14},{3,15},{4,8},{5,9},{6,10},{7,11},{8,4},{9,5},... | collective-permute-start | bytes 196616 | tf_op jit(solution)/shard_map/ppermute | solution.py:183
  6.5 5.6 %collective-permute-start.1 = (bf16[2,16,1024]{2,1,0:T(8,128)(2,1)S(1)}, bf16[2,16,1024]{2,1,0:T(8,128)(2,1)S(1)}, u32[]{:S(2)}, u32[]{:S(2)}) collective-permute-start(bf16[2,16,1024]{2,1,0:T(8,128)(2,1)S(1)} %pad_maximum_fusion.2), channel_id=1, source_target_pairs={{0,8},{1,9},{2,10},{3,11},{4,12},{5,13},{6,14},{7,15},{8,0},{9,1},... | collective-permute-start | bytes 196616 | tf_op jit(solution)/shard_map/ppermute | solution.py:183
  6.5 5.6 %collective-permute-start = (bf16[2,16,1024]{2,1,0:T(8,128)(2,1)S(1)}, bf16[2,16,1024]{2,1,0:T(8,128)(2,1)S(1)}, u32[]{:S(2)}, u32[]{:S(2)}) collective-permute-start(bf16[2,16,1024]{2,1,0:T(8,128)(2,1)S(1)} %pad_maximum_fusion.2), channel_id=1, source_target_pairs={{0,4},{1,5},{2,6},{3,7},{4,0},{5,1},{6,2},{7,3},{8,12},{9,13},{10,... | collective-permute-start | bytes 196616 | tf_op jit(solution)/shard_map/ppermute | solution.py:183
  12.9 10.2 %collective-permute-start.5 = (bf16[8,16,1024]{2,1,0:T(8,128)(2,1)S(1)}, bf16[8,16,1024]{2,1,0:T(8,128)(2,1)S(1)}, u32[]{:S(2)}, u32[]{:S(2)}) collective-permute-start(bf16[8,16,1024]{2,1,0:T(8,128)(2,1)S(1)} %pad_maximum_fusion.refs_0_), channel_id=1, source_target_pairs={{0,3},{1,2},{2,1},{3,0},{4,7},{5,6},{6,5},{7,4},{8,11},{9,10},{10,... | collective-permute-start | bytes 786440 | tf_op jit(solution)/shard_map/ppermute | solution.py:183
  15.4 11.9 %collective-permute-start.4 = (bf16[8,16,1024]{2,1,0:T(8,128)(2,1)S(1)}, bf16[8,16,1024]{2,1,0:T(8,128)(2,1)S(1)}, u32[]{:S(2)}, u32[]{:S(2)}) collective-permute-start(bf16[8,16,1024]{2,1,0:T(8,128)(2,1)S(1)} %pad_maximum_fusion.refs_0_), channel_id=1, source_target_pairs={{0,2},{1,3},{2,0},{3,1},{4,6},{5,7},{6,4},{7,5},{8,10},{9,11},{10,... | collective-permute-start | bytes 786440 | tf_op jit(solution)/shard_map/ppermute | solution.py:183
  15.9 11.7 %collective-permute-start.3 = (bf16[8,16,1024]{2,1,0:T(8,128)(2,1)S(1)}, bf16[8,16,1024]{2,1,0:T(8,128)(2,1)S(1)}, u32[]{:S(2)}, u32[]{:S(2)}) collective-permute-start(bf16[8,16,1024]{2,1,0:T(8,128)(2,1)S(1)} %pad_maximum_fusion.refs_0_), channel_id=1, source_target_pairs={{0,1},{1,0},{2,3},{3,2},{4,5},{5,4},{6,7},{7,6},{8,9},{9,8},{10,11... | collective-permute-start | bytes 786440 | tf_op jit(solution)/shard_map/ppermute | solution.py:183
  27.6 63.2 %copy-start.1 = (bf16[1,2,16,5120]{3,2,1,0:T(8,128)(2,1)S(1)}, bf16[1,2,16,5120]{3,2,1,0:T(8,128)(2,1)}, u32[]{:S(2)}) copy-start(bf16[1,2,16,5120]{3,2,1,0:T(8,128)(2,1)} %param.12) | copy-start | bytes 983044
  27.6 74.0 %copy-start.8 = (s32[16]{0:T(128)S(1)}, s32[16]{0:T(128)}, u32[]{:S(2)}) copy-start(s32[16]{0:T(128)} %constant.58.clone) | copy-start | bytes 196
  57.3 0.7 copy-start
  58.0 9.2 %collective-permute-start.6 = (bf16[8,16,1024]{2,1,0:T(8,128)(2,1)S(1)}, bf16[8,16,1024]{2,1,0:T(8,128)(2,1)S(1)}, u32[]{:S(2)}, u32[]{:S(2)}) collective-permute-start(bf16[8,16,1024]{2,1,0:T(8,128)(2,1)S(1)} %get-tuple-element.15), channel_id=1, source_target_pairs={{0,1},{1,0},{2,3},{3,2},{4,5},{5,4},{6,7},{7,6},{8,9},{9,8},{10,11... | collective-permute-start | bytes 786440 | tf_op jit(solution)/shard_map/ppermute | solution.py:183
  59.5 13.5 %collective-permute-start.7 = (bf16[8,16,1024]{2,1,0:T(8,128)(2,1)S(1)}, bf16[8,16,1024]{2,1,0:T(8,128)(2,1)S(1)}, u32[]{:S(2)}, u32[]{:S(2)}) collective-permute-start(bf16[8,16,1024]{2,1,0:T(8,128)(2,1)S(1)} %get-tuple-element.16), channel_id=1, source_target_pairs={{0,2},{1,3},{2,0},{3,1},{4,6},{5,7},{6,4},{7,5},{8,10},{9,11},{10,... | collective-permute-start | bytes 786440 | tf_op jit(solution)/shard_map/ppermute | solution.py:183
  60.1 12.9 %collective-permute-start.8 = (bf16[8,16,1024]{2,1,0:T(8,128)(2,1)S(1)}, bf16[8,16,1024]{2,1,0:T(8,128)(2,1)S(1)}, u32[]{:S(2)}, u32[]{:S(2)}) collective-permute-start(bf16[8,16,1024]{2,1,0:T(8,128)(2,1)S(1)} %get-tuple-element.17), channel_id=1, source_target_pairs={{0,3},{1,2},{2,1},{3,0},{4,7},{5,6},{6,5},{7,4},{8,11},{9,10},{10,... | collective-permute-start | bytes 786440 | tf_op jit(solution)/shard_map/ppermute | solution.py:183
  67.2 5.8 %copy-start.2 = (bf16[8,16,1024]{2,1,0:T(8,128)(2,1)}, bf16[8,16,1024]{2,1,0:T(8,128)(2,1)S(1)}, u32[]{:S(2)}) copy-start(bf16[8,16,1024]{2,1,0:T(8,128)(2,1)S(1)} %collective-permute-done.6.refs_1_) | copy-start | bytes 786436
  73.0 0.7 copy-start.3
  73.0 0.8 copy-start.4
  75.8 4.5 %collective-permute-start.9 = (bf16[2,16,1024]{2,1,0:T(8,128)(2,1)}, bf16[2,16,1024]{2,1,0:T(8,128)(2,1)S(1)}, u32[]{:S(2)}, u32[]{:S(2)}) collective-permute-start(bf16[2,16,1024]{2,1,0:T(8,128)(2,1)} %get-tuple-element.19), channel_id=1, source_target_pairs={{0,4},{1,5},{2,6},{3,7},{4,0},{5,1},{6,2},{7,3},{8,12},{9,13},{10,... | collective-permute-start | bytes 196616 | tf_op jit(solution)/shard_map/ppermute | solution.py:183
  75.8 6.9 %collective-permute-start.10 = (bf16[2,16,1024]{2,1,0:T(8,128)(2,1)}, bf16[2,16,1024]{2,1,0:T(8,128)(2,1)S(1)}, u32[]{:S(2)}, u32[]{:S(2)}) collective-permute-start(bf16[2,16,1024]{2,1,0:T(8,128)(2,1)} %get-tuple-element.20), channel_id=1, source_target_pairs={{0,8},{1,9},{2,10},{3,11},{4,12},{5,13},{6,14},{7,15},{8,0},{9,1},... | collective-permute-start | bytes 196616 | tf_op jit(solution)/shard_map/ppermute | solution.py:183
  77.8 6.3 %collective-permute-start.11 = (bf16[2,16,1024]{2,1,0:T(8,128)(2,1)}, bf16[2,16,1024]{2,1,0:T(8,128)(2,1)S(1)}, u32[]{:S(2)}, u32[]{:S(2)}) collective-permute-start(bf16[2,16,1024]{2,1,0:T(8,128)(2,1)} %get-tuple-element.21), channel_id=1, source_target_pairs={{0,12},{1,13},{2,14},{3,15},{4,8},{5,9},{6,10},{7,11},{8,4},{9,5},... | collective-permute-start | bytes 196616 | tf_op jit(solution)/shard_map/ppermute | solution.py:183
  80.2 3.9 %copy-start.5 = (bf16[2,16,1024]{2,1,0:T(8,128)(2,1)}, bf16[2,16,1024]{2,1,0:T(8,128)(2,1)S(1)}, u32[]{:S(2)}) copy-start(bf16[2,16,1024]{2,1,0:T(8,128)(2,1)S(1)} %collective-permute-done.9.refs_1_) | copy-start | bytes 196612
  82.7 1.4 %copy-start.6 = (bf16[2,16,1024]{2,1,0:T(8,128)(2,1)}, bf16[2,16,1024]{2,1,0:T(8,128)(2,1)S(1)}, u32[]{:S(2)}) copy-start(bf16[2,16,1024]{2,1,0:T(8,128)(2,1)S(1)} %collective-permute-done.10.refs_2_) | copy-start | bytes 196612
  84.1 0.6 copy-start.7
  86.3 10.8 %collective-permute-start.14 = (bf16[32,1024]{1,0:T(8,128)(2,1)}, bf16[32,1024]{1,0:T(8,128)(2,1)S(1)}, u32[]{:S(2)}, u32[]{:S(2)}) collective-permute-start(bf16[32,1024]{1,0:T(8,128)(2,1)} %bitcast.26), channel_id=1, source_target_pairs={{0,12},{1,13},{2,14},{3,15},{4,8},{5,9},{6,10},{7,11},{8,4},{9,5},... | collective-permute-start | bytes 196616 | tf_op jit(solution)/shard_map/ppermute | solution.py:183
  88.6 8.5 %collective-permute-start.13 = (bf16[32,1024]{1,0:T(8,128)(2,1)}, bf16[32,1024]{1,0:T(8,128)(2,1)S(1)}, u32[]{:S(2)}, u32[]{:S(2)}) collective-permute-start(bf16[32,1024]{1,0:T(8,128)(2,1)} %bitcast.27), channel_id=1, source_target_pairs={{0,8},{1,9},{2,10},{3,11},{4,12},{5,13},{6,14},{7,15},{8,0},{9,1},... | collective-permute-start | bytes 196616 | tf_op jit(solution)/shard_map/ppermute | solution.py:183
  88.7 8.5 %collective-permute-start.12 = (bf16[32,1024]{1,0:T(8,128)(2,1)}, bf16[32,1024]{1,0:T(8,128)(2,1)S(1)}, u32[]{:S(2)}, u32[]{:S(2)}) collective-permute-start(bf16[32,1024]{1,0:T(8,128)(2,1)} %bitcast.28), channel_id=1, source_target_pairs={{0,4},{1,5},{2,6},{3,7},{4,0},{5,1},{6,2},{7,3},{8,12},{9,13},{10,... | collective-permute-start | bytes 196616 | tf_op jit(solution)/shard_map/ppermute | solution.py:183
  92.5 16.4 %all-to-all-start = ((bf16[16,2,32,160]{3,2,1,0:T(8,128)(2,1)}), bf16[16,2,32,160]{3,2,1,0:T(8,128)(2,1)S(1)}, u32[]{:S(2)}, u32[]{:S(2)}) async-start(bf16[16,2,32,160]{3,2,1,0:T(8,128)(2,1)} %bitcast.25), calls=%async_computation | async-start | bytes 1048576 | tf_op jit(solution)/shard_map/all_to_all | solution.py:209
  98.0 13.4 %collective-permute-start.17 = (bf16[128,1024]{1,0:T(8,128)(2,1)S(1)}, bf16[128,1024]{1,0:T(8,128)(2,1)S(1)}, u32[]{:S(2)}, u32[]{:S(2)}) collective-permute-start(bf16[128,1024]{1,0:T(8,128)(2,1)S(1)} %pad_maximum_fusion.1.refs_0_), channel_id=1, source_target_pairs={{0,3},{1,2},{2,1},{3,0},{4,7},{5,6},{6,5},{7,4},{8,11},{9,10},{10,... | collective-permute-start | bytes 786440 | tf_op jit(solution)/shard_map/ppermute | solution.py:183
  100.9 12.7 %collective-permute-start.16 = (bf16[128,1024]{1,0:T(8,128)(2,1)S(1)}, bf16[128,1024]{1,0:T(8,128)(2,1)S(1)}, u32[]{:S(2)}, u32[]{:S(2)}) collective-permute-start(bf16[128,1024]{1,0:T(8,128)(2,1)S(1)} %pad_maximum_fusion.1.refs_0_), channel_id=1, source_target_pairs={{0,2},{1,3},{2,0},{3,1},{4,6},{5,7},{6,4},{7,5},{8,10},{9,11},{10,... | collective-permute-start | bytes 786440 | tf_op jit(solution)/shard_map/ppermute | solution.py:183
  101.4 12.7 %collective-permute-start.15 = (bf16[128,1024]{1,0:T(8,128)(2,1)S(1)}, bf16[128,1024]{1,0:T(8,128)(2,1)S(1)}, u32[]{:S(2)}, u32[]{:S(2)}) collective-permute-start(bf16[128,1024]{1,0:T(8,128)(2,1)S(1)} %pad_maximum_fusion.1.refs_0_), channel_id=1, source_target_pairs={{0,1},{1,0},{2,3},{3,2},{4,5},{5,4},{6,7},{7,6},{8,9},{9,8},{10,11... | collective-permute-start | bytes 786440 | tf_op jit(solution)/shard_map/ppermute | solution.py:183
  115.2 2.2 %collective-permute-start.18 = (f32[160,1024]{1,0:T(8,128)S(1)}, f32[160,1024]{1,0:T(8,128)S(1)}, u32[]{:S(2)}, u32[]{:S(2)}) collective-permute-start(f32[160,1024]{1,0:T(8,128)S(1)} %get-tuple-element.23), channel_id=1, source_target_pairs={{0,16},{16,0},{1,17},{17,1},{2,18},{18,2},{3,19},{19,3},{4,20},{20... | collective-permute-start | bytes 1966088 | tf_op jit(solution)/shard_map/ppermute | solution.py:183

commit v2 on v1

v2 whole, which is shorter than its diff:
```python
import math

import jax
import jax.numpy as jnp
from jax import lax
from jax.experimental import pallas as pl
from jax.experimental.pallas import tpu as pltpu
from jax.sharding import PartitionSpec as P


HEAD = 128
OUTER = 4
VMEM_LIMIT = 28 << 20
CHUNKS = (4,)
F32 = jnp.float32
BF16 = jnp.bfloat16


def dg(a, b, ca, cb):
    return lax.dot_general(a, b, (((ca,), (cb,)), ((), ())), preferred_element_type=F32)


def attention(siblings, me, queries, grad_out, kv_parts, pos, first, heads, kv_heads, before):
    own, length, width = queries.shape
    inner = len(kv_parts) // 2
    sizes = [part.shape[0] for part in kv_parts]
    starts = [sum(sizes[:i]) for i in range(2 * inner)]
    total = sum(sizes)
    kvw2 = kv_parts[0].shape[1]
    group = width // (kv_heads * HEAD)
    span = group * HEAD
    sib = siblings.shape[1]
    rows = sib * pos
    scale = 1.0 / math.sqrt(HEAD)
    scale2 = scale * math.log2(math.e)
    chunk = 128

    def kern(sib_ref, me_ref, q_hbm, g_hbm, *refs):
        kv_in = refs[: 2 * inner]
        refs = refs[2 * inner + (before is not None) :]
        dq_hbm = refs[0]
        outs = refs[1 : 2 * inner + 1]
        kv_s, k_s, v_s, acc, q_buf, g_buf, d_buf, idx_ref, in_sem, out_sem = refs[
            2 * inner + 1 :
        ]
        items = [(c, h) for c in range(own) for h in range(group)]

        def fetches(g, slot, c, h):
            at = pl.ds(pl.multiple_of(((first + g) * group + h) * HEAD, HEAD), HEAD)
            to = slice(h * HEAD, (h + 1) * HEAD)
            return [
                pltpu.make_async_copy(
                    src.at[c, :, at], buf.at[slot, c, :, to], in_sem.at[slot, c, h, n]
                )
                for n, (src, buf) in enumerate(((q_hbm, q_buf), (g_hbm, g_buf)))
            ]

        def store(g, slot, c, h):
            at = pl.ds(pl.multiple_of(((first + g) * group + h) * HEAD, HEAD), HEAD)
            return pltpu.make_async_copy(
                d_buf.at[slot, c, :, h * HEAD : (h + 1) * HEAD],
                dq_hbm.at[c, :, at],
                out_sem.at[slot, c, h],
            )

        for c, h in items:
            for copy in fetches(0, 0, c, h):
                copy.start()
        for c in range(own):
            for j in range(sib):
                which = sib_ref[c, j]
                rel = jnp.bitwise_xor(lax.div(which, own), me_ref[0])
                block = (lax.rem(rel, inner) * OUTER + lax.div(rel, inner)) * own
                idx_ref[c, j] = (block + lax.rem(which, own)) * pos
        for i in range(2 * inner):
            kv_s[starts[i] : starts[i] + sizes[i], :] = kv_in[i][...]

        @pl.loop(0, heads)
        def _(g):
            slot = lax.rem(g, 2)

            @pl.when(g + 1 < heads)
            def _():
                for c, h in items:
                    for copy in fetches(g + 1, 1 - slot, c, h):
                        copy.start()

            k_at = pl.ds(pl.multiple_of(g * HEAD, HEAD), HEAD)
            v_at = pl.ds(pl.multiple_of((heads + g) * HEAD, HEAD), HEAD)
            for c in range(own):
                for j in range(sib):
                    b = pl.ds(pl.multiple_of(idx_ref[c, j], pos), pos)
                    k_s[c, j * pos : (j + 1) * pos, :] = kv_s[b, k_at]
                    v_s[c, j * pos : (j + 1) * pos, :] = kv_s[b, v_at]
            acc[...] = jnp.zeros_like(acc)

            for c, h in items:
                for copy in fetches(g, slot, c, h):
                    copy.wait()

            @pl.when(g >= 2)
            def _():
                for c, h in items:
                    store(g - 2, slot, c, h).wait()

            at = [slice(h * HEAD, (h + 1) * HEAD) for h in range(group)]
            held = {}
            sums = {}

            def scores(n):
                c, h = items[n]
                held[n] = (
                    dg(k_s[c], q_buf[slot, c, :, at[h]], 1, 1),
                    dg(v_s[c], g_buf[slot, c, :, at[h]], 1, 1),
                )

            def soften(n):
                probs = []
                grads = []
                for w in range(0, length, chunk):
                    s = held[n][0][:, w : w + chunk]
                    dp = held[n][1][:, w : w + chunk]
                    m = jnp.max(s, axis=0, keepdims=True)
                    e = jnp.exp2(s * scale2 - m * scale2)
                    p = e * (1.0 / jnp.sum(e, axis=0, keepdims=True))
                    ph = p.astype(BF16)
                    delta = jnp.sum(ph.astype(F32) * dp, axis=0, keepdims=True)
                    grads.append((p * (dp - delta)).astype(BF16))
                    probs.append(ph)
                held[n] = (jnp.concatenate(probs, axis=1), jnp.concatenate(grads, axis=1))

            def products(n):
                c, h = items[n]
                ph, sh = held.pop(n)
                d_buf[slot, c, :, at[h]] = (dg(sh, k_s[c], 0, 0) * scale).astype(BF16)
                dk = dg(sh, q_buf[slot, c, :, at[h]], 1, 0)
                dv = dg(ph, g_buf[slot, c, :, at[h]], 1, 0)
                if h:
                    dk = sums[c][0] + dk
                    dv = sums[c][1] + dv
                sums[c] = (dk, dv)
                if h == group - 1:
                    for j in range(sib):
                        b = pl.ds(pl.multiple_of(idx_ref[c, j], pos), pos)
                        acc[b, :HEAD] += dk[j * pos : (j + 1) * pos, :] * scale
                        acc[b, HEAD:] += dv[j * pos : (j + 1) * pos, :]

            scores(0)
            for n in range(len(items)):
                if n:
                    products(n - 1)
                if n + 1 < len(items):
                    scores(n + 1)
                soften(n)
            products(len(items) - 1)
            for c, h in items:
                store(g, slot, c, h).start()
            o_at = pl.ds(pl.multiple_of(g * 2 * HEAD, 2 * HEAD), 2 * HEAD)
            for i in range(2 * inner):
                outs[i][:, o_at] = acc[starts[i] : starts[i] + sizes[i], :].astype(BF16)

        for g in range(max(heads - 2, 0), heads):
            for c, h in items:
                store(g, g % 2, c, h).wait()

    vmem = pl.BlockSpec(memory_space=pltpu.VMEM)
    hbm = pl.BlockSpec(memory_space=pl.ANY)
    smem = pl.BlockSpec(memory_space=pltpu.SMEM)
    flops = 20 * own * length * group * heads * rows * HEAD
    queries = pltpu.with_memory_space_constraint(queries, pltpu.HBM)
    grad_out = pltpu.with_memory_space_constraint(grad_out, pltpu.HBM)
    args = [siblings, me, queries, grad_out, *kv_parts] + ([before] if before is not None else [])
    res = pl.pallas_call(
        kern,
        in_specs=[smem, smem, hbm, hbm]
        + [vmem] * (2 * inner)
        + ([hbm] if before is not None else []),
        out_specs=[hbm] + [vmem] * (2 * inner),
        scratch_shapes=[
            pltpu.VMEM((total, kvw2), BF16),
            pltpu.VMEM((own, rows, HEAD), BF16),
            pltpu.VMEM((own, rows, HEAD), BF16),
            pltpu.VMEM((total, 2 * HEAD), F32),
            pltpu.VMEM((2, own, length, span), BF16),
            pltpu.VMEM((2, own, length, span), BF16),
            pltpu.VMEM((2, own, length, span), BF16),
            pltpu.SMEM((own, sib), jnp.int32),
            pltpu.SemaphoreType.DMA((2, own, group, 2)),
            pltpu.SemaphoreType.DMA((2, own, group)),
        ],
        out_shape=[jax.ShapeDtypeStruct(queries.shape, BF16)]
        + [jax.ShapeDtypeStruct((size, kvw2), BF16) for size in sizes],
        input_output_aliases={4 + 2 * inner: 0} if before is not None else {},
        compiler_params=pltpu.CompilerParams(vmem_limit_bytes=VMEM_LIMIT),
        cost_estimate=pl.CostEstimate(
            flops=flops, bytes_accessed=6 * queries.size, transcendentals=0
        ),
        name="attention",
    )(*args)
    return res[0], res[1:]


def add_split(parts, pieces):
    shape = parts[0].shape
    each = shape[0] // pieces
    count = len(parts)

    def kern(*refs):
        for i in range(pieces):
            at = slice(i * each, (i + 1) * each)
            total = refs[0][at].astype(F32)
            for r in refs[1:count]:
                total = total + r[at].astype(F32)
            refs[count + i][...] = total.astype(BF16)

    vmem = pl.BlockSpec(memory_space=pltpu.VMEM)
    return pl.pallas_call(
        kern,
        in_specs=[vmem] * count,
        out_specs=[vmem] * pieces,
        out_shape=[jax.ShapeDtypeStruct((each,) + shape[1:], BF16)] * pieces,
        cost_estimate=pl.CostEstimate(
            flops=0, bytes_accessed=2 * count * parts[0].size, transcendentals=0
        ),
        compiler_params=pltpu.CompilerParams(vmem_limit_bytes=8 << 20),
        name="add_split",
    )(*parts)


def weight_parts(place, columns, grads, heads_of, kv_heads):
    devices, dps, rows, width = columns.shape
    chunks = len(grads)
    parts_of = len(grads[0])
    inner = parts_of // 2
    sizes = [part.shape[0] for part in grads[0]]
    starts = [sum(sizes[:i]) for i in range(parts_of)]
    kvw2 = 2 * kv_heads * HEAD

    def kern(place_ref, c_ref, *refs):
        g_in = [refs[i * parts_of : (i + 1) * parts_of] for i in range(chunks)]
        outs = refs[chunks * parts_of : chunks * parts_of + dps]
        g_s, c_s = refs[chunks * parts_of + dps :]
        col = 0
        for n in range(chunks):
            wide = 2 * heads_of[n] * HEAD
            for i in range(parts_of):
                g_s[starts[i] : starts[i] + sizes[i], col : col + wide] = g_in[n][i][...]
            col += wide
        for k in range(dps):
            which = place_ref[k]
            for i in range(inner):
                for o in range(OUTER):
                    at = (i * OUTER + o) * rows
                    c_s[at : at + rows, :] = c_ref[place_ref[dps + i * OUTER + o], which]
            both = dg(c_s[...], g_s[...], 0, 0)
            for h in range(kv_heads):
                lo = 2 * h * HEAD
                outs[k][:, h * HEAD : (h + 1) * HEAD] = both[:, lo : lo + HEAD]
                outs[k][:, (kv_heads + h) * HEAD : (kv_heads + h + 1) * HEAD] = both[
                    :, lo + HEAD : lo + 2 * HEAD
                ]

    vmem = pl.BlockSpec(memory_space=pltpu.VMEM)
    return pl.pallas_call(
        kern,
        in_specs=[pl.BlockSpec(memory_space=pltpu.SMEM)] + [vmem] * (1 + chunks * parts_of),
        out_specs=[vmem] * dps,
        out_shape=[jax.ShapeDtypeStruct((width, kvw2), F32)] * dps,
        scratch_shapes=[
            pltpu.VMEM((devices * rows, kvw2), BF16),
            pltpu.VMEM((devices * rows, width), BF16),
        ],
        compiler_params=pltpu.CompilerParams(vmem_limit_bytes=32 << 20),
        name="weight_parts",
    )(place, columns, *[g for part in grads for g in part])


def make_per_device(n_seq, n_dp):
    inner = n_seq // OUTER

    def swap(x, axis, count, by):
        return lax.ppermute(x, axis, [(i, i ^ by) for i in range(count)])

    def seq_swap(x, by):
        return swap(x, "seq", n_seq, by)

    def gather_all(x):
        rest = [seq_swap(x, k * inner) for k in range(1, OUTER)]
        ones = [x] + [seq_swap(x, k) for k in range(1, inner)]
        rest = jnp.concatenate(rest, axis=0)
        rests = [rest] + [seq_swap(rest, k) for k in range(1, inner)]
        return [part for pair in zip(ones, rests, strict=True) for part in pair]

    def per_device(siblings, queries, grad_out, keys_in, input_values, summary):
        own, pos, kvw = keys_in.shape[1:]
        kv_heads = kvw // HEAD
        me = lax.axis_index("seq").astype(jnp.int32)
        me_dp = lax.axis_index("dp").astype(jnp.int32)

        width = summary.shape[3] // (n_dp * n_seq)
        hidden = summary[0].reshape(own * pos, n_dp, n_seq, width)
        hidden = jnp.transpose(hidden, (2, 1, 0, 3))
        columns = lax.all_to_all(hidden, "seq", split_axis=0, concat_axis=0, tiled=True)

        kv_parts = []
        first = 0
        for heads in CHUNKS:
            at = slice(first * HEAD, (first + heads) * HEAD)
            kv_parts.append(
                gather_all(
                    jnp.concatenate(
                        [keys_in[0, :, :, at], input_values[0, :, :, at]], axis=-1
                    ).reshape(own * pos, 2 * heads * HEAD)
                )
            )
            first += heads

        query_grad = None
        grads = []
        first = 0
        for n, heads in enumerate(CHUNKS):
            query_grad, terms = attention(
                siblings[0],
                me[None],
                queries[0],
                grad_out[0],
                 kv_parts[n], pos, first, heads, kv_heads, query_grad
            )
            first += heads
            ones, rests = terms[::2], terms[1::2]
            near = add_split(
                [rests[0]] + [seq_swap(rests[k], k) for k in range(1, inner)], OUTER - 1
            )
            mine = add_split(
                [ones[0]]
                + [seq_swap(ones[k], k) for k in range(1, inner)]
                + [seq_swap(near[k - 1], k * inner) for k in range(1, OUTER)],
                1,
            )[0]
            grads.append(gather_all(mine))

        dps = jnp.bitwise_xor(jnp.arange(n_dp, dtype=jnp.int32), me_dp)
        order = jnp.array(
            [o * inner + i for i in range(inner) for o in range(OUTER)], dtype=jnp.int32
        )
        place = jnp.concatenate([dps, jnp.bitwise_xor(order, me)])
        parts = weight_parts(place, columns, grads, CHUNKS, kv_heads)
        total = parts[0]
        for k in range(1, n_dp):
            total = total + swap(parts[k], "dp", n_dp, k)
        return query_grad[None], total

    return per_device


def solution(mesh):
    rows = P("dp", "seq", None, None)
    return jax.shard_map(
        make_per_device(mesh.shape["seq"], mesh.shape["dp"]),
        mesh=mesh,
        in_specs=(P("dp", "seq", None), rows, rows, rows, rows, rows),
        out_specs=(rows, P(("dp", "seq"), None)),
        check_vma=False,
    )
```

time: 119 us -> 106 us (0.89)
  starting transfers between devices: 29.8 us -> 43.9 us
  waiting for transfers between devices: 45.4 us -> 31.6 us
  Pallas kernels: 34.4 us -> 25.4 us
  other arithmetic: 4.16 us -> 1.8 us
  local copies, waits for them, and re-layouts: 3.87 us -> 2.45 us
    ppermute x19 -> x28, starting transfers between devices: 25.1 us -> 40.3 us  [swap(): return lax.ppermute(x, axis, [(i, i ^ by) for i in range(count)])]
    pallas_call x3, Pallas kernels: 33.3 us -> 24.3 us  [the longest x1 24.1 us: attention(): pl.pallas_call(kern, in_specs=[smem, smem, hbm, hbm] + [vmem] * (2 * inne...]
    all_to_all x1, waiting for transfers between devices: 7.24 us -> 0.01 us  [per_device(): lax.all_to_all(hidden, 'seq', split_axis=0, concat_axis=0, tiled=True)]
    ppermute x19 -> x28, waiting for transfers between devices: 38.2 us -> 31.6 us  [swap(): return lax.ppermute(x, axis, [(i, i ^ by) for i in range(count)])]
    concatenate x4 -> x2, other arithmetic: 2.52 us -> 0.86 us  [the longest x1 0.78 us: per_device(): jnp.concatenate([keys_in[0, :, :, at], input_values[0, :, :, at]], axis=-1)]
    unnamed x18 -> x10, local copies, waits for them, and re-layouts: 2.13 us -> 0.7 us
  transfers between devices with their start and end apart: 20 -> 29, of which waited for: 15 -> 10; matrix products, arithmetic and copies ran while one was open for 3% -> 2% of each run, Pallas kernels for 0% -> 0%
where the time goes in v2:
time: 106 us
  starting transfers between devices  43.9 us (41%)
  waiting for transfers between devices  31.6 us (30%)
  Pallas kernels  25.4 us (24%)
  local copies, waits for them, and re-layouts  2.45 us (2%)
  other arithmetic  1.8 us (2%)
    ppermute x28, starting transfers between devices, swap(): return lax.ppermute(x, axis, [(i, i ^ by) for i in range(count)])  40.3 us
    ppermute x28, waiting for transfers between devices, swap(): return lax.ppermute(x, axis, [(i, i ^ by) for i in range(count)])  31.6 us
    pallas_call x1, Pallas kernels, attention(): pl.pallas_call(kern, in_specs=[smem, smem, hbm, hbm] + [vmem] * (2 * inne...  24.1 us
    all_to_all x1, starting transfers between devices, per_device(): lax.all_to_all(hidden, 'seq', split_axis=0, concat_axis=0, tiled=True)  3.57 us
  transfers between devices with their start and end apart: 29, of which 10 were waited for; matrix products, arithmetic and copies ran while one was open for 2% of the time, Pallas kernels for 0%

profile of v2, /device:TPU:0, one launch (start us, length us, event | category | flops | bytes accessed | tf_op | source)
XLA Modules:
  0.0 106.0 jit_solution(564910735872147944)
XLA Ops:
  0.6 0.8 pad_maximum_fusion.refs_0_
  1.4 3.1 %collective-permute-start = (bf16[32,1024]{1,0:T(8,128)(2,1)S(1)}, bf16[32,1024]{1,0:T(8,128)(2,1)S(1)}, u32[]{:S(2)}, u32[]{:S(2)}) collective-permute-start(bf16[32,1024]{1,0:T(8,128)(2,1)S(1)} %pad_maximum_fusion.refs_0_), channel_id=1, source_target_pairs={{0,4},{1,5},{2,6},{3,7},{4,0},{5,1},{6,2},{7,3},{8,12},{9,13},{10,... | collective-permute-start | bytes 196616 | tf_op jit(solution)/shard_map/ppermute | solution.py:282
  4.5 2.5 %collective-permute-start.2 = (bf16[32,1024]{1,0:T(8,128)(2,1)S(1)}, bf16[32,1024]{1,0:T(8,128)(2,1)S(1)}, u32[]{:S(2)}, u32[]{:S(2)}) collective-permute-start(bf16[32,1024]{1,0:T(8,128)(2,1)S(1)} %pad_maximum_fusion.refs_0_), channel_id=1, source_target_pairs={{0,12},{1,13},{2,14},{3,15},{4,8},{5,9},{6,10},{7,11},{8,4},{9,5},... | collective-permute-start | bytes 196616 | tf_op jit(solution)/shard_map/ppermute | solution.py:282
  6.9 0.1 collective-permute-start.1
  7.1 0.0 collective-permute-done
  7.1 6.3 %collective-permute-done.1 = bf16[32,1024]{1,0:T(8,128)(2,1)S(1)} collective-permute-done((bf16[32,1024]{1,0:T(8,128)(2,1)S(1)}, bf16[32,1024]{1,0:T(8,128)(2,1)S(1)}, u32[]{:S(2)}, u32[]{:S(2)}) %collective-permute-start.1) | collective-permute-done | bytes 65568 | tf_op jit(solution)/shard_map/ppermute | solution.py:282
  13.4 2.5 %collective-permute-start.8 = (bf16[96,1024]{1,0:T(8,128)(2,1)S(1)}, bf16[96,1024]{1,0:T(8,128)(2,1)S(1)}, u32[]{:S(2)}, u32[]{:S(2)}) collective-permute-start(bf16[96,1024]{1,0:T(8,128)(2,1)S(1)} %constant_dynamic-update-slice_fusion.refs_1_), channel_id=1, source_target_pairs={{0,3},{1,2},{2,1},{3,0},{4,7},{5,6},{6,5},{7,4},{8,11},{9,10},{10,... | collective-permute-start | bytes 589832 | tf_op jit(solution)/shard_map/ppermute | solution.py:282
  15.9 0.5 collective-permute-start.6
  16.4 0.5 collective-permute-start.4
  17.0 2.4 %collective-permute-start.7 = (bf16[32,1024]{1,0:T(8,128)(2,1)S(1)}, bf16[32,1024]{1,0:T(8,128)(2,1)S(1)}, u32[]{:S(2)}, u32[]{:S(2)}) collective-permute-start(bf16[32,1024]{1,0:T(8,128)(2,1)S(1)} %pad_maximum_fusion.refs_0_), channel_id=1, source_target_pairs={{0,3},{1,2},{2,1},{3,0},{4,7},{5,6},{6,5},{7,4},{8,11},{9,10},{10,... | collective-permute-start | bytes 196616 | tf_op jit(solution)/shard_map/ppermute | solution.py:282
  19.4 0.5 collective-permute-start.5
  19.9 7.0 %collective-permute-done.7.refs_6_ = bf16[32,1024]{1,0:T(8,128)(2,1)S(1)} collective-permute-done((bf16[32,1024]{1,0:T(8,128)(2,1)S(1)}, bf16[32,1024]{1,0:T(8,128)(2,1)S(1)}, u32[]{:S(2)}, u32[]{:S(2)}) %collective-permute-start.7) | collective-permute-done | bytes 65568 | tf_op jit(solution)/shard_map/ppermute | solution.py:282
  26.9 1.5 %collective-permute-start.3 = (bf16[32,1024]{1,0:T(8,128)(2,1)S(1)}, bf16[32,1024]{1,0:T(8,128)(2,1)S(1)}, u32[]{:S(2)}, u32[]{:S(2)}) collective-permute-start(bf16[32,1024]{1,0:T(8,128)(2,1)S(1)} %pad_maximum_fusion.refs_0_), channel_id=1, source_target_pairs={{0,1},{1,0},{2,3},{3,2},{4,5},{5,4},{6,7},{7,6},{8,9},{9,8},{10,11... | collective-permute-start | bytes 196616 | tf_op jit(solution)/shard_map/ppermute | solution.py:282
  28.4 0.0 collective-permute-done.5.refs_4_
  28.4 2.8 %collective-permute-done.3.refs_2_ = bf16[32,1024]{1,0:T(8,128)(2,1)S(1)} collective-permute-done((bf16[32,1024]{1,0:T(8,128)(2,1)S(1)}, bf16[32,1024]{1,0:T(8,128)(2,1)S(1)}, u32[]{:S(2)}, u32[]{:S(2)}) %collective-permute-start.3) | collective-permute-done | bytes 65568 | tf_op jit(solution)/shard_map/ppermute | solution.py:282
  31.2 0.0 collective-permute-done.8.refs_7_
  31.2 0.0 collective-permute-done.6.refs_5_
  31.2 0.0 collective-permute-done.4.refs_3_
  31.2 0.0 copy-start
  31.2 0.7 copy-done
  31.9 24.1 %attention.1 = (bf16[2,512,2560]{2,1,0:T(8,128)(2,1)}, bf16[32,1024]{1,0:T(8,128)(2,1)S(1)}, bf16[96,1024]{1,0:T(8,128)(2,1)S(1)}, bf16[32,1024]{1,0:T(8,128)(2,...) custom-call(s32[2,16]{1,0:T(2,128)S(1)} %bitcast.12, ...), custom_call_target="tpu_custom_call" | custom-call | flops 13421772800 | bytes 15728640 | tf_op jit(solution)/shard_map/attention/pallas_call | solution.py:173
  56.0 1.6 %collective-permute-start.12 = (bf16[96,1024]{1,0:T(8,128)(2,1)S(1)}, bf16[96,1024]{1,0:T(8,128)(2,1)S(1)}, u32[]{:S(2)}, u32[]{:S(2)}) collective-permute-start(bf16[96,1024]{1,0:T(8,128)(2,1)S(1)} %get-tuple-element.22), channel_id=1, source_target_pairs={{0,1},{1,0},{2,3},{3,2},{4,5},{5,4},{6,7},{7,6},{8,9},{9,8},{10,11... | collective-permute-start | bytes 589832 | tf_op jit(solution)/shard_map/ppermute | solution.py:282
  57.6 1.5 %collective-permute-start.13 = (bf16[96,1024]{1,0:T(8,128)(2,1)S(1)}, bf16[96,1024]{1,0:T(8,128)(2,1)S(1)}, u32[]{:S(2)}, u32[]{:S(2)}) collective-permute-start(bf16[96,1024]{1,0:T(8,128)(2,1)S(1)} %get-tuple-element.23), channel_id=1, source_target_pairs={{0,2},{1,3},{2,0},{3,1},{4,6},{5,7},{6,4},{7,5},{8,10},{9,11},{10,... | collective-permute-start | bytes 589832 | tf_op jit(solution)/shard_map/ppermute | solution.py:282
  59.1 0.5 collective-permute-start.14
  59.6 1.5 %collective-permute-start.9 = (bf16[32,1024]{1,0:T(8,128)(2,1)S(1)}, bf16[32,1024]{1,0:T(8,128)(2,1)S(1)}, u32[]{:S(2)}, u32[]{:S(2)}) collective-permute-start(bf16[32,1024]{1,0:T(8,128)(2,1)S(1)} %get-tuple-element.18), channel_id=1, source_target_pairs={{0,1},{1,0},{2,3},{3,2},{4,5},{5,4},{6,7},{7,6},{8,9},{9,8},{10,11... | collective-permute-start | bytes 196616 | tf_op jit(solution)/shard_map/ppermute | solution.py:282
  61.1 1.5 %collective-permute-start.10 = (bf16[32,1024]{1,0:T(8,128)(2,1)S(1)}, bf16[32,1024]{1,0:T(8,128)(2,1)S(1)}, u32[]{:S(2)}, u32[]{:S(2)}) collective-permute-start(bf16[32,1024]{1,0:T(8,128)(2,1)S(1)} %get-tuple-element.19), channel_id=1, source_target_pairs={{0,2},{1,3},{2,0},{3,1},{4,6},{5,7},{6,4},{7,5},{8,10},{9,11},{10,... | collective-permute-start | bytes 196616 | tf_op jit(solution)/shard_map/ppermute | solution.py:282
  62.6 1.3 %collective-permute-done.12.refs_1_ = bf16[96,1024]{1,0:T(8,128)(2,1)S(1)} collective-permute-done((bf16[96,1024]{1,0:T(8,128)(2,1)S(1)}, bf16[96,1024]{1,0:T(8,128)(2,1)S(1)}, u32[]{:S(2)}, u32[]{:S(2)}) %collective-permute-start.12) | collective-permute-done | bytes 196640 | tf_op jit(solution)/shard_map/ppermute | solution.py:282
  63.9 2.5 %collective-permute-start.11 = (bf16[32,1024]{1,0:T(8,128)(2,1)S(1)}, bf16[32,1024]{1,0:T(8,128)(2,1)S(1)}, u32[]{:S(2)}, u32[]{:S(2)}) collective-permute-start(bf16[32,1024]{1,0:T(8,128)(2,1)S(1)} %get-tuple-element.20), channel_id=1, source_target_pairs={{0,3},{1,2},{2,1},{3,0},{4,7},{5,6},{6,5},{7,4},{8,11},{9,10},{10,... | collective-permute-start | bytes 196616 | tf_op jit(solution)/shard_map/ppermute | solution.py:282
  66.3 0.1 collective-permute-done.13.refs_2_
  66.4 1.1 %collective-permute-done.14.refs_3_ = bf16[96,1024]{1,0:T(8,128)(2,1)S(1)} collective-permute-done((bf16[96,1024]{1,0:T(8,128)(2,1)S(1)}, bf16[96,1024]{1,0:T(8,128)(2,1)S(1)}, u32[]{:S(2)}, u32[]{:S(2)}) %collective-permute-start.14) | collective-permute-done | bytes 196640 | tf_op jit(solution)/shard_map/ppermute | solution.py:282
  67.5 0.1 add_split.2
  67.6 0.1 collective-permute-start.15
  67.7 1.3 %collective-permute-start.16 = (bf16[32,1024]{1,0:T(8,128)(2,1)S(1)}, bf16[32,1024]{1,0:T(8,128)(2,1)S(1)}, u32[]{:S(2)}, u32[]{:S(2)}) collective-permute-start(bf16[32,1024]{1,0:T(8,128)(2,1)S(1)} %get-tuple-element.26), channel_id=1, source_target_pairs={{0,8},{1,9},{2,10},{3,11},{4,12},{5,13},{6,14},{7,15},{8,0},{9,1},... | collective-permute-start | bytes 196616 | tf_op jit(solution)/shard_map/ppermute | solution.py:282
  69.0 0.0 collective-permute-done.9.refs_1_
  69.0 3.0 %collective-permute-start.17 = (bf16[32,1024]{1,0:T(8,128)(2,1)S(1)}, bf16[32,1024]{1,0:T(8,128)(2,1)S(1)}, u32[]{:S(2)}, u32[]{:S(2)}) collective-permute-start(bf16[32,1024]{1,0:T(8,128)(2,1)S(1)} %get-tuple-element.27), channel_id=1, source_target_pairs={{0,12},{1,13},{2,14},{3,15},{4,8},{5,9},{6,10},{7,11},{8,4},{9,5},... | collective-permute-start | bytes 196616 | tf_op jit(solution)/shard_map/ppermute | solution.py:282
  72.0 0.6 reshape_squeeze.3
  72.7 1.1 %copy.11 = bf16[32,2,16,160]{3,0,1,2:T(8,128)(2,1)} copy(bf16[32,2,16,160]{3,2,1,0:T(8,128)(2,1)S(1)} %reshape_squeeze.3) | data formatting | bytes 655360 | tf_op jit(solution)/shard_map/reshape;squeeze | solution.py:301
  73.8 3.6 %all-to-all-start = ((bf16[16,2,32,160]{3,2,1,0:T(8,128)(2,1)}), bf16[16,2,32,160]{3,2,1,0:T(8,128)(2,1)S(1)}, u32[]{:S(2)}, u32[]{:S(2)}) async-start(bf16[16,2,32,160]{3,2,1,0:T(8,128)(2,1)} %bitcast.11), calls=%async_computation | async-start | bytes 1048576 | tf_op jit(solution)/shard_map/all_to_all | solution.py:303
  77.4 0.0 collective-permute-done.11.refs_3_
  77.4 0.0 collective-permute-done.15.refs_4_
  77.4 0.0 collective-permute-done.17.refs_6_
  77.4 0.1 add_split.3.refs_0_
  77.5 1.9 %collective-permute-start.18 = (bf16[32,1024]{1,0:T(8,128)(2,1)S(1)}, bf16[32,1024]{1,0:T(8,128)(2,1)S(1)}, u32[]{:S(2)}, u32[]{:S(2)}) collective-permute-start(bf16[32,1024]{1,0:T(8,128)(2,1)S(1)} %add_split.3.refs_0_), channel_id=1, source_target_pairs={{0,4},{1,5},{2,6},{3,7},{4,0},{5,1},{6,2},{7,3},{8,12},{9,13},{10,... | collective-permute-start | bytes 196616 | tf_op jit(solution)/shard_map/ppermute | solution.py:282
  79.4 2.4 %collective-permute-start.25 = (bf16[32,1024]{1,0:T(8,128)(2,1)S(1)}, bf16[32,1024]{1,0:T(8,128)(2,1)S(1)}, u32[]{:S(2)}, u32[]{:S(2)}) collective-permute-start(bf16[32,1024]{1,0:T(8,128)(2,1)S(1)} %add_split.3.refs_0_), channel_id=1, source_target_pairs={{0,3},{1,2},{2,1},{3,0},{4,7},{5,6},{6,5},{7,4},{8,11},{9,10},{10,... | collective-permute-start | bytes 196616 | tf_op jit(solution)/shard_map/ppermute | solution.py:282
  81.8 2.4 %collective-permute-start.20 = (bf16[32,1024]{1,0:T(8,128)(2,1)S(1)}, bf16[32,1024]{1,0:T(8,128)(2,1)S(1)}, u32[]{:S(2)}, u32[]{:S(2)}) collective-permute-start(bf16[32,1024]{1,0:T(8,128)(2,1)S(1)} %add_split.3.refs_0_), channel_id=1, source_target_pairs={{0,12},{1,13},{2,14},{3,15},{4,8},{5,9},{6,10},{7,11},{8,4},{9,5},... | collective-permute-start | bytes 196616 | tf_op jit(solution)/shard_map/ppermute | solution.py:282
  84.1 0.0 collective-permute-start.19
  84.2 0.6 collective-permute-done.18
  84.7 7.5 %collective-permute-done.19 = bf16[32,1024]{1,0:T(8,128)(2,1)S(1)} collective-permute-done((bf16[32,1024]{1,0:T(8,128)(2,1)S(1)}, bf16[32,1024]{1,0:T(8,128)(2,1)S(1)}, u32[]{:S(2)}, u32[]{:S(2)}) %collective-permute-start.19) | collective-permute-done | bytes 65568 | tf_op jit(solution)/shard_map/ppermute | solution.py:282
  92.2 0.0 collective-permute-done.20
  92.2 2.4 %collective-permute-start.26 = (bf16[96,1024]{1,0:T(8,128)(2,1)S(1)}, bf16[96,1024]{1,0:T(8,128)(2,1)S(1)}, u32[]{:S(2)}, u32[]{:S(2)}) collective-permute-start(bf16[96,1024]{1,0:T(8,128)(2,1)S(1)} %constant_dynamic-update-slice_fusion.3.refs_1_), channel_id=1, source_target_pairs={{0,3},{1,2},{2,1},{3,0},{4,7},{5,6},{6,5},{7,4},{8,11},{9,10},{10,... | collective-permute-start | bytes 589832 | tf_op jit(solution)/shard_map/ppermute | solution.py:282
  94.6 0.6 collective-permute-start.24
  95.2 0.6 collective-permute-start.22
  95.8 1.5 %collective-permute-start.23 = (bf16[32,1024]{1,0:T(8,128)(2,1)S(1)}, bf16[32,1024]{1,0:T(8,128)(2,1)S(1)}, u32[]{:S(2)}, u32[]{:S(2)}) collective-permute-start(bf16[32,1024]{1,0:T(8,128)(2,1)S(1)} %add_split.3.refs_0_), channel_id=1, source_target_pairs={{0,2},{1,3},{2,0},{3,1},{4,6},{5,7},{6,4},{7,5},{8,10},{9,11},{10,... | collective-permute-start | bytes 196616 | tf_op jit(solution)/shard_map/ppermute | solution.py:282
  97.3 0.0 collective-permute-done.25.refs_6_
  97.3 1.4 %collective-permute-start.21 = (bf16[32,1024]{1,0:T(8,128)(2,1)S(1)}, bf16[32,1024]{1,0:T(8,128)(2,1)S(1)}, u32[]{:S(2)}, u32[]{:S(2)}) collective-permute-start(bf16[32,1024]{1,0:T(8,128)(2,1)S(1)} %add_split.3.refs_0_), channel_id=1, source_target_pairs={{0,1},{1,0},{2,3},{3,2},{4,5},{5,4},{6,7},{7,6},{8,9},{9,8},{10,11... | collective-permute-start | bytes 196616 | tf_op jit(solution)/shard_map/ppermute | solution.py:282
  98.7 0.1 pad_add_fusion.place_ref
  98.8 3.0 %collective-permute-done.23.refs_4_ = bf16[32,1024]{1,0:T(8,128)(2,1)S(1)} collective-permute-done((bf16[32,1024]{1,0:T(8,128)(2,1)S(1)}, bf16[32,1024]{1,0:T(8,128)(2,1)S(1)}, u32[]{:S(2)}, u32[]{:S(2)}) %collective-permute-start.23) | collective-permute-done | bytes 65568 | tf_op jit(solution)/shard_map/ppermute | solution.py:282
  101.7 0.0 all-to-all-done.c_ref
  101.7 0.0 collective-permute-done.26.refs_7_
  101.8 0.0 collective-permute-done.24.refs_5_
  101.8 1.1 %weight_parts.1 = (f32[160,1024]{1,0:T(8,128)S(1)}, f32[160,1024]{1,0:T(8,128)S(1)}) custom-call(s32[18]{0:T(128)S(1)} %pad_add_fusion.place_ref, bf16[16,2,32,160]{3,2,1,0:T(8,128)(2,1)S(1)} %all-to-all-done.c_ref, bf16[32,1024]{1,0:T(8,128)(2,1)S(1)} %add_split.3.refs_0_, bf16[96,1024]{1,0:T(8,128)(2,1)S(1)} %constant_dynamic-update-slice_fusion.3.refs_1_, ...), custom_call_target="tpu_custom_call" | custom-call | tf_op jit(solution)/shard_map/weight_parts/pallas_call | solution.py:264
  102.9 0.1 collective-permute-start.27
  103.0 2.1 %collective-permute-done.27 = f32[160,1024]{1,0:T(8,128)S(1)} collective-permute-done((f32[160,1024]{1,0:T(8,128)S(1)}, f32[160,1024]{1,0:T(8,128)S(1)}, u32[]{:S(2)}, u32[]{:S(2)}) %collective-permute-start.27) | collective-permute-done | bytes 655392 | tf_op jit(solution)/shard_map/ppermute | solution.py:282
  105.1 0.9 add.3
  (17 shorter events, 0.1 us)
Async XLA Ops:
  1.4 5.6 %collective-permute-start = (bf16[32,1024]{1,0:T(8,128)(2,1)S(1)}, bf16[32,1024]{1,0:T(8,128)(2,1)S(1)}, u32[]{:S(2)}, u32[]{:S(2)}) collective-permute-start(bf16[32,1024]{1,0:T(8,128)(2,1)S(1)} %pad_maximum_fusion.refs_0_), channel_id=1, source_target_pairs={{0,4},{1,5},{2,6},{3,7},{4,0},{5,1},{6,2},{7,3},{8,12},{9,13},{10,... | collective-permute-start | bytes 196616 | tf_op jit(solution)/shard_map/ppermute | solution.py:282
  4.5 8.9 %collective-permute-start.2 = (bf16[32,1024]{1,0:T(8,128)(2,1)S(1)}, bf16[32,1024]{1,0:T(8,128)(2,1)S(1)}, u32[]{:S(2)}, u32[]{:S(2)}) collective-permute-start(bf16[32,1024]{1,0:T(8,128)(2,1)S(1)} %pad_maximum_fusion.refs_0_), channel_id=1, source_target_pairs={{0,12},{1,13},{2,14},{3,15},{4,8},{5,9},{6,10},{7,11},{8,4},{9,5},... | collective-permute-start | bytes 196616 | tf_op jit(solution)/shard_map/ppermute | solution.py:282
  6.9 6.4 %collective-permute-start.1 = (bf16[32,1024]{1,0:T(8,128)(2,1)S(1)}, bf16[32,1024]{1,0:T(8,128)(2,1)S(1)}, u32[]{:S(2)}, u32[]{:S(2)}) collective-permute-start(bf16[32,1024]{1,0:T(8,128)(2,1)S(1)} %pad_maximum_fusion.refs_0_), channel_id=1, source_target_pairs={{0,8},{1,9},{2,10},{3,11},{4,12},{5,13},{6,14},{7,15},{8,0},{9,1},... | collective-permute-start | bytes 196616 | tf_op jit(solution)/shard_map/ppermute | solution.py:282
  13.4 17.8 %collective-permute-start.8 = (bf16[96,1024]{1,0:T(8,128)(2,1)S(1)}, bf16[96,1024]{1,0:T(8,128)(2,1)S(1)}, u32[]{:S(2)}, u32[]{:S(2)}) collective-permute-start(bf16[96,1024]{1,0:T(8,128)(2,1)S(1)} %constant_dynamic-update-slice_fusion.refs_1_), channel_id=1, source_target_pairs={{0,3},{1,2},{2,1},{3,0},{4,7},{5,6},{6,5},{7,4},{8,11},{9,10},{10,... | collective-permute-start | bytes 589832 | tf_op jit(solution)/shard_map/ppermute | solution.py:282
  15.9 15.3 %collective-permute-start.6 = (bf16[96,1024]{1,0:T(8,128)(2,1)S(1)}, bf16[96,1024]{1,0:T(8,128)(2,1)S(1)}, u32[]{:S(2)}, u32[]{:S(2)}) collective-permute-start(bf16[96,1024]{1,0:T(8,128)(2,1)S(1)} %constant_dynamic-update-slice_fusion.refs_1_), channel_id=1, source_target_pairs={{0,2},{1,3},{2,0},{3,1},{4,6},{5,7},{6,4},{7,5},{8,10},{9,11},{10,... | collective-permute-start | bytes 589832 | tf_op jit(solution)/shard_map/ppermute | solution.py:282
  16.4 14.8 %collective-permute-start.4 = (bf16[96,1024]{1,0:T(8,128)(2,1)S(1)}, bf16[96,1024]{1,0:T(8,128)(2,1)S(1)}, u32[]{:S(2)}, u32[]{:S(2)}) collective-permute-start(bf16[96,1024]{1,0:T(8,128)(2,1)S(1)} %constant_dynamic-update-slice_fusion.refs_1_), channel_id=1, source_target_pairs={{0,1},{1,0},{2,3},{3,2},{4,5},{5,4},{6,7},{7,6},{8,9},{9,8},{10,11... | collective-permute-start | bytes 589832 | tf_op jit(solution)/shard_map/ppermute | solution.py:282
  17.0 9.9 %collective-permute-start.7 = (bf16[32,1024]{1,0:T(8,128)(2,1)S(1)}, bf16[32,1024]{1,0:T(8,128)(2,1)S(1)}, u32[]{:S(2)}, u32[]{:S(2)}) collective-permute-start(bf16[32,1024]{1,0:T(8,128)(2,1)S(1)} %pad_maximum_fusion.refs_0_), channel_id=1, source_target_pairs={{0,3},{1,2},{2,1},{3,0},{4,7},{5,6},{6,5},{7,4},{8,11},{9,10},{10,... | collective-permute-start | bytes 196616 | tf_op jit(solution)/shard_map/ppermute | solution.py:282
  19.4 9.0 %collective-permute-start.5 = (bf16[32,1024]{1,0:T(8,128)(2,1)S(1)}, bf16[32,1024]{1,0:T(8,128)(2,1)S(1)}, u32[]{:S(2)}, u32[]{:S(2)}) collective-permute-start(bf16[32,1024]{1,0:T(8,128)(2,1)S(1)} %pad_maximum_fusion.refs_0_), channel_id=1, source_target_pairs={{0,2},{1,3},{2,0},{3,1},{4,6},{5,7},{6,4},{7,5},{8,10},{9,11},{10,... | collective-permute-start | bytes 196616 | tf_op jit(solution)/shard_map/ppermute | solution.py:282
  26.9 4.3 %collective-permute-start.3 = (bf16[32,1024]{1,0:T(8,128)(2,1)S(1)}, bf16[32,1024]{1,0:T(8,128)(2,1)S(1)}, u32[]{:S(2)}, u32[]{:S(2)}) collective-permute-start(bf16[32,1024]{1,0:T(8,128)(2,1)S(1)} %pad_maximum_fusion.refs_0_), channel_id=1, source_target_pairs={{0,1},{1,0},{2,3},{3,2},{4,5},{5,4},{6,7},{7,6},{8,9},{9,8},{10,11... | collective-permute-start | bytes 196616 | tf_op jit(solution)/shard_map/ppermute | solution.py:282
  31.2 0.7 copy-start
  31.9 40.2 %copy-start.1 = (bf16[1,2,16,5120]{3,2,1,0:T(8,128)(2,1)S(1)}, bf16[1,2,16,5120]{3,2,1,0:T(8,128)(2,1)}, u32[]{:S(2)}) copy-start(bf16[1,2,16,5120]{3,2,1,0:T(8,128)(2,1)} %param.12) | copy-start | bytes 983044
  31.9 47.5 %copy-start.2 = (s32[16]{0:T(128)S(1)}, s32[16]{0:T(128)}, u32[]{:S(2)}) copy-start(s32[16]{0:T(128)} %constant.11.clone) | copy-start | bytes 196
  56.0 7.8 %collective-permute-start.12 = (bf16[96,1024]{1,0:T(8,128)(2,1)S(1)}, bf16[96,1024]{1,0:T(8,128)(2,1)S(1)}, u32[]{:S(2)}, u32[]{:S(2)}) collective-permute-start(bf16[96,1024]{1,0:T(8,128)(2,1)S(1)} %get-tuple-element.22), channel_id=1, source_target_pairs={{0,1},{1,0},{2,3},{3,2},{4,5},{5,4},{6,7},{7,6},{8,9},{9,8},{10,11... | collective-permute-start | bytes 589832 | tf_op jit(solution)/shard_map/ppermute | solution.py:282
  57.6 8.8 %collective-permute-start.13 = (bf16[96,1024]{1,0:T(8,128)(2,1)S(1)}, bf16[96,1024]{1,0:T(8,128)(2,1)S(1)}, u32[]{:S(2)}, u32[]{:S(2)}) collective-permute-start(bf16[96,1024]{1,0:T(8,128)(2,1)S(1)} %get-tuple-element.23), channel_id=1, source_target_pairs={{0,2},{1,3},{2,0},{3,1},{4,6},{5,7},{6,4},{7,5},{8,10},{9,11},{10,... | collective-permute-start | bytes 589832 | tf_op jit(solution)/shard_map/ppermute | solution.py:282
  59.1 8.4 %collective-permute-start.14 = (bf16[96,1024]{1,0:T(8,128)(2,1)S(1)}, bf16[96,1024]{1,0:T(8,128)(2,1)S(1)}, u32[]{:S(2)}, u32[]{:S(2)}) collective-permute-start(bf16[96,1024]{1,0:T(8,128)(2,1)S(1)} %get-tuple-element.24), channel_id=1, source_target_pairs={{0,3},{1,2},{2,1},{3,0},{4,7},{5,6},{6,5},{7,4},{8,11},{9,10},{10,... | collective-permute-start | bytes 589832 | tf_op jit(solution)/shard_map/ppermute | solution.py:282
  59.6 9.4 %collective-permute-start.9 = (bf16[32,1024]{1,0:T(8,128)(2,1)S(1)}, bf16[32,1024]{1,0:T(8,128)(2,1)S(1)}, u32[]{:S(2)}, u32[]{:S(2)}) collective-permute-start(bf16[32,1024]{1,0:T(8,128)(2,1)S(1)} %get-tuple-element.18), channel_id=1, source_target_pairs={{0,1},{1,0},{2,3},{3,2},{4,5},{5,4},{6,7},{7,6},{8,9},{9,8},{10,11... | collective-permute-start | bytes 196616 | tf_op jit(solution)/shard_map/ppermute | solution.py:282
  61.1 16.3 %collective-permute-start.10 = (bf16[32,1024]{1,0:T(8,128)(2,1)S(1)}, bf16[32,1024]{1,0:T(8,128)(2,1)S(1)}, u32[]{:S(2)}, u32[]{:S(2)}) collective-permute-start(bf16[32,1024]{1,0:T(8,128)(2,1)S(1)} %get-tuple-element.19), channel_id=1, source_target_pairs={{0,2},{1,3},{2,0},{3,1},{4,6},{5,7},{6,4},{7,5},{8,10},{9,11},{10,... | collective-permute-start | bytes 196616 | tf_op jit(solution)/shard_map/ppermute | solution.py:282
  63.9 13.5 %collective-permute-start.11 = (bf16[32,1024]{1,0:T(8,128)(2,1)S(1)}, bf16[32,1024]{1,0:T(8,128)(2,1)S(1)}, u32[]{:S(2)}, u32[]{:S(2)}) collective-permute-start(bf16[32,1024]{1,0:T(8,128)(2,1)S(1)} %get-tuple-element.20), channel_id=1, source_target_pairs={{0,3},{1,2},{2,1},{3,0},{4,7},{5,6},{6,5},{7,4},{8,11},{9,10},{10,... | collective-permute-start | bytes 196616 | tf_op jit(solution)/shard_map/ppermute | solution.py:282
  67.6 9.8 %collective-permute-start.15 = (bf16[32,1024]{1,0:T(8,128)(2,1)S(1)}, bf16[32,1024]{1,0:T(8,128)(2,1)S(1)}, u32[]{:S(2)}, u32[]{:S(2)}) collective-permute-start(bf16[32,1024]{1,0:T(8,128)(2,1)S(1)} %get-tuple-element.25), channel_id=1, source_target_pairs={{0,4},{1,5},{2,6},{3,7},{4,0},{5,1},{6,2},{7,3},{8,12},{9,13},{10,... | collective-permute-start | bytes 196616 | tf_op jit(solution)/shard_map/ppermute | solution.py:282
  67.7 9.7 %collective-permute-start.16 = (bf16[32,1024]{1,0:T(8,128)(2,1)S(1)}, bf16[32,1024]{1,0:T(8,128)(2,1)S(1)}, u32[]{:S(2)}, u32[]{:S(2)}) collective-permute-start(bf16[32,1024]{1,0:T(8,128)(2,1)S(1)} %get-tuple-element.26), channel_id=1, source_target_pairs={{0,8},{1,9},{2,10},{3,11},{4,12},{5,13},{6,14},{7,15},{8,0},{9,1},... | collective-permute-start | bytes 196616 | tf_op jit(solution)/shard_map/ppermute | solution.py:282
  69.0 8.4 %collective-permute-start.17 = (bf16[32,1024]{1,0:T(8,128)(2,1)S(1)}, bf16[32,1024]{1,0:T(8,128)(2,1)S(1)}, u32[]{:S(2)}, u32[]{:S(2)}) collective-permute-start(bf16[32,1024]{1,0:T(8,128)(2,1)S(1)} %get-tuple-element.27), channel_id=1, source_target_pairs={{0,12},{1,13},{2,14},{3,15},{4,8},{5,9},{6,10},{7,11},{8,4},{9,5},... | collective-permute-start | bytes 196616 | tf_op jit(solution)/shard_map/ppermute | solution.py:282
  73.8 28.0 %all-to-all-start = ((bf16[16,2,32,160]{3,2,1,0:T(8,128)(2,1)}), bf16[16,2,32,160]{3,2,1,0:T(8,128)(2,1)S(1)}, u32[]{:S(2)}, u32[]{:S(2)}) async-start(bf16[16,2,32,160]{3,2,1,0:T(8,128)(2,1)} %bitcast.11), calls=%async_computation | async-start | bytes 1048576 | tf_op jit(solution)/shard_map/all_to_all | solution.py:303
  77.5 7.2 %collective-permute-start.18 = (bf16[32,1024]{1,0:T(8,128)(2,1)S(1)}, bf16[32,1024]{1,0:T(8,128)(2,1)S(1)}, u32[]{:S(2)}, u32[]{:S(2)}) collective-permute-start(bf16[32,1024]{1,0:T(8,128)(2,1)S(1)} %add_split.3.refs_0_), channel_id=1, source_target_pairs={{0,4},{1,5},{2,6},{3,7},{4,0},{5,1},{6,2},{7,3},{8,12},{9,13},{10,... | collective-permute-start | bytes 196616 | tf_op jit(solution)/shard_map/ppermute | solution.py:282
  79.4 17.9 %collective-permute-start.25 = (bf16[32,1024]{1,0:T(8,128)(2,1)S(1)}, bf16[32,1024]{1,0:T(8,128)(2,1)S(1)}, u32[]{:S(2)}, u32[]{:S(2)}) collective-permute-start(bf16[32,1024]{1,0:T(8,128)(2,1)S(1)} %add_split.3.refs_0_), channel_id=1, source_target_pairs={{0,3},{1,2},{2,1},{3,0},{4,7},{5,6},{6,5},{7,4},{8,11},{9,10},{10,... | collective-permute-start | bytes 196616 | tf_op jit(solution)/shard_map/ppermute | solution.py:282
  81.8 10.5 %collective-permute-start.20 = (bf16[32,1024]{1,0:T(8,128)(2,1)S(1)}, bf16[32,1024]{1,0:T(8,128)(2,1)S(1)}, u32[]{:S(2)}, u32[]{:S(2)}) collective-permute-start(bf16[32,1024]{1,0:T(8,128)(2,1)S(1)} %add_split.3.refs_0_), channel_id=1, source_target_pairs={{0,12},{1,13},{2,14},{3,15},{4,8},{5,9},{6,10},{7,11},{8,4},{9,5},... | collective-permute-start | bytes 196616 | tf_op jit(solution)/shard_map/ppermute | solution.py:282
  84.1 8.1 %collective-permute-start.19 = (bf16[32,1024]{1,0:T(8,128)(2,1)S(1)}, bf16[32,1024]{1,0:T(8,128)(2,1)S(1)}, u32[]{:S(2)}, u32[]{:S(2)}) collective-permute-start(bf16[32,1024]{1,0:T(8,128)(2,1)S(1)} %add_split.3.refs_0_), channel_id=1, source_target_pairs={{0,8},{1,9},{2,10},{3,11},{4,12},{5,13},{6,14},{7,15},{8,0},{9,1},... | collective-permute-start | bytes 196616 | tf_op jit(solution)/shard_map/ppermute | solution.py:282
  92.2 9.5 %collective-permute-start.26 = (bf16[96,1024]{1,0:T(8,128)(2,1)S(1)}, bf16[96,1024]{1,0:T(8,128)(2,1)S(1)}, u32[]{:S(2)}, u32[]{:S(2)}) collective-permute-start(bf16[96,1024]{1,0:T(8,128)(2,1)S(1)} %constant_dynamic-update-slice_fusion.3.refs_1_), channel_id=1, source_target_pairs={{0,3},{1,2},{2,1},{3,0},{4,7},{5,6},{6,5},{7,4},{8,11},{9,10},{10,... | collective-permute-start | bytes 589832 | tf_op jit(solution)/shard_map/ppermute | solution.py:282
  94.6 7.1 %collective-permute-start.24 = (bf16[96,1024]{1,0:T(8,128)(2,1)S(1)}, bf16[96,1024]{1,0:T(8,128)(2,1)S(1)}, u32[]{:S(2)}, u32[]{:S(2)}) collective-permute-start(bf16[96,1024]{1,0:T(8,128)(2,1)S(1)} %constant_dynamic-update-slice_fusion.3.refs_1_), channel_id=1, source_target_pairs={{0,2},{1,3},{2,0},{3,1},{4,6},{5,7},{6,4},{7,5},{8,10},{9,11},{10,... | collective-permute-start | bytes 589832 | tf_op jit(solution)/shard_map/ppermute | solution.py:282
  95.2 6.5 %collective-permute-start.22 = (bf16[96,1024]{1,0:T(8,128)(2,1)S(1)}, bf16[96,1024]{1,0:T(8,128)(2,1)S(1)}, u32[]{:S(2)}, u32[]{:S(2)}) collective-permute-start(bf16[96,1024]{1,0:T(8,128)(2,1)S(1)} %constant_dynamic-update-slice_fusion.3.refs_1_), channel_id=1, source_target_pairs={{0,1},{1,0},{2,3},{3,2},{4,5},{5,4},{6,7},{7,6},{8,9},{9,8},{10,11... | collective-permute-start | bytes 589832 | tf_op jit(solution)/shard_map/ppermute | solution.py:282
  95.8 5.9 %collective-permute-start.23 = (bf16[32,1024]{1,0:T(8,128)(2,1)S(1)}, bf16[32,1024]{1,0:T(8,128)(2,1)S(1)}, u32[]{:S(2)}, u32[]{:S(2)}) collective-permute-start(bf16[32,1024]{1,0:T(8,128)(2,1)S(1)} %add_split.3.refs_0_), channel_id=1, source_target_pairs={{0,2},{1,3},{2,0},{3,1},{4,6},{5,7},{6,4},{7,5},{8,10},{9,11},{10,... | collective-permute-start | bytes 196616 | tf_op jit(solution)/shard_map/ppermute | solution.py:282
  97.3 4.5 %collective-permute-start.21 = (bf16[32,1024]{1,0:T(8,128)(2,1)S(1)}, bf16[32,1024]{1,0:T(8,128)(2,1)S(1)}, u32[]{:S(2)}, u32[]{:S(2)}) collective-permute-start(bf16[32,1024]{1,0:T(8,128)(2,1)S(1)} %add_split.3.refs_0_), channel_id=1, source_target_pairs={{0,1},{1,0},{2,3},{3,2},{4,5},{5,4},{6,7},{7,6},{8,9},{9,8},{10,11... | collective-permute-start | bytes 196616 | tf_op jit(solution)/shard_map/ppermute | solution.py:282
  102.9 2.2 %collective-permute-start.27 = (f32[160,1024]{1,0:T(8,128)S(1)}, f32[160,1024]{1,0:T(8,128)S(1)}, u32[]{:S(2)}, u32[]{:S(2)}) collective-permute-start(f32[160,1024]{1,0:T(8,128)S(1)} %get-tuple-element.29), channel_id=1, source_target_pairs={{0,16},{16,0},{1,17},{17,1},{2,18},{18,2},{3,19},{19,3},{4,20},{20... | collective-permute-start | bytes 1966088 | tf_op jit(solution)/shard_map/ppermute | solution.py:282

commit v3 on v2

--- a/solution.py
+++ b/solution.py
@@ -33,14 +33,13 @@
     rows = sib * pos
     scale = 1.0 / math.sqrt(HEAD)
     scale2 = scale * math.log2(math.e)
-    chunk = 128
-
-    def kern(sib_ref, me_ref, q_hbm, g_hbm, *refs):
+
+    def kern(sib_hbm, me_ref, q_hbm, g_hbm, *refs):
         kv_in = refs[: 2 * inner]
         refs = refs[2 * inner + (before is not None) :]
         dq_hbm = refs[0]
         outs = refs[1 : 2 * inner + 1]
-        kv_s, k_s, v_s, acc, q_buf, g_buf, d_buf, idx_ref, in_sem, out_sem = refs[
+        kv_s, k_s, v_s, acc, q_buf, g_buf, d_buf, sib_ref, idx_ref, sib_sem, in_sem, out_sem = refs[
             2 * inner + 1 :
         ]
         items = [(c, h) for c in range(own) for h in range(group)]
@@ -63,17 +62,20 @@
                 out_sem.at[slot, c, h],
             )
 
+        lists = pltpu.make_async_copy(sib_hbm, sib_ref, sib_sem)
+        lists.start()
         for c, h in items:
             for copy in fetches(0, 0, c, h):
                 copy.start()
+        for i in range(2 * inner):
+            kv_s[starts[i] : starts[i] + sizes[i], :] = kv_in[i][...]
+        lists.wait()
         for c in range(own):
             for j in range(sib):
                 which = sib_ref[c, j]
                 rel = jnp.bitwise_xor(lax.div(which, own), me_ref[0])
                 block = (lax.rem(rel, inner) * OUTER + lax.div(rel, inner)) * own
                 idx_ref[c, j] = (block + lax.rem(which, own)) * pos
-        for i in range(2 * inner):
-            kv_s[starts[i] : starts[i] + sizes[i], :] = kv_in[i][...]
 
         @pl.loop(0, heads)
         def _(g):
@@ -107,52 +109,69 @@
             held = {}
             sums = {}
 
-            def scores(n):
+            def scores(n, w, wide):
                 c, h = items[n]
-                held[n] = (
-                    dg(k_s[c], q_buf[slot, c, :, at[h]], 1, 1),
-                    dg(v_s[c], g_buf[slot, c, :, at[h]], 1, 1),
+                held.setdefault(n, []).append(
+                    (
+                        dg(k_s[c], q_buf[slot, c, w : w + wide, at[h]], 1, 1),
+                        dg(v_s[c], g_buf[slot, c, w : w + wide, at[h]], 1, 1),
+                    )
                 )
 
-            def soften(n):
-                probs = []
-                grads = []
-                for w in range(0, length, chunk):
-                    s = held[n][0][:, w : w + chunk]
-                    dp = held[n][1][:, w : w + chunk]
+            def soften(part, out):
+                for w in range(0, part[0].shape[1], 128):
+                    s = part[0][:, w : w + 128]
+                    dp = part[1][:, w : w + 128]
                     m = jnp.max(s, axis=0, keepdims=True)
                     e = jnp.exp2(s * scale2 - m * scale2)
                     p = e * (1.0 / jnp.sum(e, axis=0, keepdims=True))
                     ph = p.astype(BF16)
                     delta = jnp.sum(ph.astype(F32) * dp, axis=0, keepdims=True)
-                    grads.append((p * (dp - delta)).astype(BF16))
-                    probs.append(ph)
-                held[n] = (jnp.concatenate(probs, axis=1), jnp.concatenate(grads, axis=1))
-
-            def products(n):
+                    out.append((ph, (p * (dp - delta)).astype(BF16)))
+
+            def query_part(n):
                 c, h = items[n]
-                ph, sh = held.pop(n)
-                d_buf[slot, c, :, at[h]] = (dg(sh, k_s[c], 0, 0) * scale).astype(BF16)
-                dk = dg(sh, q_buf[slot, c, :, at[h]], 1, 0)
-                dv = dg(ph, g_buf[slot, c, :, at[h]], 1, 0)
+                d_buf[slot, c, :, at[h]] = (dg(held[n][1], k_s[c], 0, 0) * scale).astype(BF16)
+
+            def key_part(n, which):
+                c, h = items[n]
+                src = g_buf if which else q_buf
+                d = dg(src[slot, c, :, at[h]].T, held[n][1 - which], 1, 1)
                 if h:
-                    dk = sums[c][0] + dk
-                    dv = sums[c][1] + dv
-                sums[c] = (dk, dv)
+                    d = sums[c, which] + d
+                sums[c, which] = d
                 if h == group - 1:
+                    d = d.T
                     for j in range(sib):
                         b = pl.ds(pl.multiple_of(idx_ref[c, j], pos), pos)
-                        acc[b, :HEAD] += dk[j * pos : (j + 1) * pos, :] * scale
-                        acc[b, HEAD:] += dv[j * pos : (j + 1) * pos, :]
-
-            scores(0)
-            for n in range(len(items)):
+                        if which:
+                            acc[b, HEAD:] += d[j * pos : (j + 1) * pos, :]
+                        else:
+                            acc[b, :HEAD] += d[j * pos : (j + 1) * pos, :] * scale
+
+            count = len(items)
+            wide = length // 2
+            for w in range(2):
+                scores(0, w * wide, wide)
+            for n in range(count + 1):
+                work = []
                 if n:
-                    products(n - 1)
-                if n + 1 < len(items):
-                    scores(n + 1)
-                soften(n)
-            products(len(items) - 1)
+                    work += [
+                        (query_part, (n - 1,)), (key_part, (n - 1, 0)), (key_part, (n - 1, 1))
+                    ]
+                if n + 1 < count:
+                    work += [(scores, (n + 1, w * wide, wide)) for w in range(2)]
+                soft = list(held[n]) if n < count else []
+                out = []
+                step = -(-len(work) // max(1, len(soft)))
+                while work or soft:
+                    for f, a in work[:step]:
+                        f(*a)
+                    work = work[step:]
+                    if soft:
+                        soften(soft.pop(0), out)
+                if n < count:
+                    held[n] = [jnp.concatenate([o[i] for o in out], axis=1) for i in (0, 1)]
             for c, h in items:
                 store(g, slot, c, h).start()
             o_at = pl.ds(pl.multiple_of(g * 2 * HEAD, 2 * HEAD), 2 * HEAD)
@@ -167,12 +186,13 @@
     hbm = pl.BlockSpec(memory_space=pl.ANY)
     smem = pl.BlockSpec(memory_space=pltpu.SMEM)
     flops = 20 * own * length * group * heads * rows * HEAD
+    siblings = pltpu.with_memory_space_constraint(siblings, pltpu.HBM)
     queries = pltpu.with_memory_space_constraint(queries, pltpu.HBM)
     grad_out = pltpu.with_memory_space_constraint(grad_out, pltpu.HBM)
     args = [siblings, me, queries, grad_out, *kv_parts] + ([before] if before is not None else [])
     res = pl.pallas_call(
         kern,
-        in_specs=[smem, smem, hbm, hbm]
+        in_specs=[hbm, smem, hbm, hbm]
         + [vmem] * (2 * inner)
         + ([hbm] if before is not None else []),
         out_specs=[hbm] + [vmem] * (2 * inner),
@@ -185,6 +205,8 @@
             pltpu.VMEM((2, own, length, span), BF16),
             pltpu.VMEM((2, own, length, span), BF16),
             pltpu.SMEM((own, sib), jnp.int32),
+            pltpu.SMEM((own, sib), jnp.int32),
+            pltpu.SemaphoreType.DMA(()),
             pltpu.SemaphoreType.DMA((2, own, group, 2)),
             pltpu.SemaphoreType.DMA((2, own, group)),
         ],
@@ -227,11 +249,32 @@
     )(*parts)
 
 
-def weight_parts(place, columns, grads, heads_of, kv_heads):
-    devices, dps, rows, width = columns.shape
+def by_target(hidden, devices, dps):
+    rows, total = hidden.shape
+    width = total // (devices * dps)
+
+    def kern(h_ref, o_ref):
+        for t in range(devices):
+            for d in range(dps):
+                lo = (d * devices + t) * width
+                o_ref[t, :, d * width : (d + 1) * width] = h_ref[:, lo : lo + width]
+
+    vmem = pl.BlockSpec(memory_space=pltpu.VMEM)
+    return pl.pallas_call(
+        kern,
+        in_specs=[vmem],
+        out_specs=vmem,
+        out_shape=jax.ShapeDtypeStruct((devices, rows, dps * width), BF16),
+        compiler_params=pltpu.CompilerParams(vmem_limit_bytes=8 << 20),
+        name="by_target",
+    )(hidden)
+
+
+def weight_parts(place, columns, grads, heads_of, kv_heads, dps):
+    devices, rows, wide = columns.shape
+    width = wide // dps
     chunks = len(grads)
     parts_of = len(grads[0])
-    inner = parts_of // 2
     sizes = [part.shape[0] for part in grads[0]]
     starts = [sum(sizes[:i]) for i in range(parts_of)]
     kvw2 = 2 * kv_heads * HEAD
@@ -239,25 +282,23 @@
     def kern(place_ref, c_ref, *refs):
         g_in = [refs[i * parts_of : (i + 1) * parts_of] for i in range(chunks)]
         outs = refs[chunks * parts_of : chunks * parts_of + dps]
-        g_s, c_s = refs[chunks * parts_of + dps :]
+        g_s, c_s, w_s = refs[chunks * parts_of + dps :]
         col = 0
         for n in range(chunks):
-            wide = 2 * heads_of[n] * HEAD
+            span = 2 * heads_of[n] * HEAD
             for i in range(parts_of):
-                g_s[starts[i] : starts[i] + sizes[i], col : col + wide] = g_in[n][i][...]
-            col += wide
+                g_s[starts[i] : starts[i] + sizes[i], col : col + span] = g_in[n][i][...]
+            col += span
+        for n in range(devices):
+            c_s[n * rows : (n + 1) * rows, :] = c_ref[place_ref[dps + n]]
+        w_s[...] = dg(c_s[...], g_s[...], 0, 0)
         for k in range(dps):
-            which = place_ref[k]
-            for i in range(inner):
-                for o in range(OUTER):
-                    at = (i * OUTER + o) * rows
-                    c_s[at : at + rows, :] = c_ref[place_ref[dps + i * OUTER + o], which]
-            both = dg(c_s[...], g_s[...], 0, 0)
+            at = pl.ds(pl.multiple_of(place_ref[k] * width, 8), width)
             for h in range(kv_heads):
                 lo = 2 * h * HEAD
-                outs[k][:, h * HEAD : (h + 1) * HEAD] = both[:, lo : lo + HEAD]
-                outs[k][:, (kv_heads + h) * HEAD : (kv_heads + h + 1) * HEAD] = both[
-                    :, lo + HEAD : lo + 2 * HEAD
+                outs[k][:, h * HEAD : (h + 1) * HEAD] = w_s[at, lo : lo + HEAD]
+                outs[k][:, (kv_heads + h) * HEAD : (kv_heads + h + 1) * HEAD] = w_s[
+                    at, lo + HEAD : lo + 2 * HEAD
                 ]
 
     vmem = pl.BlockSpec(memory_space=pltpu.VMEM)
@@ -268,7 +309,8 @@
         out_shape=[jax.ShapeDtypeStruct((width, kvw2), F32)] * dps,
         scratch_shapes=[
             pltpu.VMEM((devices * rows, kvw2), BF16),
-            pltpu.VMEM((devices * rows, width), BF16),
+            pltpu.VMEM((devices * rows, wide), BF16),
+            pltpu.VMEM((wide, kvw2), F32),
         ],
         compiler_params=pltpu.CompilerParams(vmem_limit_bytes=32 << 20),
         name="weight_parts",
@@ -297,9 +339,7 @@
         me = lax.axis_index("seq").astype(jnp.int32)
         me_dp = lax.axis_index("dp").astype(jnp.int32)
 
-        width = summary.shape[3] // (n_dp * n_seq)
-        hidden = summary[0].reshape(own * pos, n_dp, n_seq, width)
-        hidden = jnp.transpose(hidden, (2, 1, 0, 3))
+        hidden = by_target(summary[0].reshape(own * pos, summary.shape[3]), n_seq, n_dp)
         columns = lax.all_to_all(hidden, "seq", split_axis=0, concat_axis=0, tiled=True)
 
         kv_parts = []
@@ -344,7 +384,7 @@
             [o * inner + i for i in range(inner) for o in range(OUTER)], dtype=jnp.int32
         )
         place = jnp.concatenate([dps, jnp.bitwise_xor(order, me)])
-        parts = weight_parts(place, columns, grads, CHUNKS, kv_heads)
+        parts = weight_parts(place, columns, grads, CHUNKS, kv_heads, n_dp)
         total = parts[0]
         for k in range(1, n_dp):
             total = total + swap(parts[k], "dp", n_dp, k)

time: 106 us -> 101 us (0.953)
  local copies, waits for them, and re-layouts: 2.45 us -> 0.05 us
  waiting for transfers between devices: 31.6 us -> 30.3 us
    another operation x2 -> x0, local copies, waits for them, and re-layouts: 1.73 us -> none  [per_device(): hidden = summary[0].reshape(own * pos, n_dp, n_seq, width)]
    ppermute x28, waiting for transfers between devices: 31.6 us -> 30.3 us  [swap(): return lax.ppermute(x, axis, [(i, i ^ by) for i in range(count)])]
    pallas_call x1 -> x2, Pallas kernels: 24.1 us -> 23.3 us  [the longest x1 22.4 us: attention(): pl.pallas_call(kern, in_specs=[hbm, smem, hbm, hbm] + [vmem] * (2 * inner...]
  transfers between devices with their start and end apart: 29 -> 29, of which waited for: 10 -> 9; matrix products, arithmetic and copies ran while one was open for 2% -> 0% of each run, Pallas kernels for 0% -> 1%
where the time goes in v3:
time: 101 us
  starting transfers between devices  43.3 us (43%)
  waiting for transfers between devices  30.3 us (30%)
  Pallas kernels  24.7 us (24%)
  other arithmetic  1.8 us (2%)
    ppermute x28, starting transfers between devices, swap(): return lax.ppermute(x, axis, [(i, i ^ by) for i in range(count)])  39.7 us
    ppermute x28, waiting for transfers between devices, swap(): return lax.ppermute(x, axis, [(i, i ^ by) for i in range(count)])  30.3 us
    pallas_call x1, Pallas kernels, attention(): pl.pallas_call(kern, in_specs=[hbm, smem, hbm, hbm] + [vmem] * (2 * inner...  22.4 us
    all_to_all x1, starting transfers between devices, per_device(): lax.all_to_all(hidden, 'seq', split_axis=0, concat_axis=0, tiled=True)  3.55 us
  transfers between devices with their start and end apart: 29, of which 9 were waited for; matrix products, arithmetic and copies ran while one was open for 0% of the time, Pallas kernels for 1%

profile of v3, /device:TPU:0, one launch (start us, length us, event | category | flops | bytes accessed | tf_op | source)
XLA Modules:
  0.0 100.9 jit_solution(12536290340590137378)
XLA Ops:
  0.6 0.8 pad_maximum_fusion.refs_0_
  1.4 3.1 %collective-permute-start = (bf16[32,1024]{1,0:T(8,128)(2,1)S(1)}, bf16[32,1024]{1,0:T(8,128)(2,1)S(1)}, u32[]{:S(2)}, u32[]{:S(2)}) collective-permute-start(bf16[32,1024]{1,0:T(8,128)(2,1)S(1)} %pad_maximum_fusion.refs_0_), channel_id=1, source_target_pairs={{0,4},{1,5},{2,6},{3,7},{4,0},{5,1},{6,2},{7,3},{8,12},{9,13},{10,... | collective-permute-start | bytes 196616 | tf_op jit(solution)/shard_map/ppermute | solution.py:324
  4.5 2.5 %collective-permute-start.2 = (bf16[32,1024]{1,0:T(8,128)(2,1)S(1)}, bf16[32,1024]{1,0:T(8,128)(2,1)S(1)}, u32[]{:S(2)}, u32[]{:S(2)}) collective-permute-start(bf16[32,1024]{1,0:T(8,128)(2,1)S(1)} %pad_maximum_fusion.refs_0_), channel_id=1, source_target_pairs={{0,12},{1,13},{2,14},{3,15},{4,8},{5,9},{6,10},{7,11},{8,4},{9,5},... | collective-permute-start | bytes 196616 | tf_op jit(solution)/shard_map/ppermute | solution.py:324
  6.9 0.1 collective-permute-start.1
  7.1 0.0 collective-permute-done
  7.1 6.3 %collective-permute-done.1 = bf16[32,1024]{1,0:T(8,128)(2,1)S(1)} collective-permute-done((bf16[32,1024]{1,0:T(8,128)(2,1)S(1)}, bf16[32,1024]{1,0:T(8,128)(2,1)S(1)}, u32[]{:S(2)}, u32[]{:S(2)}) %collective-permute-start.1) | collective-permute-done | bytes 65568 | tf_op jit(solution)/shard_map/ppermute | solution.py:324
  13.4 0.0 collective-permute-done.2
  13.4 2.5 %collective-permute-start.8 = (bf16[96,1024]{1,0:T(8,128)(2,1)S(1)}, bf16[96,1024]{1,0:T(8,128)(2,1)S(1)}, u32[]{:S(2)}, u32[]{:S(2)}) collective-permute-start(bf16[96,1024]{1,0:T(8,128)(2,1)S(1)} %constant_dynamic-update-slice_fusion.refs_1_), channel_id=1, source_target_pairs={{0,3},{1,2},{2,1},{3,0},{4,7},{5,6},{6,5},{7,4},{8,11},{9,10},{10,... | collective-permute-start | bytes 589832 | tf_op jit(solution)/shard_map/ppermute | solution.py:324
  15.9 0.5 collective-permute-start.6
  16.4 0.5 collective-permute-start.4
  17.0 2.4 %collective-permute-start.7 = (bf16[32,1024]{1,0:T(8,128)(2,1)S(1)}, bf16[32,1024]{1,0:T(8,128)(2,1)S(1)}, u32[]{:S(2)}, u32[]{:S(2)}) collective-permute-start(bf16[32,1024]{1,0:T(8,128)(2,1)S(1)} %pad_maximum_fusion.refs_0_), channel_id=1, source_target_pairs={{0,3},{1,2},{2,1},{3,0},{4,7},{5,6},{6,5},{7,4},{8,11},{9,10},{10,... | collective-permute-start | bytes 196616 | tf_op jit(solution)/shard_map/ppermute | solution.py:324
  19.4 0.5 collective-permute-start.5
  19.9 7.0 %collective-permute-done.7.refs_6_ = bf16[32,1024]{1,0:T(8,128)(2,1)S(1)} collective-permute-done((bf16[32,1024]{1,0:T(8,128)(2,1)S(1)}, bf16[32,1024]{1,0:T(8,128)(2,1)S(1)}, u32[]{:S(2)}, u32[]{:S(2)}) %collective-permute-start.7) | collective-permute-done | bytes 65568 | tf_op jit(solution)/shard_map/ppermute | solution.py:324
  26.9 1.5 %collective-permute-start.3 = (bf16[32,1024]{1,0:T(8,128)(2,1)S(1)}, bf16[32,1024]{1,0:T(8,128)(2,1)S(1)}, u32[]{:S(2)}, u32[]{:S(2)}) collective-permute-start(bf16[32,1024]{1,0:T(8,128)(2,1)S(1)} %pad_maximum_fusion.refs_0_), channel_id=1, source_target_pairs={{0,1},{1,0},{2,3},{3,2},{4,5},{5,4},{6,7},{7,6},{8,9},{9,8},{10,11... | collective-permute-start | bytes 196616 | tf_op jit(solution)/shard_map/ppermute | solution.py:324
  28.4 0.0 collective-permute-done.5.refs_4_
  28.4 2.8 %collective-permute-done.3.refs_2_ = bf16[32,1024]{1,0:T(8,128)(2,1)S(1)} collective-permute-done((bf16[32,1024]{1,0:T(8,128)(2,1)S(1)}, bf16[32,1024]{1,0:T(8,128)(2,1)S(1)}, u32[]{:S(2)}, u32[]{:S(2)}) %collective-permute-start.3) | collective-permute-done | bytes 65568 | tf_op jit(solution)/shard_map/ppermute | solution.py:324
  31.2 0.0 collective-permute-done.8.refs_7_
  31.2 0.0 collective-permute-done.6.refs_5_
  31.2 0.0 collective-permute-done.4.refs_3_
  31.2 0.0 copy-start
  31.2 0.0 copy-start.1
  31.2 22.4 %attention.1 = (bf16[2,512,2560]{2,1,0:T(8,128)(2,1)}, bf16[32,1024]{1,0:T(8,128)(2,1)S(1)}, bf16[96,1024]{1,0:T(8,128)(2,1)S(1)}, bf16[32,1024]{1,0:T(8,128)(2,...) custom-call(s32[2,16]{1,0:T(2,128)} %bitcast.13, ...), custom_call_target="tpu_custom_call" | custom-call | flops 13421772800 | bytes 15728640 | tf_op jit(solution)/shard_map/attention/pallas_call | solution.py:193
  53.6 1.6 %collective-permute-start.12 = (bf16[96,1024]{1,0:T(8,128)(2,1)S(1)}, bf16[96,1024]{1,0:T(8,128)(2,1)S(1)}, u32[]{:S(2)}, u32[]{:S(2)}) collective-permute-start(bf16[96,1024]{1,0:T(8,128)(2,1)S(1)} %get-tuple-element.22), channel_id=1, source_target_pairs={{0,1},{1,0},{2,3},{3,2},{4,5},{5,4},{6,7},{7,6},{8,9},{9,8},{10,11... | collective-permute-start | bytes 589832 | tf_op jit(solution)/shard_map/ppermute | solution.py:324
  55.2 1.5 %collective-permute-start.13 = (bf16[96,1024]{1,0:T(8,128)(2,1)S(1)}, bf16[96,1024]{1,0:T(8,128)(2,1)S(1)}, u32[]{:S(2)}, u32[]{:S(2)}) collective-permute-start(bf16[96,1024]{1,0:T(8,128)(2,1)S(1)} %get-tuple-element.23), channel_id=1, source_target_pairs={{0,2},{1,3},{2,0},{3,1},{4,6},{5,7},{6,4},{7,5},{8,10},{9,11},{10,... | collective-permute-start | bytes 589832 | tf_op jit(solution)/shard_map/ppermute | solution.py:324
  56.7 0.5 collective-permute-start.14
  57.2 1.5 %collective-permute-start.9 = (bf16[32,1024]{1,0:T(8,128)(2,1)S(1)}, bf16[32,1024]{1,0:T(8,128)(2,1)S(1)}, u32[]{:S(2)}, u32[]{:S(2)}) collective-permute-start(bf16[32,1024]{1,0:T(8,128)(2,1)S(1)} %get-tuple-element.18), channel_id=1, source_target_pairs={{0,1},{1,0},{2,3},{3,2},{4,5},{5,4},{6,7},{7,6},{8,9},{9,8},{10,11... | collective-permute-start | bytes 196616 | tf_op jit(solution)/shard_map/ppermute | solution.py:324
  58.7 1.5 %collective-permute-start.10 = (bf16[32,1024]{1,0:T(8,128)(2,1)S(1)}, bf16[32,1024]{1,0:T(8,128)(2,1)S(1)}, u32[]{:S(2)}, u32[]{:S(2)}) collective-permute-start(bf16[32,1024]{1,0:T(8,128)(2,1)S(1)} %get-tuple-element.19), channel_id=1, source_target_pairs={{0,2},{1,3},{2,0},{3,1},{4,6},{5,7},{6,4},{7,5},{8,10},{9,11},{10,... | collective-permute-start | bytes 196616 | tf_op jit(solution)/shard_map/ppermute | solution.py:324
  60.2 1.3 %collective-permute-done.12.refs_1_ = bf16[96,1024]{1,0:T(8,128)(2,1)S(1)} collective-permute-done((bf16[96,1024]{1,0:T(8,128)(2,1)S(1)}, bf16[96,1024]{1,0:T(8,128)(2,1)S(1)}, u32[]{:S(2)}, u32[]{:S(2)}) %collective-permute-start.12) | collective-permute-done | bytes 196640 | tf_op jit(solution)/shard_map/ppermute | solution.py:324
  61.5 2.4 %collective-permute-start.11 = (bf16[32,1024]{1,0:T(8,128)(2,1)S(1)}, bf16[32,1024]{1,0:T(8,128)(2,1)S(1)}, u32[]{:S(2)}, u32[]{:S(2)}) collective-permute-start(bf16[32,1024]{1,0:T(8,128)(2,1)S(1)} %get-tuple-element.20), channel_id=1, source_target_pairs={{0,3},{1,2},{2,1},{3,0},{4,7},{5,6},{6,5},{7,4},{8,11},{9,10},{10,... | collective-permute-start | bytes 196616 | tf_op jit(solution)/shard_map/ppermute | solution.py:324
  63.9 0.1 collective-permute-done.13.refs_2_
  64.0 1.1 %collective-permute-done.14.refs_3_ = bf16[96,1024]{1,0:T(8,128)(2,1)S(1)} collective-permute-done((bf16[96,1024]{1,0:T(8,128)(2,1)S(1)}, bf16[96,1024]{1,0:T(8,128)(2,1)S(1)}, u32[]{:S(2)}, u32[]{:S(2)}) %collective-permute-start.14) | collective-permute-done | bytes 196640 | tf_op jit(solution)/shard_map/ppermute | solution.py:324
  65.1 0.1 add_split.2
  65.2 0.1 collective-permute-start.15
  65.2 1.4 %collective-permute-start.16 = (bf16[32,1024]{1,0:T(8,128)(2,1)S(1)}, bf16[32,1024]{1,0:T(8,128)(2,1)S(1)}, u32[]{:S(2)}, u32[]{:S(2)}) collective-permute-start(bf16[32,1024]{1,0:T(8,128)(2,1)S(1)} %get-tuple-element.26), channel_id=1, source_target_pairs={{0,8},{1,9},{2,10},{3,11},{4,12},{5,13},{6,14},{7,15},{8,0},{9,1},... | collective-permute-start | bytes 196616 | tf_op jit(solution)/shard_map/ppermute | solution.py:324
  66.6 0.0 collective-permute-done.9.refs_1_
  66.6 3.0 %collective-permute-start.17 = (bf16[32,1024]{1,0:T(8,128)(2,1)S(1)}, bf16[32,1024]{1,0:T(8,128)(2,1)S(1)}, u32[]{:S(2)}, u32[]{:S(2)}) collective-permute-start(bf16[32,1024]{1,0:T(8,128)(2,1)S(1)} %get-tuple-element.27), channel_id=1, source_target_pairs={{0,12},{1,13},{2,14},{3,15},{4,8},{5,9},{6,10},{7,11},{8,4},{9,5},... | collective-permute-start | bytes 196616 | tf_op jit(solution)/shard_map/ppermute | solution.py:324
  69.6 0.9 by_target.1
  70.5 3.6 %all-to-all-start = ((bf16[16,32,320]{2,1,0:T(8,128)(2,1)}), bf16[16,32,320]{2,1,0:T(8,128)(2,1)S(1)}, u32[]{:S(2)}, u32[]{:S(2)}) async-start(bf16[16,32,320]{2,1,0:T(8,128)(2,1)} %by_target.1), calls=%async_computation | async-start | bytes 786432 | tf_op jit(solution)/shard_map/all_to_all | solution.py:343
  74.1 0.0 collective-permute-done.10.refs_2_
  74.1 0.0 collective-permute-done.11.refs_3_
  74.1 0.0 collective-permute-done.15.refs_4_
  74.1 0.0 collective-permute-done.16.refs_5_
  74.1 0.0 collective-permute-done.17.refs_6_
  74.2 0.1 add_split.3.refs_0_
  74.2 1.9 %collective-permute-start.18 = (bf16[32,1024]{1,0:T(8,128)(2,1)S(1)}, bf16[32,1024]{1,0:T(8,128)(2,1)S(1)}, u32[]{:S(2)}, u32[]{:S(2)}) collective-permute-start(bf16[32,1024]{1,0:T(8,128)(2,1)S(1)} %add_split.3.refs_0_), channel_id=1, source_target_pairs={{0,4},{1,5},{2,6},{3,7},{4,0},{5,1},{6,2},{7,3},{8,12},{9,13},{10,... | collective-permute-start | bytes 196616 | tf_op jit(solution)/shard_map/ppermute | solution.py:324
  76.1 2.4 %collective-permute-start.25 = (bf16[32,1024]{1,0:T(8,128)(2,1)S(1)}, bf16[32,1024]{1,0:T(8,128)(2,1)S(1)}, u32[]{:S(2)}, u32[]{:S(2)}) collective-permute-start(bf16[32,1024]{1,0:T(8,128)(2,1)S(1)} %add_split.3.refs_0_), channel_id=1, source_target_pairs={{0,3},{1,2},{2,1},{3,0},{4,7},{5,6},{6,5},{7,4},{8,11},{9,10},{10,... | collective-permute-start | bytes 196616 | tf_op jit(solution)/shard_map/ppermute | solution.py:324
  78.5 2.4 %collective-permute-start.20 = (bf16[32,1024]{1,0:T(8,128)(2,1)S(1)}, bf16[32,1024]{1,0:T(8,128)(2,1)S(1)}, u32[]{:S(2)}, u32[]{:S(2)}) collective-permute-start(bf16[32,1024]{1,0:T(8,128)(2,1)S(1)} %add_split.3.refs_0_), channel_id=1, source_target_pairs={{0,12},{1,13},{2,14},{3,15},{4,8},{5,9},{6,10},{7,11},{8,4},{9,5},... | collective-permute-start | bytes 196616 | tf_op jit(solution)/shard_map/ppermute | solution.py:324
  80.9 0.0 collective-permute-start.19
  80.9 5.8 %collective-permute-done.19 = bf16[32,1024]{1,0:T(8,128)(2,1)S(1)} collective-permute-done((bf16[32,1024]{1,0:T(8,128)(2,1)S(1)}, bf16[32,1024]{1,0:T(8,128)(2,1)S(1)}, u32[]{:S(2)}, u32[]{:S(2)}) %collective-permute-start.19) | collective-permute-done | bytes 65568 | tf_op jit(solution)/shard_map/ppermute | solution.py:324
  86.8 1.8 %collective-permute-start.26 = (bf16[96,1024]{1,0:T(8,128)(2,1)S(1)}, bf16[96,1024]{1,0:T(8,128)(2,1)S(1)}, u32[]{:S(2)}, u32[]{:S(2)}) collective-permute-start(bf16[96,1024]{1,0:T(8,128)(2,1)S(1)} %constant_dynamic-update-slice_fusion.3.refs_1_), channel_id=1, source_target_pairs={{0,3},{1,2},{2,1},{3,0},{4,7},{5,6},{6,5},{7,4},{8,11},{9,10},{10,... | collective-permute-start | bytes 589832 | tf_op jit(solution)/shard_map/ppermute | solution.py:324
  88.6 0.9 collective-permute-start.24
  89.5 0.8 collective-permute-start.22
  90.3 1.3 %collective-permute-start.23 = (bf16[32,1024]{1,0:T(8,128)(2,1)S(1)}, bf16[32,1024]{1,0:T(8,128)(2,1)S(1)}, u32[]{:S(2)}, u32[]{:S(2)}) collective-permute-start(bf16[32,1024]{1,0:T(8,128)(2,1)S(1)} %add_split.3.refs_0_), channel_id=1, source_target_pairs={{0,2},{1,3},{2,0},{3,1},{4,6},{5,7},{6,4},{7,5},{8,10},{9,11},{10,... | collective-permute-start | bytes 196616 | tf_op jit(solution)/shard_map/ppermute | solution.py:324
  91.7 1.0 collective-permute-start.21
  92.7 0.1 pad_add_fusion.place_ref
  92.7 3.8 %collective-permute-done.23.refs_4_ = bf16[32,1024]{1,0:T(8,128)(2,1)S(1)} collective-permute-done((bf16[32,1024]{1,0:T(8,128)(2,1)S(1)}, bf16[32,1024]{1,0:T(8,128)(2,1)S(1)}, u32[]{:S(2)}, u32[]{:S(2)}) %collective-permute-start.23) | collective-permute-done | bytes 65568 | tf_op jit(solution)/shard_map/ppermute | solution.py:324
  96.6 0.0 all-to-all-done.c_ref
  96.6 0.0 collective-permute-done.26.refs_7_
  96.6 0.0 collective-permute-done.24.refs_5_
  96.6 0.0 collective-permute-done.22.refs_3_
  96.6 1.2 %weight_parts.1 = (f32[160,1024]{1,0:T(8,128)S(1)}, f32[160,1024]{1,0:T(8,128)S(1)}) custom-call(s32[18]{0:T(128)S(1)} %pad_add_fusion.place_ref, bf16[16,32,320]{2,1,0:T(8,128)(2,1)S(1)} %all-to-all-done.c_ref, bf16[32,1024]{1,0:T(8,128)(2,1)S(1)} %add_split.3.refs_0_, bf16[96,1024]{1,0:T(8,128)(2,1)S(1)} %constant_dynamic-update-slice_fusion.3.refs_1_, ...), custom_call_target="tpu_custom_call" | custom-call | tf_op jit(solution)/shard_map/weight_parts/pallas_call | solution.py:305
  97.8 0.1 collective-permute-start.27
  97.9 2.1 %collective-permute-done.27 = f32[160,1024]{1,0:T(8,128)S(1)} collective-permute-done((f32[160,1024]{1,0:T(8,128)S(1)}, f32[160,1024]{1,0:T(8,128)S(1)}, u32[]{:S(2)}, u32[]{:S(2)}) %collective-permute-start.27) | collective-permute-done | bytes 655392 | tf_op jit(solution)/shard_map/ppermute | solution.py:324
  100.0 0.9 add.3
  (14 shorter events, 0.1 us)
Async XLA Ops:
  1.4 5.6 %collective-permute-start = (bf16[32,1024]{1,0:T(8,128)(2,1)S(1)}, bf16[32,1024]{1,0:T(8,128)(2,1)S(1)}, u32[]{:S(2)}, u32[]{:S(2)}) collective-permute-start(bf16[32,1024]{1,0:T(8,128)(2,1)S(1)} %pad_maximum_fusion.refs_0_), channel_id=1, source_target_pairs={{0,4},{1,5},{2,6},{3,7},{4,0},{5,1},{6,2},{7,3},{8,12},{9,13},{10,... | collective-permute-start | bytes 196616 | tf_op jit(solution)/shard_map/ppermute | solution.py:324
  4.5 8.9 %collective-permute-start.2 = (bf16[32,1024]{1,0:T(8,128)(2,1)S(1)}, bf16[32,1024]{1,0:T(8,128)(2,1)S(1)}, u32[]{:S(2)}, u32[]{:S(2)}) collective-permute-start(bf16[32,1024]{1,0:T(8,128)(2,1)S(1)} %pad_maximum_fusion.refs_0_), channel_id=1, source_target_pairs={{0,12},{1,13},{2,14},{3,15},{4,8},{5,9},{6,10},{7,11},{8,4},{9,5},... | collective-permute-start | bytes 196616 | tf_op jit(solution)/shard_map/ppermute | solution.py:324
  6.9 6.4 %collective-permute-start.1 = (bf16[32,1024]{1,0:T(8,128)(2,1)S(1)}, bf16[32,1024]{1,0:T(8,128)(2,1)S(1)}, u32[]{:S(2)}, u32[]{:S(2)}) collective-permute-start(bf16[32,1024]{1,0:T(8,128)(2,1)S(1)} %pad_maximum_fusion.refs_0_), channel_id=1, source_target_pairs={{0,8},{1,9},{2,10},{3,11},{4,12},{5,13},{6,14},{7,15},{8,0},{9,1},... | collective-permute-start | bytes 196616 | tf_op jit(solution)/shard_map/ppermute | solution.py:324
  13.4 17.8 %collective-permute-start.8 = (bf16[96,1024]{1,0:T(8,128)(2,1)S(1)}, bf16[96,1024]{1,0:T(8,128)(2,1)S(1)}, u32[]{:S(2)}, u32[]{:S(2)}) collective-permute-start(bf16[96,1024]{1,0:T(8,128)(2,1)S(1)} %constant_dynamic-update-slice_fusion.refs_1_), channel_id=1, source_target_pairs={{0,3},{1,2},{2,1},{3,0},{4,7},{5,6},{6,5},{7,4},{8,11},{9,10},{10,... | collective-permute-start | bytes 589832 | tf_op jit(solution)/shard_map/ppermute | solution.py:324
  15.9 15.3 %collective-permute-start.6 = (bf16[96,1024]{1,0:T(8,128)(2,1)S(1)}, bf16[96,1024]{1,0:T(8,128)(2,1)S(1)}, u32[]{:S(2)}, u32[]{:S(2)}) collective-permute-start(bf16[96,1024]{1,0:T(8,128)(2,1)S(1)} %constant_dynamic-update-slice_fusion.refs_1_), channel_id=1, source_target_pairs={{0,2},{1,3},{2,0},{3,1},{4,6},{5,7},{6,4},{7,5},{8,10},{9,11},{10,... | collective-permute-start | bytes 589832 | tf_op jit(solution)/shard_map/ppermute | solution.py:324
  16.4 14.8 %collective-permute-start.4 = (bf16[96,1024]{1,0:T(8,128)(2,1)S(1)}, bf16[96,1024]{1,0:T(8,128)(2,1)S(1)}, u32[]{:S(2)}, u32[]{:S(2)}) collective-permute-start(bf16[96,1024]{1,0:T(8,128)(2,1)S(1)} %constant_dynamic-update-slice_fusion.refs_1_), channel_id=1, source_target_pairs={{0,1},{1,0},{2,3},{3,2},{4,5},{5,4},{6,7},{7,6},{8,9},{9,8},{10,11... | collective-permute-start | bytes 589832 | tf_op jit(solution)/shard_map/ppermute | solution.py:324
  17.0 9.9 %collective-permute-start.7 = (bf16[32,1024]{1,0:T(8,128)(2,1)S(1)}, bf16[32,1024]{1,0:T(8,128)(2,1)S(1)}, u32[]{:S(2)}, u32[]{:S(2)}) collective-permute-start(bf16[32,1024]{1,0:T(8,128)(2,1)S(1)} %pad_maximum_fusion.refs_0_), channel_id=1, source_target_pairs={{0,3},{1,2},{2,1},{3,0},{4,7},{5,6},{6,5},{7,4},{8,11},{9,10},{10,... | collective-permute-start | bytes 196616 | tf_op jit(solution)/shard_map/ppermute | solution.py:324
  19.4 9.0 %collective-permute-start.5 = (bf16[32,1024]{1,0:T(8,128)(2,1)S(1)}, bf16[32,1024]{1,0:T(8,128)(2,1)S(1)}, u32[]{:S(2)}, u32[]{:S(2)}) collective-permute-start(bf16[32,1024]{1,0:T(8,128)(2,1)S(1)} %pad_maximum_fusion.refs_0_), channel_id=1, source_target_pairs={{0,2},{1,3},{2,0},{3,1},{4,6},{5,7},{6,4},{7,5},{8,10},{9,11},{10,... | collective-permute-start | bytes 196616 | tf_op jit(solution)/shard_map/ppermute | solution.py:324
  26.9 4.3 %collective-permute-start.3 = (bf16[32,1024]{1,0:T(8,128)(2,1)S(1)}, bf16[32,1024]{1,0:T(8,128)(2,1)S(1)}, u32[]{:S(2)}, u32[]{:S(2)}) collective-permute-start(bf16[32,1024]{1,0:T(8,128)(2,1)S(1)} %pad_maximum_fusion.refs_0_), channel_id=1, source_target_pairs={{0,1},{1,0},{2,3},{3,2},{4,5},{5,4},{6,7},{7,6},{8,9},{9,8},{10,11... | collective-permute-start | bytes 196616 | tf_op jit(solution)/shard_map/ppermute | solution.py:324
  31.2 38.4 %copy-start = (bf16[1,2,16,5120]{3,2,1,0:T(8,128)(2,1)S(1)}, bf16[1,2,16,5120]{3,2,1,0:T(8,128)(2,1)}, u32[]{:S(2)}) copy-start(bf16[1,2,16,5120]{3,2,1,0:T(8,128)(2,1)} %param.12) | copy-start | bytes 983044
  31.2 44.9 %copy-start.1 = (s32[16]{0:T(128)S(1)}, s32[16]{0:T(128)}, u32[]{:S(2)}) copy-start(s32[16]{0:T(128)} %constant.11.clone) | copy-start | bytes 196
  53.6 7.8 %collective-permute-start.12 = (bf16[96,1024]{1,0:T(8,128)(2,1)S(1)}, bf16[96,1024]{1,0:T(8,128)(2,1)S(1)}, u32[]{:S(2)}, u32[]{:S(2)}) collective-permute-start(bf16[96,1024]{1,0:T(8,128)(2,1)S(1)} %get-tuple-element.22), channel_id=1, source_target_pairs={{0,1},{1,0},{2,3},{3,2},{4,5},{5,4},{6,7},{7,6},{8,9},{9,8},{10,11... | collective-permute-start | bytes 589832 | tf_op jit(solution)/shard_map/ppermute | solution.py:324
  55.2 8.8 %collective-permute-start.13 = (bf16[96,1024]{1,0:T(8,128)(2,1)S(1)}, bf16[96,1024]{1,0:T(8,128)(2,1)S(1)}, u32[]{:S(2)}, u32[]{:S(2)}) collective-permute-start(bf16[96,1024]{1,0:T(8,128)(2,1)S(1)} %get-tuple-element.23), channel_id=1, source_target_pairs={{0,2},{1,3},{2,0},{3,1},{4,6},{5,7},{6,4},{7,5},{8,10},{9,11},{10,... | collective-permute-start | bytes 589832 | tf_op jit(solution)/shard_map/ppermute | solution.py:324
  56.7 8.4 %collective-permute-start.14 = (bf16[96,1024]{1,0:T(8,128)(2,1)S(1)}, bf16[96,1024]{1,0:T(8,128)(2,1)S(1)}, u32[]{:S(2)}, u32[]{:S(2)}) collective-permute-start(bf16[96,1024]{1,0:T(8,128)(2,1)S(1)} %get-tuple-element.24), channel_id=1, source_target_pairs={{0,3},{1,2},{2,1},{3,0},{4,7},{5,6},{6,5},{7,4},{8,11},{9,10},{10,... | collective-permute-start | bytes 589832 | tf_op jit(solution)/shard_map/ppermute | solution.py:324
  57.2 9.4 %collective-permute-start.9 = (bf16[32,1024]{1,0:T(8,128)(2,1)S(1)}, bf16[32,1024]{1,0:T(8,128)(2,1)S(1)}, u32[]{:S(2)}, u32[]{:S(2)}) collective-permute-start(bf16[32,1024]{1,0:T(8,128)(2,1)S(1)} %get-tuple-element.18), channel_id=1, source_target_pairs={{0,1},{1,0},{2,3},{3,2},{4,5},{5,4},{6,7},{7,6},{8,9},{9,8},{10,11... | collective-permute-start | bytes 196616 | tf_op jit(solution)/shard_map/ppermute | solution.py:324
  58.7 15.4 %collective-permute-start.10 = (bf16[32,1024]{1,0:T(8,128)(2,1)S(1)}, bf16[32,1024]{1,0:T(8,128)(2,1)S(1)}, u32[]{:S(2)}, u32[]{:S(2)}) collective-permute-start(bf16[32,1024]{1,0:T(8,128)(2,1)S(1)} %get-tuple-element.19), channel_id=1, source_target_pairs={{0,2},{1,3},{2,0},{3,1},{4,6},{5,7},{6,4},{7,5},{8,10},{9,11},{10,... | collective-permute-start | bytes 196616 | tf_op jit(solution)/shard_map/ppermute | solution.py:324
  61.5 12.6 %collective-permute-start.11 = (bf16[32,1024]{1,0:T(8,128)(2,1)S(1)}, bf16[32,1024]{1,0:T(8,128)(2,1)S(1)}, u32[]{:S(2)}, u32[]{:S(2)}) collective-permute-start(bf16[32,1024]{1,0:T(8,128)(2,1)S(1)} %get-tuple-element.20), channel_id=1, source_target_pairs={{0,3},{1,2},{2,1},{3,0},{4,7},{5,6},{6,5},{7,4},{8,11},{9,10},{10,... | collective-permute-start | bytes 196616 | tf_op jit(solution)/shard_map/ppermute | solution.py:324
  65.2 9.0 %collective-permute-start.15 = (bf16[32,1024]{1,0:T(8,128)(2,1)S(1)}, bf16[32,1024]{1,0:T(8,128)(2,1)S(1)}, u32[]{:S(2)}, u32[]{:S(2)}) collective-permute-start(bf16[32,1024]{1,0:T(8,128)(2,1)S(1)} %get-tuple-element.25), channel_id=1, source_target_pairs={{0,4},{1,5},{2,6},{3,7},{4,0},{5,1},{6,2},{7,3},{8,12},{9,13},{10,... | collective-permute-start | bytes 196616 | tf_op jit(solution)/shard_map/ppermute | solution.py:324
  65.2 8.9 %collective-permute-start.16 = (bf16[32,1024]{1,0:T(8,128)(2,1)S(1)}, bf16[32,1024]{1,0:T(8,128)(2,1)S(1)}, u32[]{:S(2)}, u32[]{:S(2)}) collective-permute-start(bf16[32,1024]{1,0:T(8,128)(2,1)S(1)} %get-tuple-element.26), channel_id=1, source_target_pairs={{0,8},{1,9},{2,10},{3,11},{4,12},{5,13},{6,14},{7,15},{8,0},{9,1},... | collective-permute-start | bytes 196616 | tf_op jit(solution)/shard_map/ppermute | solution.py:324
  66.6 7.5 %collective-permute-start.17 = (bf16[32,1024]{1,0:T(8,128)(2,1)S(1)}, bf16[32,1024]{1,0:T(8,128)(2,1)S(1)}, u32[]{:S(2)}, u32[]{:S(2)}) collective-permute-start(bf16[32,1024]{1,0:T(8,128)(2,1)S(1)} %get-tuple-element.27), channel_id=1, source_target_pairs={{0,12},{1,13},{2,14},{3,15},{4,8},{5,9},{6,10},{7,11},{8,4},{9,5},... | collective-permute-start | bytes 196616 | tf_op jit(solution)/shard_map/ppermute | solution.py:324
  70.5 26.0 %all-to-all-start = ((bf16[16,32,320]{2,1,0:T(8,128)(2,1)}), bf16[16,32,320]{2,1,0:T(8,128)(2,1)S(1)}, u32[]{:S(2)}, u32[]{:S(2)}) async-start(bf16[16,32,320]{2,1,0:T(8,128)(2,1)} %by_target.1), calls=%async_computation | async-start | bytes 786432 | tf_op jit(solution)/shard_map/all_to_all | solution.py:343
  74.2 6.7 %collective-permute-start.18 = (bf16[32,1024]{1,0:T(8,128)(2,1)S(1)}, bf16[32,1024]{1,0:T(8,128)(2,1)S(1)}, u32[]{:S(2)}, u32[]{:S(2)}) collective-permute-start(bf16[32,1024]{1,0:T(8,128)(2,1)S(1)} %add_split.3.refs_0_), channel_id=1, source_target_pairs={{0,4},{1,5},{2,6},{3,7},{4,0},{5,1},{6,2},{7,3},{8,12},{9,13},{10,... | collective-permute-start | bytes 196616 | tf_op jit(solution)/shard_map/ppermute | solution.py:324
  76.1 15.5 %collective-permute-start.25 = (bf16[32,1024]{1,0:T(8,128)(2,1)S(1)}, bf16[32,1024]{1,0:T(8,128)(2,1)S(1)}, u32[]{:S(2)}, u32[]{:S(2)}) collective-permute-start(bf16[32,1024]{1,0:T(8,128)(2,1)S(1)} %add_split.3.refs_0_), channel_id=1, source_target_pairs={{0,3},{1,2},{2,1},{3,0},{4,7},{5,6},{6,5},{7,4},{8,11},{9,10},{10,... | collective-permute-start | bytes 196616 | tf_op jit(solution)/shard_map/ppermute | solution.py:324
  78.5 8.3 %collective-permute-start.20 = (bf16[32,1024]{1,0:T(8,128)(2,1)S(1)}, bf16[32,1024]{1,0:T(8,128)(2,1)S(1)}, u32[]{:S(2)}, u32[]{:S(2)}) collective-permute-start(bf16[32,1024]{1,0:T(8,128)(2,1)S(1)} %add_split.3.refs_0_), channel_id=1, source_target_pairs={{0,12},{1,13},{2,14},{3,15},{4,8},{5,9},{6,10},{7,11},{8,4},{9,5},... | collective-permute-start | bytes 196616 | tf_op jit(solution)/shard_map/ppermute | solution.py:324
  80.9 5.9 %collective-permute-start.19 = (bf16[32,1024]{1,0:T(8,128)(2,1)S(1)}, bf16[32,1024]{1,0:T(8,128)(2,1)S(1)}, u32[]{:S(2)}, u32[]{:S(2)}) collective-permute-start(bf16[32,1024]{1,0:T(8,128)(2,1)S(1)} %add_split.3.refs_0_), channel_id=1, source_target_pairs={{0,8},{1,9},{2,10},{3,11},{4,12},{5,13},{6,14},{7,15},{8,0},{9,1},... | collective-permute-start | bytes 196616 | tf_op jit(solution)/shard_map/ppermute | solution.py:324
  86.8 9.8 %collective-permute-start.26 = (bf16[96,1024]{1,0:T(8,128)(2,1)S(1)}, bf16[96,1024]{1,0:T(8,128)(2,1)S(1)}, u32[]{:S(2)}, u32[]{:S(2)}) collective-permute-start(bf16[96,1024]{1,0:T(8,128)(2,1)S(1)} %constant_dynamic-update-slice_fusion.3.refs_1_), channel_id=1, source_target_pairs={{0,3},{1,2},{2,1},{3,0},{4,7},{5,6},{6,5},{7,4},{8,11},{9,10},{10,... | collective-permute-start | bytes 589832 | tf_op jit(solution)/shard_map/ppermute | solution.py:324
  88.6 8.0 %collective-permute-start.24 = (bf16[96,1024]{1,0:T(8,128)(2,1)S(1)}, bf16[96,1024]{1,0:T(8,128)(2,1)S(1)}, u32[]{:S(2)}, u32[]{:S(2)}) collective-permute-start(bf16[96,1024]{1,0:T(8,128)(2,1)S(1)} %constant_dynamic-update-slice_fusion.3.refs_1_), channel_id=1, source_target_pairs={{0,2},{1,3},{2,0},{3,1},{4,6},{5,7},{6,4},{7,5},{8,10},{9,11},{10,... | collective-permute-start | bytes 589832 | tf_op jit(solution)/shard_map/ppermute | solution.py:324
  89.5 7.1 %collective-permute-start.22 = (bf16[96,1024]{1,0:T(8,128)(2,1)S(1)}, bf16[96,1024]{1,0:T(8,128)(2,1)S(1)}, u32[]{:S(2)}, u32[]{:S(2)}) collective-permute-start(bf16[96,1024]{1,0:T(8,128)(2,1)S(1)} %constant_dynamic-update-slice_fusion.3.refs_1_), channel_id=1, source_target_pairs={{0,1},{1,0},{2,3},{3,2},{4,5},{5,4},{6,7},{7,6},{8,9},{9,8},{10,11... | collective-permute-start | bytes 589832 | tf_op jit(solution)/shard_map/ppermute | solution.py:324
  90.3 6.2 %collective-permute-start.23 = (bf16[32,1024]{1,0:T(8,128)(2,1)S(1)}, bf16[32,1024]{1,0:T(8,128)(2,1)S(1)}, u32[]{:S(2)}, u32[]{:S(2)}) collective-permute-start(bf16[32,1024]{1,0:T(8,128)(2,1)S(1)} %add_split.3.refs_0_), channel_id=1, source_target_pairs={{0,2},{1,3},{2,0},{3,1},{4,6},{5,7},{6,4},{7,5},{8,10},{9,11},{10,... | collective-permute-start | bytes 196616 | tf_op jit(solution)/shard_map/ppermute | solution.py:324
  91.7 4.9 %collective-permute-start.21 = (bf16[32,1024]{1,0:T(8,128)(2,1)S(1)}, bf16[32,1024]{1,0:T(8,128)(2,1)S(1)}, u32[]{:S(2)}, u32[]{:S(2)}) collective-permute-start(bf16[32,1024]{1,0:T(8,128)(2,1)S(1)} %add_split.3.refs_0_), channel_id=1, source_target_pairs={{0,1},{1,0},{2,3},{3,2},{4,5},{5,4},{6,7},{7,6},{8,9},{9,8},{10,11... | collective-permute-start | bytes 196616 | tf_op jit(solution)/shard_map/ppermute | solution.py:324
  97.8 2.2 %collective-permute-start.27 = (f32[160,1024]{1,0:T(8,128)S(1)}, f32[160,1024]{1,0:T(8,128)S(1)}, u32[]{:S(2)}, u32[]{:S(2)}) collective-permute-start(f32[160,1024]{1,0:T(8,128)S(1)} %get-tuple-element.29), channel_id=1, source_target_pairs={{0,16},{16,0},{1,17},{17,1},{2,18},{18,2},{3,19},{19,3},{4,20},{20... | collective-permute-start | bytes 1966088 | tf_op jit(solution)/shard_map/ppermute | solution.py:324

commit v4 on v3

--- a/solution.py
+++ b/solution.py
@@ -12,6 +12,7 @@
 OUTER = 4
 VMEM_LIMIT = 28 << 20
 CHUNKS = (4,)
+EARLY = {"rows": True, "sum": False, "grads": True}
 F32 = jnp.float32
 BF16 = jnp.bfloat16
 
@@ -20,12 +21,13 @@
     return lax.dot_general(a, b, (((ca,), (cb,)), ((), ())), preferred_element_type=F32)
 
 
-def attention(siblings, me, queries, grad_out, kv_parts, pos, first, heads, kv_heads, before):
+def attention(siblings, me, queries, grad_out, kv_parts, sizes_out, pos, first, heads, kv_heads, before):
     own, length, width = queries.shape
-    inner = len(kv_parts) // 2
     sizes = [part.shape[0] for part in kv_parts]
-    starts = [sum(sizes[:i]) for i in range(2 * inner)]
+    starts = [sum(sizes[:i]) for i in range(len(sizes))]
+    starts_out = [sum(sizes_out[:i]) for i in range(len(sizes_out))]
     total = sum(sizes)
+    inner = total // (OUTER * queries.shape[0] * pos)
     kvw2 = kv_parts[0].shape[1]
     group = width // (kv_heads * HEAD)
     span = group * HEAD
@@ -35,12 +37,12 @@
     scale2 = scale * math.log2(math.e)
 
     def kern(sib_hbm, me_ref, q_hbm, g_hbm, *refs):
-        kv_in = refs[: 2 * inner]
-        refs = refs[2 * inner + (before is not None) :]
+        kv_in = refs[: len(sizes)]
+        refs = refs[len(sizes) + (before is not None) :]
         dq_hbm = refs[0]
-        outs = refs[1 : 2 * inner + 1]
+        outs = refs[1 : len(sizes_out) + 1]
         kv_s, k_s, v_s, acc, q_buf, g_buf, d_buf, sib_ref, idx_ref, sib_sem, in_sem, out_sem = refs[
-            2 * inner + 1 :
+            len(sizes_out) + 1 :
         ]
         items = [(c, h) for c in range(own) for h in range(group)]
 
@@ -67,7 +69,7 @@
         for c, h in items:
             for copy in fetches(0, 0, c, h):
                 copy.start()
-        for i in range(2 * inner):
+        for i in range(len(sizes)):
             kv_s[starts[i] : starts[i] + sizes[i], :] = kv_in[i][...]
         lists.wait()
         for c in range(own):
@@ -170,13 +172,16 @@
                     work = work[step:]
                     if soft:
                         soften(soft.pop(0), out)
+                if n and items[n - 1][1] == group - 1:
+                    for one in range(group):
+                        store(g, slot, items[n - 1][0], one).start()
                 if n < count:
                     held[n] = [jnp.concatenate([o[i] for o in out], axis=1) for i in (0, 1)]
-            for c, h in items:
-                store(g, slot, c, h).start()
             o_at = pl.ds(pl.multiple_of(g * 2 * HEAD, 2 * HEAD), 2 * HEAD)
-            for i in range(2 * inner):
-                outs[i][:, o_at] = acc[starts[i] : starts[i] + sizes[i], :].astype(BF16)
+            for i in range(len(sizes_out)):
+                outs[i][:, o_at] = acc[
+                    starts_out[i] : starts_out[i] + sizes_out[i], :
+                ].astype(BF16)
 
         for g in range(max(heads - 2, 0), heads):
             for c, h in items:
@@ -193,9 +198,9 @@
     res = pl.pallas_call(
         kern,
         in_specs=[hbm, smem, hbm, hbm]
-        + [vmem] * (2 * inner)
+        + [vmem] * len(sizes)
         + ([hbm] if before is not None else []),
-        out_specs=[hbm] + [vmem] * (2 * inner),
+        out_specs=[hbm] + [vmem] * len(sizes_out),
         scratch_shapes=[
             pltpu.VMEM((total, kvw2), BF16),
             pltpu.VMEM((own, rows, HEAD), BF16),
@@ -211,8 +216,8 @@
             pltpu.SemaphoreType.DMA((2, own, group)),
         ],
         out_shape=[jax.ShapeDtypeStruct(queries.shape, BF16)]
-        + [jax.ShapeDtypeStruct((size, kvw2), BF16) for size in sizes],
-        input_output_aliases={4 + 2 * inner: 0} if before is not None else {},
+        + [jax.ShapeDtypeStruct((size, kvw2), BF16) for size in sizes_out],
+        input_output_aliases={4 + len(sizes): 0} if before is not None else {},
         compiler_params=pltpu.CompilerParams(vmem_limit_bytes=VMEM_LIMIT),
         cost_estimate=pl.CostEstimate(
             flops=flops, bytes_accessed=6 * queries.size, transcendentals=0
@@ -326,8 +331,11 @@
     def seq_swap(x, by):
         return swap(x, "seq", n_seq, by)
 
-    def gather_all(x):
+    def gather_all(x, early):
         rest = [seq_swap(x, k * inner) for k in range(1, OUTER)]
+        if not early:
+            rest = jnp.concatenate([x] + rest, axis=0)
+            return [rest] + [seq_swap(rest, k) for k in range(1, inner)]
         ones = [x] + [seq_swap(x, k) for k in range(1, inner)]
         rest = jnp.concatenate(rest, axis=0)
         rests = [rest] + [seq_swap(rest, k) for k in range(1, inner)]
@@ -350,7 +358,8 @@
                 gather_all(
                     jnp.concatenate(
                         [keys_in[0, :, :, at], input_values[0, :, :, at]], axis=-1
-                    ).reshape(own * pos, 2 * heads * HEAD)
+                    ).reshape(own * pos, 2 * heads * HEAD),
+                    EARLY["rows"],
                 )
             )
             first += heads
@@ -364,20 +373,23 @@
                 me[None],
                 queries[0],
                 grad_out[0],
-                 kv_parts[n], pos, first, heads, kv_heads, query_grad
+                 kv_parts[n],
+                ([own * pos, (OUTER - 1) * own * pos] if EARLY["sum"] else [OUTER * own * pos])
+                * inner,
+                pos, first, heads, kv_heads, query_grad
             )
             first += heads
-            ones, rests = terms[::2], terms[1::2]
+            ones, rests = (terms[::2], terms[1::2]) if EARLY["sum"] else ([], terms)
             near = add_split(
-                [rests[0]] + [seq_swap(rests[k], k) for k in range(1, inner)], OUTER - 1
+                [rests[0]] + [seq_swap(rests[k], k) for k in range(1, inner)],
+                rests[0].shape[0] // (own * pos),
             )
-            mine = add_split(
-                [ones[0]]
-                + [seq_swap(ones[k], k) for k in range(1, inner)]
-                + [seq_swap(near[k - 1], k * inner) for k in range(1, OUTER)],
-                1,
-            )[0]
-            grads.append(gather_all(mine))
+            here = [ones[0]] if EARLY["sum"] else [near[0]]
+            here += [seq_swap(ones[k], k) for k in range(1, len(ones))]
+            away = near if EARLY["sum"] else near[1:]
+            here += [seq_swap(away[k - 1], k * inner) for k in range(1, OUTER)]
+            mine = add_split(here, 1)[0]
+            grads.append(gather_all(mine, EARLY["grads"]))
 
         dps = jnp.bitwise_xor(jnp.arange(n_dp, dtype=jnp.int32), me_dp)
         order = jnp.array(

time: 101 us -> 102 us (level)
  waiting for transfers between devices: 30.3 us -> 36.4 us
  starting transfers between devices: 43.3 us -> 38.4 us
    ppermute x28 -> x25, waiting for transfers between devices: 30.3 us -> 36.4 us  [swap(): return lax.ppermute(x, axis, [(i, i ^ by) for i in range(count)])]
    ppermute x28 -> x25, starting transfers between devices: 39.7 us -> 34.9 us  [swap(): return lax.ppermute(x, axis, [(i, i ^ by) for i in range(count)])]
  transfers between devices with their start and end apart: 29 -> 26, of which waited for: 9 -> 9; matrix products, arithmetic and copies ran while one was open for 0% -> 0% of each run, Pallas kernels for 1% -> 1%
where the time goes in v4:
time: 102 us
  starting transfers between devices  38.4 us (38%)
  waiting for transfers between devices  36.4 us (36%)
  Pallas kernels  24.5 us (24%)
  other arithmetic  1.8 us (2%)
    ppermute x25, waiting for transfers between devices, swap(): return lax.ppermute(x, axis, [(i, i ^ by) for i in range(count)])  36.4 us
    ppermute x25, starting transfers between devices, swap(): return lax.ppermute(x, axis, [(i, i ^ by) for i in range(count)])  34.9 us
    pallas_call x1, Pallas kernels, attention(): pl.pallas_call(kern, in_specs=[hbm, smem, hbm, hbm] + [vmem] * len(sizes)...  22.2 us
    all_to_all x1, starting transfers between devices, per_device(): lax.all_to_all(hidden, 'seq', split_axis=0, concat_axis=0, tiled=True)  3.55 us
  transfers between devices with their start and end apart: 26, of which 9 were waited for; matrix products, arithmetic and copies ran while one was open for 0% of the time, Pallas kernels for 1%

profile of v4, /device:TPU:0, one launch (start us, length us, event | category | flops | bytes accessed | tf_op | source)
XLA Modules:
  0.0 101.9 jit_solution(12206538179617047693)
XLA Ops:
  0.6 0.8 pad_maximum_fusion.refs_0_
  1.4 3.1 %collective-permute-start = (bf16[32,1024]{1,0:T(8,128)(2,1)S(1)}, bf16[32,1024]{1,0:T(8,128)(2,1)S(1)}, u32[]{:S(2)}, u32[]{:S(2)}) collective-permute-start(bf16[32,1024]{1,0:T(8,128)(2,1)S(1)} %pad_maximum_fusion.refs_0_), channel_id=1, source_target_pairs={{0,4},{1,5},{2,6},{3,7},{4,0},{5,1},{6,2},{7,3},{8,12},{9,13},{10,... | collective-permute-start | bytes 196616 | tf_op jit(solution)/shard_map/ppermute | solution.py:329
  4.5 2.5 %collective-permute-start.2 = (bf16[32,1024]{1,0:T(8,128)(2,1)S(1)}, bf16[32,1024]{1,0:T(8,128)(2,1)S(1)}, u32[]{:S(2)}, u32[]{:S(2)}) collective-permute-start(bf16[32,1024]{1,0:T(8,128)(2,1)S(1)} %pad_maximum_fusion.refs_0_), channel_id=1, source_target_pairs={{0,12},{1,13},{2,14},{3,15},{4,8},{5,9},{6,10},{7,11},{8,4},{9,5},... | collective-permute-start | bytes 196616 | tf_op jit(solution)/shard_map/ppermute | solution.py:329
  6.9 0.1 collective-permute-start.1
  7.1 0.0 collective-permute-done
  7.1 6.3 %collective-permute-done.1 = bf16[32,1024]{1,0:T(8,128)(2,1)S(1)} collective-permute-done((bf16[32,1024]{1,0:T(8,128)(2,1)S(1)}, bf16[32,1024]{1,0:T(8,128)(2,1)S(1)}, u32[]{:S(2)}, u32[]{:S(2)}) %collective-permute-start.1) | collective-permute-done | bytes 65568 | tf_op jit(solution)/shard_map/ppermute | solution.py:329
  13.4 0.0 collective-permute-done.2
  13.4 2.5 %collective-permute-start.8 = (bf16[96,1024]{1,0:T(8,128)(2,1)S(1)}, bf16[96,1024]{1,0:T(8,128)(2,1)S(1)}, u32[]{:S(2)}, u32[]{:S(2)}) collective-permute-start(bf16[96,1024]{1,0:T(8,128)(2,1)S(1)} %constant_dynamic-update-slice_fusion.refs_1_), channel_id=1, source_target_pairs={{0,3},{1,2},{2,1},{3,0},{4,7},{5,6},{6,5},{7,4},{8,11},{9,10},{10,... | collective-permute-start | bytes 589832 | tf_op jit(solution)/shard_map/ppermute | solution.py:329
  15.9 0.5 collective-permute-start.6
  16.4 0.5 collective-permute-start.4
  17.0 2.4 %collective-permute-start.7 = (bf16[32,1024]{1,0:T(8,128)(2,1)S(1)}, bf16[32,1024]{1,0:T(8,128)(2,1)S(1)}, u32[]{:S(2)}, u32[]{:S(2)}) collective-permute-start(bf16[32,1024]{1,0:T(8,128)(2,1)S(1)} %pad_maximum_fusion.refs_0_), channel_id=1, source_target_pairs={{0,3},{1,2},{2,1},{3,0},{4,7},{5,6},{6,5},{7,4},{8,11},{9,10},{10,... | collective-permute-start | bytes 196616 | tf_op jit(solution)/shard_map/ppermute | solution.py:329
  19.4 0.5 collective-permute-start.5
  19.9 7.0 %collective-permute-done.7.refs_6_ = bf16[32,1024]{1,0:T(8,128)(2,1)S(1)} collective-permute-done((bf16[32,1024]{1,0:T(8,128)(2,1)S(1)}, bf16[32,1024]{1,0:T(8,128)(2,1)S(1)}, u32[]{:S(2)}, u32[]{:S(2)}) %collective-permute-start.7) | collective-permute-done | bytes 65568 | tf_op jit(solution)/shard_map/ppermute | solution.py:329
  26.9 1.5 %collective-permute-start.3 = (bf16[32,1024]{1,0:T(8,128)(2,1)S(1)}, bf16[32,1024]{1,0:T(8,128)(2,1)S(1)}, u32[]{:S(2)}, u32[]{:S(2)}) collective-permute-start(bf16[32,1024]{1,0:T(8,128)(2,1)S(1)} %pad_maximum_fusion.refs_0_), channel_id=1, source_target_pairs={{0,1},{1,0},{2,3},{3,2},{4,5},{5,4},{6,7},{7,6},{8,9},{9,8},{10,11... | collective-permute-start | bytes 196616 | tf_op jit(solution)/shard_map/ppermute | solution.py:329
  28.4 0.0 collective-permute-done.5.refs_4_
  28.4 2.8 %collective-permute-done.3.refs_2_ = bf16[32,1024]{1,0:T(8,128)(2,1)S(1)} collective-permute-done((bf16[32,1024]{1,0:T(8,128)(2,1)S(1)}, bf16[32,1024]{1,0:T(8,128)(2,1)S(1)}, u32[]{:S(2)}, u32[]{:S(2)}) %collective-permute-start.3) | collective-permute-done | bytes 65568 | tf_op jit(solution)/shard_map/ppermute | solution.py:329
  31.2 0.0 collective-permute-done.8.refs_7_
  31.2 0.0 collective-permute-done.6.refs_5_
  31.2 0.0 collective-permute-done.4.refs_3_
  31.2 0.0 copy-start
  31.2 0.0 copy-start.1
  31.2 22.2 %attention.1 = (bf16[2,512,2560]{2,1,0:T(8,128)(2,1)}, bf16[128,1024]{1,0:T(8,128)(2,1)S(1)}, bf16[128,1024]{1,0:T(8,128)(2,1)S(1)}, bf16[128,1024]{1,0:T(8,128)(2,1)S(1)}, bf16[128,1024]{1,0:T(8,128)(2,1)S(1)}) custom-call(s32[2,16]{1,0:T(2,128)} %bitcast.13, s32[1]{0:T(128)} %bitcast.1.me_ref, bf16[2,512,2560]{2,1,0:T(8,128)(2,1)} %bitcast.11, ...), custom_call_target="tpu_custom_call" | custom-call | flops 13421772800 | bytes 15728640 | tf_op jit(solution)/shard_map/attention/pallas_call | solution.py:198
  53.4 1.6 %collective-permute-start.9 = (bf16[128,1024]{1,0:T(8,128)(2,1)S(1)}, bf16[128,1024]{1,0:T(8,128)(2,1)S(1)}, u32[]{:S(2)}, u32[]{:S(2)}) collective-permute-start(bf16[128,1024]{1,0:T(8,128)(2,1)S(1)} %get-tuple-element.15), channel_id=1, source_target_pairs={{0,1},{1,0},{2,3},{3,2},{4,5},{5,4},{6,7},{7,6},{8,9},{9,8},{10,11... | collective-permute-start | bytes 786440 | tf_op jit(solution)/shard_map/ppermute | solution.py:329
  54.9 1.5 %collective-permute-start.10 = (bf16[128,1024]{1,0:T(8,128)(2,1)S(1)}, bf16[128,1024]{1,0:T(8,128)(2,1)S(1)}, u32[]{:S(2)}, u32[]{:S(2)}) collective-permute-start(bf16[128,1024]{1,0:T(8,128)(2,1)S(1)} %get-tuple-element.16), channel_id=1, source_target_pairs={{0,2},{1,3},{2,0},{3,1},{4,6},{5,7},{6,4},{7,5},{8,10},{9,11},{10,... | collective-permute-start | bytes 786440 | tf_op jit(solution)/shard_map/ppermute | solution.py:329
  56.5 0.5 collective-permute-start.11
  56.9 5.1 %collective-permute-done.9.refs_1_ = bf16[128,1024]{1,0:T(8,128)(2,1)S(1)} collective-permute-done((bf16[128,1024]{1,0:T(8,128)(2,1)S(1)}, bf16[128,1024]{1,0:T(8,128)(2,1)S(1)}, u32[]{:S(2)}, u32[]{:S(2)}) %collective-permute-start.9) | collective-permute-done | bytes 262176 | tf_op jit(solution)/shard_map/ppermute | solution.py:329
  62.0 4.0 %collective-permute-done.10.refs_2_ = bf16[128,1024]{1,0:T(8,128)(2,1)S(1)} collective-permute-done((bf16[128,1024]{1,0:T(8,128)(2,1)S(1)}, bf16[128,1024]{1,0:T(8,128)(2,1)S(1)}, u32[]{:S(2)}, u32[]{:S(2)}) %collective-permute-start.10) | collective-permute-done | bytes 262176 | tf_op jit(solution)/shard_map/ppermute | solution.py:329
  66.1 0.0 collective-permute-done.11.refs_3_
  66.1 0.1 add_split.2
  66.2 0.1 collective-permute-start.12
  66.3 1.6 %collective-permute-start.13 = (bf16[32,1024]{1,0:T(8,128)(2,1)S(1)}, bf16[32,1024]{1,0:T(8,128)(2,1)S(1)}, u32[]{:S(2)}, u32[]{:S(2)}) collective-permute-start(bf16[32,1024]{1,0:T(8,128)(2,1)S(1)} %get-tuple-element.20), channel_id=1, source_target_pairs={{0,8},{1,9},{2,10},{3,11},{4,12},{5,13},{6,14},{7,15},{8,0},{9,1},... | collective-permute-start | bytes 196616 | tf_op jit(solution)/shard_map/ppermute | solution.py:329
  67.9 2.8 %collective-permute-start.14 = (bf16[32,1024]{1,0:T(8,128)(2,1)S(1)}, bf16[32,1024]{1,0:T(8,128)(2,1)S(1)}, u32[]{:S(2)}, u32[]{:S(2)}) collective-permute-start(bf16[32,1024]{1,0:T(8,128)(2,1)S(1)} %get-tuple-element.21), channel_id=1, source_target_pairs={{0,12},{1,13},{2,14},{3,15},{4,8},{5,9},{6,10},{7,11},{8,4},{9,5},... | collective-permute-start | bytes 196616 | tf_op jit(solution)/shard_map/ppermute | solution.py:329
  70.7 0.0 copy-done
  70.7 0.9 by_target.1
  71.6 3.6 %all-to-all-start = ((bf16[16,32,320]{2,1,0:T(8,128)(2,1)}), bf16[16,32,320]{2,1,0:T(8,128)(2,1)S(1)}, u32[]{:S(2)}, u32[]{:S(2)}) async-start(bf16[16,32,320]{2,1,0:T(8,128)(2,1)} %by_target.1), calls=%async_computation | async-start | bytes 786432 | tf_op jit(solution)/shard_map/all_to_all | solution.py:351
  75.1 0.0 collective-permute-done.12.refs_1_
  75.1 0.0 collective-permute-done.13.refs_2_
  75.2 0.0 collective-permute-done.14.refs_3_
  75.2 1.9 %collective-permute-start.15 = (bf16[32,1024]{1,0:T(8,128)(2,1)S(1)}, bf16[32,1024]{1,0:T(8,128)(2,1)S(1)}, u32[]{:S(2)}, u32[]{:S(2)}) collective-permute-start(bf16[32,1024]{1,0:T(8,128)(2,1)S(1)} %add_split.3.refs_0_), channel_id=1, source_target_pairs={{0,4},{1,5},{2,6},{3,7},{4,0},{5,1},{6,2},{7,3},{8,12},{9,13},{10,... | collective-permute-start | bytes 196616 | tf_op jit(solution)/shard_map/ppermute | solution.py:329
  77.1 0.0 copy-done.1
  77.1 2.4 %collective-permute-start.22 = (bf16[32,1024]{1,0:T(8,128)(2,1)S(1)}, bf16[32,1024]{1,0:T(8,128)(2,1)S(1)}, u32[]{:S(2)}, u32[]{:S(2)}) collective-permute-start(bf16[32,1024]{1,0:T(8,128)(2,1)S(1)} %add_split.3.refs_0_), channel_id=1, source_target_pairs={{0,3},{1,2},{2,1},{3,0},{4,7},{5,6},{6,5},{7,4},{8,11},{9,10},{10,... | collective-permute-start | bytes 196616 | tf_op jit(solution)/shard_map/ppermute | solution.py:329
  79.5 2.4 %collective-permute-start.17 = (bf16[32,1024]{1,0:T(8,128)(2,1)S(1)}, bf16[32,1024]{1,0:T(8,128)(2,1)S(1)}, u32[]{:S(2)}, u32[]{:S(2)}) collective-permute-start(bf16[32,1024]{1,0:T(8,128)(2,1)S(1)} %add_split.3.refs_0_), channel_id=1, source_target_pairs={{0,12},{1,13},{2,14},{3,15},{4,8},{5,9},{6,10},{7,11},{8,4},{9,5},... | collective-permute-start | bytes 196616 | tf_op jit(solution)/shard_map/ppermute | solution.py:329
  81.9 0.0 collective-permute-start.16
  81.9 1.2 %collective-permute-done.15 = bf16[32,1024]{1,0:T(8,128)(2,1)S(1)} collective-permute-done((bf16[32,1024]{1,0:T(8,128)(2,1)S(1)}, bf16[32,1024]{1,0:T(8,128)(2,1)S(1)}, u32[]{:S(2)}, u32[]{:S(2)}) %collective-permute-start.15) | collective-permute-done | bytes 65568 | tf_op jit(solution)/shard_map/ppermute | solution.py:329
  83.1 4.9 %collective-permute-done.16 = bf16[32,1024]{1,0:T(8,128)(2,1)S(1)} collective-permute-done((bf16[32,1024]{1,0:T(8,128)(2,1)S(1)}, bf16[32,1024]{1,0:T(8,128)(2,1)S(1)}, u32[]{:S(2)}, u32[]{:S(2)}) %collective-permute-start.16) | collective-permute-done | bytes 65568 | tf_op jit(solution)/shard_map/ppermute | solution.py:329
  88.1 0.0 collective-permute-done.17
  88.1 2.4 %collective-permute-start.23 = (bf16[96,1024]{1,0:T(8,128)(2,1)S(1)}, bf16[96,1024]{1,0:T(8,128)(2,1)S(1)}, u32[]{:S(2)}, u32[]{:S(2)}) collective-permute-start(bf16[96,1024]{1,0:T(8,128)(2,1)S(1)} %constant_dynamic-update-slice_fusion.3.refs_1_), channel_id=1, source_target_pairs={{0,3},{1,2},{2,1},{3,0},{4,7},{5,6},{6,5},{7,4},{8,11},{9,10},{10,... | collective-permute-start | bytes 589832 | tf_op jit(solution)/shard_map/ppermute | solution.py:329
  90.5 0.6 collective-permute-start.21
  91.0 0.6 collective-permute-start.19
  91.7 1.4 %collective-permute-start.20 = (bf16[32,1024]{1,0:T(8,128)(2,1)S(1)}, bf16[32,1024]{1,0:T(8,128)(2,1)S(1)}, u32[]{:S(2)}, u32[]{:S(2)}) collective-permute-start(bf16[32,1024]{1,0:T(8,128)(2,1)S(1)} %add_split.3.refs_0_), channel_id=1, source_target_pairs={{0,2},{1,3},{2,0},{3,1},{4,6},{5,7},{6,4},{7,5},{8,10},{9,11},{10,... | collective-permute-start | bytes 196616 | tf_op jit(solution)/shard_map/ppermute | solution.py:329
  93.1 0.0 collective-permute-done.22.refs_6_
  93.1 1.5 %collective-permute-start.18 = (bf16[32,1024]{1,0:T(8,128)(2,1)S(1)}, bf16[32,1024]{1,0:T(8,128)(2,1)S(1)}, u32[]{:S(2)}, u32[]{:S(2)}) collective-permute-start(bf16[32,1024]{1,0:T(8,128)(2,1)S(1)} %add_split.3.refs_0_), channel_id=1, source_target_pairs={{0,1},{1,0},{2,3},{3,2},{4,5},{5,4},{6,7},{7,6},{8,9},{9,8},{10,11... | collective-permute-start | bytes 196616 | tf_op jit(solution)/shard_map/ppermute | solution.py:329
  94.6 0.1 pad_add_fusion.place_ref
  94.6 0.0 all-to-all-done.c_ref
  94.6 2.9 %collective-permute-done.20.refs_4_ = bf16[32,1024]{1,0:T(8,128)(2,1)S(1)} collective-permute-done((bf16[32,1024]{1,0:T(8,128)(2,1)S(1)}, bf16[32,1024]{1,0:T(8,128)(2,1)S(1)}, u32[]{:S(2)}, u32[]{:S(2)}) %collective-permute-start.20) | collective-permute-done | bytes 65568 | tf_op jit(solution)/shard_map/ppermute | solution.py:329
  97.5 0.0 collective-permute-done.18.refs_2_
  97.5 0.0 collective-permute-done.23.refs_7_
  97.5 0.0 collective-permute-done.21.refs_5_
  97.5 0.0 collective-permute-done.19.refs_3_
  97.6 1.2 %weight_parts.1 = (f32[160,1024]{1,0:T(8,128)S(1)}, f32[160,1024]{1,0:T(8,128)S(1)}) custom-call(s32[18]{0:T(128)S(1)} %pad_add_fusion.place_ref, bf16[16,32,320]{2,1,0:T(8,128)(2,1)S(1)} %all-to-all-done.c_ref, bf16[32,1024]{1,0:T(8,128)(2,1)S(1)} %add_split.3.refs_0_, bf16[96,1024]{1,0:T(8,128)(2,1)S(1)} %constant_dynamic-update-slice_fusion.3.refs_1_, ...), custom_call_target="tpu_custom_call" | custom-call | tf_op jit(solution)/shard_map/weight_parts/pallas_call | solution.py:310
  98.8 0.1 collective-permute-start.24
  98.9 2.1 %collective-permute-done.24 = f32[160,1024]{1,0:T(8,128)S(1)} collective-permute-done((f32[160,1024]{1,0:T(8,128)S(1)}, f32[160,1024]{1,0:T(8,128)S(1)}, u32[]{:S(2)}, u32[]{:S(2)}) %collective-permute-start.24) | collective-permute-done | bytes 655392 | tf_op jit(solution)/shard_map/ppermute | solution.py:329
  101.0 0.9 add.3
  (9 shorter events, 0.1 us)
Async XLA Ops:
  1.4 5.6 %collective-permute-start = (bf16[32,1024]{1,0:T(8,128)(2,1)S(1)}, bf16[32,1024]{1,0:T(8,128)(2,1)S(1)}, u32[]{:S(2)}, u32[]{:S(2)}) collective-permute-start(bf16[32,1024]{1,0:T(8,128)(2,1)S(1)} %pad_maximum_fusion.refs_0_), channel_id=1, source_target_pairs={{0,4},{1,5},{2,6},{3,7},{4,0},{5,1},{6,2},{7,3},{8,12},{9,13},{10,... | collective-permute-start | bytes 196616 | tf_op jit(solution)/shard_map/ppermute | solution.py:329
  4.5 8.9 %collective-permute-start.2 = (bf16[32,1024]{1,0:T(8,128)(2,1)S(1)}, bf16[32,1024]{1,0:T(8,128)(2,1)S(1)}, u32[]{:S(2)}, u32[]{:S(2)}) collective-permute-start(bf16[32,1024]{1,0:T(8,128)(2,1)S(1)} %pad_maximum_fusion.refs_0_), channel_id=1, source_target_pairs={{0,12},{1,13},{2,14},{3,15},{4,8},{5,9},{6,10},{7,11},{8,4},{9,5},... | collective-permute-start | bytes 196616 | tf_op jit(solution)/shard_map/ppermute | solution.py:329
  6.9 6.4 %collective-permute-start.1 = (bf16[32,1024]{1,0:T(8,128)(2,1)S(1)}, bf16[32,1024]{1,0:T(8,128)(2,1)S(1)}, u32[]{:S(2)}, u32[]{:S(2)}) collective-permute-start(bf16[32,1024]{1,0:T(8,128)(2,1)S(1)} %pad_maximum_fusion.refs_0_), channel_id=1, source_target_pairs={{0,8},{1,9},{2,10},{3,11},{4,12},{5,13},{6,14},{7,15},{8,0},{9,1},... | collective-permute-start | bytes 196616 | tf_op jit(solution)/shard_map/ppermute | solution.py:329
  13.4 17.8 %collective-permute-start.8 = (bf16[96,1024]{1,0:T(8,128)(2,1)S(1)}, bf16[96,1024]{1,0:T(8,128)(2,1)S(1)}, u32[]{:S(2)}, u32[]{:S(2)}) collective-permute-start(bf16[96,1024]{1,0:T(8,128)(2,1)S(1)} %constant_dynamic-update-slice_fusion.refs_1_), channel_id=1, source_target_pairs={{0,3},{1,2},{2,1},{3,0},{4,7},{5,6},{6,5},{7,4},{8,11},{9,10},{10,... | collective-permute-start | bytes 589832 | tf_op jit(solution)/shard_map/ppermute | solution.py:329
  15.9 15.3 %collective-permute-start.6 = (bf16[96,1024]{1,0:T(8,128)(2,1)S(1)}, bf16[96,1024]{1,0:T(8,128)(2,1)S(1)}, u32[]{:S(2)}, u32[]{:S(2)}) collective-permute-start(bf16[96,1024]{1,0:T(8,128)(2,1)S(1)} %constant_dynamic-update-slice_fusion.refs_1_), channel_id=1, source_target_pairs={{0,2},{1,3},{2,0},{3,1},{4,6},{5,7},{6,4},{7,5},{8,10},{9,11},{10,... | collective-permute-start | bytes 589832 | tf_op jit(solution)/shard_map/ppermute | solution.py:329
  16.4 14.8 %collective-permute-start.4 = (bf16[96,1024]{1,0:T(8,128)(2,1)S(1)}, bf16[96,1024]{1,0:T(8,128)(2,1)S(1)}, u32[]{:S(2)}, u32[]{:S(2)}) collective-permute-start(bf16[96,1024]{1,0:T(8,128)(2,1)S(1)} %constant_dynamic-update-slice_fusion.refs_1_), channel_id=1, source_target_pairs={{0,1},{1,0},{2,3},{3,2},{4,5},{5,4},{6,7},{7,6},{8,9},{9,8},{10,11... | collective-permute-start | bytes 589832 | tf_op jit(solution)/shard_map/ppermute | solution.py:329
  17.0 9.9 %collective-permute-start.7 = (bf16[32,1024]{1,0:T(8,128)(2,1)S(1)}, bf16[32,1024]{1,0:T(8,128)(2,1)S(1)}, u32[]{:S(2)}, u32[]{:S(2)}) collective-permute-start(bf16[32,1024]{1,0:T(8,128)(2,1)S(1)} %pad_maximum_fusion.refs_0_), channel_id=1, source_target_pairs={{0,3},{1,2},{2,1},{3,0},{4,7},{5,6},{6,5},{7,4},{8,11},{9,10},{10,... | collective-permute-start | bytes 196616 | tf_op jit(solution)/shard_map/ppermute | solution.py:329
  19.4 9.0 %collective-permute-start.5 = (bf16[32,1024]{1,0:T(8,128)(2,1)S(1)}, bf16[32,1024]{1,0:T(8,128)(2,1)S(1)}, u32[]{:S(2)}, u32[]{:S(2)}) collective-permute-start(bf16[32,1024]{1,0:T(8,128)(2,1)S(1)} %pad_maximum_fusion.refs_0_), channel_id=1, source_target_pairs={{0,2},{1,3},{2,0},{3,1},{4,6},{5,7},{6,4},{7,5},{8,10},{9,11},{10,... | collective-permute-start | bytes 196616 | tf_op jit(solution)/shard_map/ppermute | solution.py:329
  26.9 4.3 %collective-permute-start.3 = (bf16[32,1024]{1,0:T(8,128)(2,1)S(1)}, bf16[32,1024]{1,0:T(8,128)(2,1)S(1)}, u32[]{:S(2)}, u32[]{:S(2)}) collective-permute-start(bf16[32,1024]{1,0:T(8,128)(2,1)S(1)} %pad_maximum_fusion.refs_0_), channel_id=1, source_target_pairs={{0,1},{1,0},{2,3},{3,2},{4,5},{5,4},{6,7},{7,6},{8,9},{9,8},{10,11... | collective-permute-start | bytes 196616 | tf_op jit(solution)/shard_map/ppermute | solution.py:329
  31.2 39.5 %copy-start = (bf16[1,2,16,5120]{3,2,1,0:T(8,128)(2,1)S(1)}, bf16[1,2,16,5120]{3,2,1,0:T(8,128)(2,1)}, u32[]{:S(2)}) copy-start(bf16[1,2,16,5120]{3,2,1,0:T(8,128)(2,1)} %param.12) | copy-start | bytes 983044
  31.2 45.9 %copy-start.1 = (s32[16]{0:T(128)S(1)}, s32[16]{0:T(128)}, u32[]{:S(2)}) copy-start(s32[16]{0:T(128)} %constant.11.clone) | copy-start | bytes 196
  53.4 8.7 %collective-permute-start.9 = (bf16[128,1024]{1,0:T(8,128)(2,1)S(1)}, bf16[128,1024]{1,0:T(8,128)(2,1)S(1)}, u32[]{:S(2)}, u32[]{:S(2)}) collective-permute-start(bf16[128,1024]{1,0:T(8,128)(2,1)S(1)} %get-tuple-element.15), channel_id=1, source_target_pairs={{0,1},{1,0},{2,3},{3,2},{4,5},{5,4},{6,7},{7,6},{8,9},{9,8},{10,11... | collective-permute-start | bytes 786440 | tf_op jit(solution)/shard_map/ppermute | solution.py:329
  54.9 11.1 %collective-permute-start.10 = (bf16[128,1024]{1,0:T(8,128)(2,1)S(1)}, bf16[128,1024]{1,0:T(8,128)(2,1)S(1)}, u32[]{:S(2)}, u32[]{:S(2)}) collective-permute-start(bf16[128,1024]{1,0:T(8,128)(2,1)S(1)} %get-tuple-element.16), channel_id=1, source_target_pairs={{0,2},{1,3},{2,0},{3,1},{4,6},{5,7},{6,4},{7,5},{8,10},{9,11},{10,... | collective-permute-start | bytes 786440 | tf_op jit(solution)/shard_map/ppermute | solution.py:329
  56.5 9.6 %collective-permute-start.11 = (bf16[128,1024]{1,0:T(8,128)(2,1)S(1)}, bf16[128,1024]{1,0:T(8,128)(2,1)S(1)}, u32[]{:S(2)}, u32[]{:S(2)}) collective-permute-start(bf16[128,1024]{1,0:T(8,128)(2,1)S(1)} %get-tuple-element.17), channel_id=1, source_target_pairs={{0,3},{1,2},{2,1},{3,0},{4,7},{5,6},{6,5},{7,4},{8,11},{9,10},{10,... | collective-permute-start | bytes 786440 | tf_op jit(solution)/shard_map/ppermute | solution.py:329
  66.2 8.9 %collective-permute-start.12 = (bf16[32,1024]{1,0:T(8,128)(2,1)S(1)}, bf16[32,1024]{1,0:T(8,128)(2,1)S(1)}, u32[]{:S(2)}, u32[]{:S(2)}) collective-permute-start(bf16[32,1024]{1,0:T(8,128)(2,1)S(1)} %get-tuple-element.19), channel_id=1, source_target_pairs={{0,4},{1,5},{2,6},{3,7},{4,0},{5,1},{6,2},{7,3},{8,12},{9,13},{10,... | collective-permute-start | bytes 196616 | tf_op jit(solution)/shard_map/ppermute | solution.py:329
  66.3 8.9 %collective-permute-start.13 = (bf16[32,1024]{1,0:T(8,128)(2,1)S(1)}, bf16[32,1024]{1,0:T(8,128)(2,1)S(1)}, u32[]{:S(2)}, u32[]{:S(2)}) collective-permute-start(bf16[32,1024]{1,0:T(8,128)(2,1)S(1)} %get-tuple-element.20), channel_id=1, source_target_pairs={{0,8},{1,9},{2,10},{3,11},{4,12},{5,13},{6,14},{7,15},{8,0},{9,1},... | collective-permute-start | bytes 196616 | tf_op jit(solution)/shard_map/ppermute | solution.py:329
  67.9 7.3 %collective-permute-start.14 = (bf16[32,1024]{1,0:T(8,128)(2,1)S(1)}, bf16[32,1024]{1,0:T(8,128)(2,1)S(1)}, u32[]{:S(2)}, u32[]{:S(2)}) collective-permute-start(bf16[32,1024]{1,0:T(8,128)(2,1)S(1)} %get-tuple-element.21), channel_id=1, source_target_pairs={{0,12},{1,13},{2,14},{3,15},{4,8},{5,9},{6,10},{7,11},{8,4},{9,5},... | collective-permute-start | bytes 196616 | tf_op jit(solution)/shard_map/ppermute | solution.py:329
  71.6 23.1 %all-to-all-start = ((bf16[16,32,320]{2,1,0:T(8,128)(2,1)}), bf16[16,32,320]{2,1,0:T(8,128)(2,1)S(1)}, u32[]{:S(2)}, u32[]{:S(2)}) async-start(bf16[16,32,320]{2,1,0:T(8,128)(2,1)} %by_target.1), calls=%async_computation | async-start | bytes 786432 | tf_op jit(solution)/shard_map/all_to_all | solution.py:351
  75.2 7.9 %collective-permute-start.15 = (bf16[32,1024]{1,0:T(8,128)(2,1)S(1)}, bf16[32,1024]{1,0:T(8,128)(2,1)S(1)}, u32[]{:S(2)}, u32[]{:S(2)}) collective-permute-start(bf16[32,1024]{1,0:T(8,128)(2,1)S(1)} %add_split.3.refs_0_), channel_id=1, source_target_pairs={{0,4},{1,5},{2,6},{3,7},{4,0},{5,1},{6,2},{7,3},{8,12},{9,13},{10,... | collective-permute-start | bytes 196616 | tf_op jit(solution)/shard_map/ppermute | solution.py:329
  77.1 16.0 %collective-permute-start.22 = (bf16[32,1024]{1,0:T(8,128)(2,1)S(1)}, bf16[32,1024]{1,0:T(8,128)(2,1)S(1)}, u32[]{:S(2)}, u32[]{:S(2)}) collective-permute-start(bf16[32,1024]{1,0:T(8,128)(2,1)S(1)} %add_split.3.refs_0_), channel_id=1, source_target_pairs={{0,3},{1,2},{2,1},{3,0},{4,7},{5,6},{6,5},{7,4},{8,11},{9,10},{10,... | collective-permute-start | bytes 196616 | tf_op jit(solution)/shard_map/ppermute | solution.py:329
  79.5 8.6 %collective-permute-start.17 = (bf16[32,1024]{1,0:T(8,128)(2,1)S(1)}, bf16[32,1024]{1,0:T(8,128)(2,1)S(1)}, u32[]{:S(2)}, u32[]{:S(2)}) collective-permute-start(bf16[32,1024]{1,0:T(8,128)(2,1)S(1)} %add_split.3.refs_0_), channel_id=1, source_target_pairs={{0,12},{1,13},{2,14},{3,15},{4,8},{5,9},{6,10},{7,11},{8,4},{9,5},... | collective-permute-start | bytes 196616 | tf_op jit(solution)/shard_map/ppermute | solution.py:329
  81.9 6.2 %collective-permute-start.16 = (bf16[32,1024]{1,0:T(8,128)(2,1)S(1)}, bf16[32,1024]{1,0:T(8,128)(2,1)S(1)}, u32[]{:S(2)}, u32[]{:S(2)}) collective-permute-start(bf16[32,1024]{1,0:T(8,128)(2,1)S(1)} %add_split.3.refs_0_), channel_id=1, source_target_pairs={{0,8},{1,9},{2,10},{3,11},{4,12},{5,13},{6,14},{7,15},{8,0},{9,1},... | collective-permute-start | bytes 196616 | tf_op jit(solution)/shard_map/ppermute | solution.py:329
  88.1 9.4 %collective-permute-start.23 = (bf16[96,1024]{1,0:T(8,128)(2,1)S(1)}, bf16[96,1024]{1,0:T(8,128)(2,1)S(1)}, u32[]{:S(2)}, u32[]{:S(2)}) collective-permute-start(bf16[96,1024]{1,0:T(8,128)(2,1)S(1)} %constant_dynamic-update-slice_fusion.3.refs_1_), channel_id=1, source_target_pairs={{0,3},{1,2},{2,1},{3,0},{4,7},{5,6},{6,5},{7,4},{8,11},{9,10},{10,... | collective-permute-start | bytes 589832 | tf_op jit(solution)/shard_map/ppermute | solution.py:329
  90.5 7.1 %collective-permute-start.21 = (bf16[96,1024]{1,0:T(8,128)(2,1)S(1)}, bf16[96,1024]{1,0:T(8,128)(2,1)S(1)}, u32[]{:S(2)}, u32[]{:S(2)}) collective-permute-start(bf16[96,1024]{1,0:T(8,128)(2,1)S(1)} %constant_dynamic-update-slice_fusion.3.refs_1_), channel_id=1, source_target_pairs={{0,2},{1,3},{2,0},{3,1},{4,6},{5,7},{6,4},{7,5},{8,10},{9,11},{10,... | collective-permute-start | bytes 589832 | tf_op jit(solution)/shard_map/ppermute | solution.py:329
  91.0 6.5 %collective-permute-start.19 = (bf16[96,1024]{1,0:T(8,128)(2,1)S(1)}, bf16[96,1024]{1,0:T(8,128)(2,1)S(1)}, u32[]{:S(2)}, u32[]{:S(2)}) collective-permute-start(bf16[96,1024]{1,0:T(8,128)(2,1)S(1)} %constant_dynamic-update-slice_fusion.3.refs_1_), channel_id=1, source_target_pairs={{0,1},{1,0},{2,3},{3,2},{4,5},{5,4},{6,7},{7,6},{8,9},{9,8},{10,11... | collective-permute-start | bytes 589832 | tf_op jit(solution)/shard_map/ppermute | solution.py:329
  91.7 5.9 %collective-permute-start.20 = (bf16[32,1024]{1,0:T(8,128)(2,1)S(1)}, bf16[32,1024]{1,0:T(8,128)(2,1)S(1)}, u32[]{:S(2)}, u32[]{:S(2)}) collective-permute-start(bf16[32,1024]{1,0:T(8,128)(2,1)S(1)} %add_split.3.refs_0_), channel_id=1, source_target_pairs={{0,2},{1,3},{2,0},{3,1},{4,6},{5,7},{6,4},{7,5},{8,10},{9,11},{10,... | collective-permute-start | bytes 196616 | tf_op jit(solution)/shard_map/ppermute | solution.py:329
  93.1 4.5 %collective-permute-start.18 = (bf16[32,1024]{1,0:T(8,128)(2,1)S(1)}, bf16[32,1024]{1,0:T(8,128)(2,1)S(1)}, u32[]{:S(2)}, u32[]{:S(2)}) collective-permute-start(bf16[32,1024]{1,0:T(8,128)(2,1)S(1)} %add_split.3.refs_0_), channel_id=1, source_target_pairs={{0,1},{1,0},{2,3},{3,2},{4,5},{5,4},{6,7},{7,6},{8,9},{9,8},{10,11... | collective-permute-start | bytes 196616 | tf_op jit(solution)/shard_map/ppermute | solution.py:329
  98.8 2.2 %collective-permute-start.24 = (f32[160,1024]{1,0:T(8,128)S(1)}, f32[160,1024]{1,0:T(8,128)S(1)}, u32[]{:S(2)}, u32[]{:S(2)}) collective-permute-start(f32[160,1024]{1,0:T(8,128)S(1)} %get-tuple-element.23), channel_id=1, source_target_pairs={{0,16},{16,0},{1,17},{17,1},{2,18},{18,2},{3,19},{19,3},{4,20},{20... | collective-permute-start | bytes 1966088 | tf_op jit(solution)/shard_map/ppermute | solution.py:329

commit v5 on v4

--- a/solution.py
+++ b/solution.py
@@ -276,27 +276,23 @@
 
 
 def weight_parts(place, columns, grads, heads_of, kv_heads, dps):
-    devices, rows, wide = columns.shape
+    devices, _, wide = columns.shape
     width = wide // dps
     chunks = len(grads)
     parts_of = len(grads[0])
-    sizes = [part.shape[0] for part in grads[0]]
-    starts = [sum(sizes[:i]) for i in range(parts_of)]
     kvw2 = 2 * kv_heads * HEAD
 
     def kern(place_ref, c_ref, *refs):
         g_in = [refs[i * parts_of : (i + 1) * parts_of] for i in range(chunks)]
         outs = refs[chunks * parts_of : chunks * parts_of + dps]
-        g_s, c_s, w_s = refs[chunks * parts_of + dps :]
+        w_s = refs[chunks * parts_of + dps]
+        cols = jnp.concatenate([c_ref[place_ref[dps + n]] for n in range(devices)], axis=0)
         col = 0
         for n in range(chunks):
             span = 2 * heads_of[n] * HEAD
-            for i in range(parts_of):
-                g_s[starts[i] : starts[i] + sizes[i], col : col + span] = g_in[n][i][...]
+            terms = jnp.concatenate([g_in[n][i][...] for i in range(parts_of)], axis=0)
+            w_s[:, col : col + span] = dg(cols, terms, 0, 0)
             col += span
-        for n in range(devices):
-            c_s[n * rows : (n + 1) * rows, :] = c_ref[place_ref[dps + n]]
-        w_s[...] = dg(c_s[...], g_s[...], 0, 0)
         for k in range(dps):
             at = pl.ds(pl.multiple_of(place_ref[k] * width, 8), width)
             for h in range(kv_heads):
@@ -313,8 +309,6 @@
         out_specs=[vmem] * dps,
         out_shape=[jax.ShapeDtypeStruct((width, kvw2), F32)] * dps,
         scratch_shapes=[
-            pltpu.VMEM((devices * rows, kvw2), BF16),
-            pltpu.VMEM((devices * rows, wide), BF16),
             pltpu.VMEM((wide, kvw2), F32),
         ],
         compiler_params=pltpu.CompilerParams(vmem_limit_bytes=32 << 20),

time: 102 us -> 102 us (level)
  no operation moved by 1% of the time
where the time goes in v5:
time: 102 us
  starting transfers between devices  38.4 us (38%)
  waiting for transfers between devices  36.4 us (36%)
  Pallas kernels  24.5 us (24%)
  other arithmetic  1.8 us (2%)
    ppermute x25, waiting for transfers between devices, swap(): return lax.ppermute(x, axis, [(i, i ^ by) for i in range(count)])  36.4 us
    ppermute x25, starting transfers between devices, swap(): return lax.ppermute(x, axis, [(i, i ^ by) for i in range(count)])  34.9 us
    pallas_call x1, Pallas kernels, attention(): pl.pallas_call(kern, in_specs=[hbm, smem, hbm, hbm] + [vmem] * len(sizes)...  22.2 us
    all_to_all x1, starting transfers between devices, per_device(): lax.all_to_all(hidden, 'seq', split_axis=0, concat_axis=0, tiled=True)  3.55 us
  transfers between devices with their start and end apart: 26, of which 9 were waited for; matrix products, arithmetic and copies ran while one was open for 0% of the time, Pallas kernels for 1%

profile of v5, /device:TPU:0, one launch (start us, length us, event | category | flops | bytes accessed | tf_op | source)
XLA Modules:
  0.0 101.9 jit_solution(14423006504645294851)
XLA Ops:
  0.6 0.8 pad_maximum_fusion.refs_0_
  1.4 3.1 %collective-permute-start = (bf16[32,1024]{1,0:T(8,128)(2,1)S(1)}, bf16[32,1024]{1,0:T(8,128)(2,1)S(1)}, u32[]{:S(2)}, u32[]{:S(2)}) collective-permute-start(bf16[32,1024]{1,0:T(8,128)(2,1)S(1)} %pad_maximum_fusion.refs_0_), channel_id=1, source_target_pairs={{0,4},{1,5},{2,6},{3,7},{4,0},{5,1},{6,2},{7,3},{8,12},{9,13},{10,... | collective-permute-start | bytes 196616 | tf_op jit(solution)/shard_map/ppermute | solution.py:323
  4.5 2.5 %collective-permute-start.2 = (bf16[32,1024]{1,0:T(8,128)(2,1)S(1)}, bf16[32,1024]{1,0:T(8,128)(2,1)S(1)}, u32[]{:S(2)}, u32[]{:S(2)}) collective-permute-start(bf16[32,1024]{1,0:T(8,128)(2,1)S(1)} %pad_maximum_fusion.refs_0_), channel_id=1, source_target_pairs={{0,12},{1,13},{2,14},{3,15},{4,8},{5,9},{6,10},{7,11},{8,4},{9,5},... | collective-permute-start | bytes 196616 | tf_op jit(solution)/shard_map/ppermute | solution.py:323
  6.9 0.1 collective-permute-start.1
  7.1 0.0 collective-permute-done
  7.1 6.3 %collective-permute-done.1 = bf16[32,1024]{1,0:T(8,128)(2,1)S(1)} collective-permute-done((bf16[32,1024]{1,0:T(8,128)(2,1)S(1)}, bf16[32,1024]{1,0:T(8,128)(2,1)S(1)}, u32[]{:S(2)}, u32[]{:S(2)}) %collective-permute-start.1) | collective-permute-done | bytes 65568 | tf_op jit(solution)/shard_map/ppermute | solution.py:323
  13.4 0.0 collective-permute-done.2
  13.4 2.5 %collective-permute-start.8 = (bf16[96,1024]{1,0:T(8,128)(2,1)S(1)}, bf16[96,1024]{1,0:T(8,128)(2,1)S(1)}, u32[]{:S(2)}, u32[]{:S(2)}) collective-permute-start(bf16[96,1024]{1,0:T(8,128)(2,1)S(1)} %constant_dynamic-update-slice_fusion.refs_1_), channel_id=1, source_target_pairs={{0,3},{1,2},{2,1},{3,0},{4,7},{5,6},{6,5},{7,4},{8,11},{9,10},{10,... | collective-permute-start | bytes 589832 | tf_op jit(solution)/shard_map/ppermute | solution.py:323
  15.9 0.5 collective-permute-start.6
  16.4 0.5 collective-permute-start.4
  17.0 2.4 %collective-permute-start.7 = (bf16[32,1024]{1,0:T(8,128)(2,1)S(1)}, bf16[32,1024]{1,0:T(8,128)(2,1)S(1)}, u32[]{:S(2)}, u32[]{:S(2)}) collective-permute-start(bf16[32,1024]{1,0:T(8,128)(2,1)S(1)} %pad_maximum_fusion.refs_0_), channel_id=1, source_target_pairs={{0,3},{1,2},{2,1},{3,0},{4,7},{5,6},{6,5},{7,4},{8,11},{9,10},{10,... | collective-permute-start | bytes 196616 | tf_op jit(solution)/shard_map/ppermute | solution.py:323
  19.4 0.5 collective-permute-start.5
  19.9 7.0 %collective-permute-done.7.refs_6_ = bf16[32,1024]{1,0:T(8,128)(2,1)S(1)} collective-permute-done((bf16[32,1024]{1,0:T(8,128)(2,1)S(1)}, bf16[32,1024]{1,0:T(8,128)(2,1)S(1)}, u32[]{:S(2)}, u32[]{:S(2)}) %collective-permute-start.7) | collective-permute-done | bytes 65568 | tf_op jit(solution)/shard_map/ppermute | solution.py:323
  26.9 1.5 %collective-permute-start.3 = (bf16[32,1024]{1,0:T(8,128)(2,1)S(1)}, bf16[32,1024]{1,0:T(8,128)(2,1)S(1)}, u32[]{:S(2)}, u32[]{:S(2)}) collective-permute-start(bf16[32,1024]{1,0:T(8,128)(2,1)S(1)} %pad_maximum_fusion.refs_0_), channel_id=1, source_target_pairs={{0,1},{1,0},{2,3},{3,2},{4,5},{5,4},{6,7},{7,6},{8,9},{9,8},{10,11... | collective-permute-start | bytes 196616 | tf_op jit(solution)/shard_map/ppermute | solution.py:323
  28.4 0.0 collective-permute-done.5.refs_4_
  28.4 2.8 %collective-permute-done.3.refs_2_ = bf16[32,1024]{1,0:T(8,128)(2,1)S(1)} collective-permute-done((bf16[32,1024]{1,0:T(8,128)(2,1)S(1)}, bf16[32,1024]{1,0:T(8,128)(2,1)S(1)}, u32[]{:S(2)}, u32[]{:S(2)}) %collective-permute-start.3) | collective-permute-done | bytes 65568 | tf_op jit(solution)/shard_map/ppermute | solution.py:323
  31.2 0.0 collective-permute-done.8.refs_7_
  31.2 0.0 collective-permute-done.6.refs_5_
  31.2 0.0 collective-permute-done.4.refs_3_
  31.2 0.0 copy-start
  31.2 0.0 copy-start.1
  31.2 22.2 %attention.1 = (bf16[2,512,2560]{2,1,0:T(8,128)(2,1)}, bf16[128,1024]{1,0:T(8,128)(2,1)S(1)}, bf16[128,1024]{1,0:T(8,128)(2,1)S(1)}, bf16[128,1024]{1,0:T(8,128)(2,1)S(1)}, bf16[128,1024]{1,0:T(8,128)(2,1)S(1)}) custom-call(s32[2,16]{1,0:T(2,128)} %bitcast.13, s32[1]{0:T(128)} %bitcast.1.me_ref, bf16[2,512,2560]{2,1,0:T(8,128)(2,1)} %bitcast.11, ...), custom_call_target="tpu_custom_call" | custom-call | flops 13421772800 | bytes 15728640 | tf_op jit(solution)/shard_map/attention/pallas_call | solution.py:198
  53.4 1.6 %collective-permute-start.9 = (bf16[128,1024]{1,0:T(8,128)(2,1)S(1)}, bf16[128,1024]{1,0:T(8,128)(2,1)S(1)}, u32[]{:S(2)}, u32[]{:S(2)}) collective-permute-start(bf16[128,1024]{1,0:T(8,128)(2,1)S(1)} %get-tuple-element.15), channel_id=1, source_target_pairs={{0,1},{1,0},{2,3},{3,2},{4,5},{5,4},{6,7},{7,6},{8,9},{9,8},{10,11... | collective-permute-start | bytes 786440 | tf_op jit(solution)/shard_map/ppermute | solution.py:323
  54.9 1.5 %collective-permute-start.10 = (bf16[128,1024]{1,0:T(8,128)(2,1)S(1)}, bf16[128,1024]{1,0:T(8,128)(2,1)S(1)}, u32[]{:S(2)}, u32[]{:S(2)}) collective-permute-start(bf16[128,1024]{1,0:T(8,128)(2,1)S(1)} %get-tuple-element.16), channel_id=1, source_target_pairs={{0,2},{1,3},{2,0},{3,1},{4,6},{5,7},{6,4},{7,5},{8,10},{9,11},{10,... | collective-permute-start | bytes 786440 | tf_op jit(solution)/shard_map/ppermute | solution.py:323
  56.5 0.5 collective-permute-start.11
  56.9 5.1 %collective-permute-done.9.refs_1_ = bf16[128,1024]{1,0:T(8,128)(2,1)S(1)} collective-permute-done((bf16[128,1024]{1,0:T(8,128)(2,1)S(1)}, bf16[128,1024]{1,0:T(8,128)(2,1)S(1)}, u32[]{:S(2)}, u32[]{:S(2)}) %collective-permute-start.9) | collective-permute-done | bytes 262176 | tf_op jit(solution)/shard_map/ppermute | solution.py:323
  62.0 4.0 %collective-permute-done.10.refs_2_ = bf16[128,1024]{1,0:T(8,128)(2,1)S(1)} collective-permute-done((bf16[128,1024]{1,0:T(8,128)(2,1)S(1)}, bf16[128,1024]{1,0:T(8,128)(2,1)S(1)}, u32[]{:S(2)}, u32[]{:S(2)}) %collective-permute-start.10) | collective-permute-done | bytes 262176 | tf_op jit(solution)/shard_map/ppermute | solution.py:323
  66.1 0.0 collective-permute-done.11.refs_3_
  66.1 0.1 add_split.2
  66.2 0.1 collective-permute-start.12
  66.3 1.6 %collective-permute-start.13 = (bf16[32,1024]{1,0:T(8,128)(2,1)S(1)}, bf16[32,1024]{1,0:T(8,128)(2,1)S(1)}, u32[]{:S(2)}, u32[]{:S(2)}) collective-permute-start(bf16[32,1024]{1,0:T(8,128)(2,1)S(1)} %get-tuple-element.20), channel_id=1, source_target_pairs={{0,8},{1,9},{2,10},{3,11},{4,12},{5,13},{6,14},{7,15},{8,0},{9,1},... | collective-permute-start | bytes 196616 | tf_op jit(solution)/shard_map/ppermute | solution.py:323
  67.9 2.8 %collective-permute-start.14 = (bf16[32,1024]{1,0:T(8,128)(2,1)S(1)}, bf16[32,1024]{1,0:T(8,128)(2,1)S(1)}, u32[]{:S(2)}, u32[]{:S(2)}) collective-permute-start(bf16[32,1024]{1,0:T(8,128)(2,1)S(1)} %get-tuple-element.21), channel_id=1, source_target_pairs={{0,12},{1,13},{2,14},{3,15},{4,8},{5,9},{6,10},{7,11},{8,4},{9,5},... | collective-permute-start | bytes 196616 | tf_op jit(solution)/shard_map/ppermute | solution.py:323
  70.7 0.0 copy-done
  70.7 0.9 by_target.1
  71.6 3.6 %all-to-all-start = ((bf16[16,32,320]{2,1,0:T(8,128)(2,1)}), bf16[16,32,320]{2,1,0:T(8,128)(2,1)S(1)}, u32[]{:S(2)}, u32[]{:S(2)}) async-start(bf16[16,32,320]{2,1,0:T(8,128)(2,1)} %by_target.1), calls=%async_computation | async-start | bytes 786432 | tf_op jit(solution)/shard_map/all_to_all | solution.py:345
  75.1 0.0 collective-permute-done.12.refs_1_
  75.1 0.0 collective-permute-done.13.refs_2_
  75.2 0.0 collective-permute-done.14.refs_3_
  75.2 1.9 %collective-permute-start.15 = (bf16[32,1024]{1,0:T(8,128)(2,1)S(1)}, bf16[32,1024]{1,0:T(8,128)(2,1)S(1)}, u32[]{:S(2)}, u32[]{:S(2)}) collective-permute-start(bf16[32,1024]{1,0:T(8,128)(2,1)S(1)} %add_split.3.refs_0_), channel_id=1, source_target_pairs={{0,4},{1,5},{2,6},{3,7},{4,0},{5,1},{6,2},{7,3},{8,12},{9,13},{10,... | collective-permute-start | bytes 196616 | tf_op jit(solution)/shard_map/ppermute | solution.py:323
  77.1 0.0 copy-done.1
  77.1 2.4 %collective-permute-start.22 = (bf16[32,1024]{1,0:T(8,128)(2,1)S(1)}, bf16[32,1024]{1,0:T(8,128)(2,1)S(1)}, u32[]{:S(2)}, u32[]{:S(2)}) collective-permute-start(bf16[32,1024]{1,0:T(8,128)(2,1)S(1)} %add_split.3.refs_0_), channel_id=1, source_target_pairs={{0,3},{1,2},{2,1},{3,0},{4,7},{5,6},{6,5},{7,4},{8,11},{9,10},{10,... | collective-permute-start | bytes 196616 | tf_op jit(solution)/shard_map/ppermute | solution.py:323
  79.5 2.4 %collective-permute-start.17 = (bf16[32,1024]{1,0:T(8,128)(2,1)S(1)}, bf16[32,1024]{1,0:T(8,128)(2,1)S(1)}, u32[]{:S(2)}, u32[]{:S(2)}) collective-permute-start(bf16[32,1024]{1,0:T(8,128)(2,1)S(1)} %add_split.3.refs_0_), channel_id=1, source_target_pairs={{0,12},{1,13},{2,14},{3,15},{4,8},{5,9},{6,10},{7,11},{8,4},{9,5},... | collective-permute-start | bytes 196616 | tf_op jit(solution)/shard_map/ppermute | solution.py:323
  81.9 0.0 collective-permute-start.16
  81.9 1.2 %collective-permute-done.15 = bf16[32,1024]{1,0:T(8,128)(2,1)S(1)} collective-permute-done((bf16[32,1024]{1,0:T(8,128)(2,1)S(1)}, bf16[32,1024]{1,0:T(8,128)(2,1)S(1)}, u32[]{:S(2)}, u32[]{:S(2)}) %collective-permute-start.15) | collective-permute-done | bytes 65568 | tf_op jit(solution)/shard_map/ppermute | solution.py:323
  83.1 4.9 %collective-permute-done.16 = bf16[32,1024]{1,0:T(8,128)(2,1)S(1)} collective-permute-done((bf16[32,1024]{1,0:T(8,128)(2,1)S(1)}, bf16[32,1024]{1,0:T(8,128)(2,1)S(1)}, u32[]{:S(2)}, u32[]{:S(2)}) %collective-permute-start.16) | collective-permute-done | bytes 65568 | tf_op jit(solution)/shard_map/ppermute | solution.py:323
  88.1 0.0 collective-permute-done.17
  88.1 2.4 %collective-permute-start.23 = (bf16[96,1024]{1,0:T(8,128)(2,1)S(1)}, bf16[96,1024]{1,0:T(8,128)(2,1)S(1)}, u32[]{:S(2)}, u32[]{:S(2)}) collective-permute-start(bf16[96,1024]{1,0:T(8,128)(2,1)S(1)} %constant_dynamic-update-slice_fusion.3.refs_1_), channel_id=1, source_target_pairs={{0,3},{1,2},{2,1},{3,0},{4,7},{5,6},{6,5},{7,4},{8,11},{9,10},{10,... | collective-permute-start | bytes 589832 | tf_op jit(solution)/shard_map/ppermute | solution.py:323
  90.5 0.6 collective-permute-start.21
  91.0 0.6 collective-permute-start.19
  91.7 1.4 %collective-permute-start.20 = (bf16[32,1024]{1,0:T(8,128)(2,1)S(1)}, bf16[32,1024]{1,0:T(8,128)(2,1)S(1)}, u32[]{:S(2)}, u32[]{:S(2)}) collective-permute-start(bf16[32,1024]{1,0:T(8,128)(2,1)S(1)} %add_split.3.refs_0_), channel_id=1, source_target_pairs={{0,2},{1,3},{2,0},{3,1},{4,6},{5,7},{6,4},{7,5},{8,10},{9,11},{10,... | collective-permute-start | bytes 196616 | tf_op jit(solution)/shard_map/ppermute | solution.py:323
  93.1 0.0 collective-permute-done.22.refs_6_
  93.1 1.5 %collective-permute-start.18 = (bf16[32,1024]{1,0:T(8,128)(2,1)S(1)}, bf16[32,1024]{1,0:T(8,128)(2,1)S(1)}, u32[]{:S(2)}, u32[]{:S(2)}) collective-permute-start(bf16[32,1024]{1,0:T(8,128)(2,1)S(1)} %add_split.3.refs_0_), channel_id=1, source_target_pairs={{0,1},{1,0},{2,3},{3,2},{4,5},{5,4},{6,7},{7,6},{8,9},{9,8},{10,11... | collective-permute-start | bytes 196616 | tf_op jit(solution)/shard_map/ppermute | solution.py:323
  94.6 0.1 pad_add_fusion.place_ref
  94.6 0.0 all-to-all-done.c_ref
  94.6 2.9 %collective-permute-done.20.refs_4_ = bf16[32,1024]{1,0:T(8,128)(2,1)S(1)} collective-permute-done((bf16[32,1024]{1,0:T(8,128)(2,1)S(1)}, bf16[32,1024]{1,0:T(8,128)(2,1)S(1)}, u32[]{:S(2)}, u32[]{:S(2)}) %collective-permute-start.20) | collective-permute-done | bytes 65568 | tf_op jit(solution)/shard_map/ppermute | solution.py:323
  97.5 0.0 collective-permute-done.18.refs_2_
  97.5 0.0 collective-permute-done.23.refs_7_
  97.5 0.0 collective-permute-done.21.refs_5_
  97.5 0.0 collective-permute-done.19.refs_3_
  97.6 1.2 %weight_parts.1 = (f32[160,1024]{1,0:T(8,128)S(1)}, f32[160,1024]{1,0:T(8,128)S(1)}) custom-call(s32[18]{0:T(128)S(1)} %pad_add_fusion.place_ref, bf16[16,32,320]{2,1,0:T(8,128)(2,1)S(1)} %all-to-all-done.c_ref, bf16[32,1024]{1,0:T(8,128)(2,1)S(1)} %add_split.3.refs_0_, bf16[96,1024]{1,0:T(8,128)(2,1)S(1)} %constant_dynamic-update-slice_fusion.3.refs_1_, ...), custom_call_target="tpu_custom_call" | custom-call | tf_op jit(solution)/shard_map/weight_parts/pallas_call | solution.py:306
  98.8 0.1 collective-permute-start.24
  98.9 2.1 %collective-permute-done.24 = f32[160,1024]{1,0:T(8,128)S(1)} collective-permute-done((f32[160,1024]{1,0:T(8,128)S(1)}, f32[160,1024]{1,0:T(8,128)S(1)}, u32[]{:S(2)}, u32[]{:S(2)}) %collective-permute-start.24) | collective-permute-done | bytes 655392 | tf_op jit(solution)/shard_map/ppermute | solution.py:323
  101.0 0.9 add.3
  (9 shorter events, 0.1 us)
Async XLA Ops:
  1.4 5.6 %collective-permute-start = (bf16[32,1024]{1,0:T(8,128)(2,1)S(1)}, bf16[32,1024]{1,0:T(8,128)(2,1)S(1)}, u32[]{:S(2)}, u32[]{:S(2)}) collective-permute-start(bf16[32,1024]{1,0:T(8,128)(2,1)S(1)} %pad_maximum_fusion.refs_0_), channel_id=1, source_target_pairs={{0,4},{1,5},{2,6},{3,7},{4,0},{5,1},{6,2},{7,3},{8,12},{9,13},{10,... | collective-permute-start | bytes 196616 | tf_op jit(solution)/shard_map/ppermute | solution.py:323
  4.5 8.9 %collective-permute-start.2 = (bf16[32,1024]{1,0:T(8,128)(2,1)S(1)}, bf16[32,1024]{1,0:T(8,128)(2,1)S(1)}, u32[]{:S(2)}, u32[]{:S(2)}) collective-permute-start(bf16[32,1024]{1,0:T(8,128)(2,1)S(1)} %pad_maximum_fusion.refs_0_), channel_id=1, source_target_pairs={{0,12},{1,13},{2,14},{3,15},{4,8},{5,9},{6,10},{7,11},{8,4},{9,5},... | collective-permute-start | bytes 196616 | tf_op jit(solution)/shard_map/ppermute | solution.py:323
  6.9 6.4 %collective-permute-start.1 = (bf16[32,1024]{1,0:T(8,128)(2,1)S(1)}, bf16[32,1024]{1,0:T(8,128)(2,1)S(1)}, u32[]{:S(2)}, u32[]{:S(2)}) collective-permute-start(bf16[32,1024]{1,0:T(8,128)(2,1)S(1)} %pad_maximum_fusion.refs_0_), channel_id=1, source_target_pairs={{0,8},{1,9},{2,10},{3,11},{4,12},{5,13},{6,14},{7,15},{8,0},{9,1},... | collective-permute-start | bytes 196616 | tf_op jit(solution)/shard_map/ppermute | solution.py:323
  13.4 17.8 %collective-permute-start.8 = (bf16[96,1024]{1,0:T(8,128)(2,1)S(1)}, bf16[96,1024]{1,0:T(8,128)(2,1)S(1)}, u32[]{:S(2)}, u32[]{:S(2)}) collective-permute-start(bf16[96,1024]{1,0:T(8,128)(2,1)S(1)} %constant_dynamic-update-slice_fusion.refs_1_), channel_id=1, source_target_pairs={{0,3},{1,2},{2,1},{3,0},{4,7},{5,6},{6,5},{7,4},{8,11},{9,10},{10,... | collective-permute-start | bytes 589832 | tf_op jit(solution)/shard_map/ppermute | solution.py:323
  15.9 15.3 %collective-permute-start.6 = (bf16[96,1024]{1,0:T(8,128)(2,1)S(1)}, bf16[96,1024]{1,0:T(8,128)(2,1)S(1)}, u32[]{:S(2)}, u32[]{:S(2)}) collective-permute-start(bf16[96,1024]{1,0:T(8,128)(2,1)S(1)} %constant_dynamic-update-slice_fusion.refs_1_), channel_id=1, source_target_pairs={{0,2},{1,3},{2,0},{3,1},{4,6},{5,7},{6,4},{7,5},{8,10},{9,11},{10,... | collective-permute-start | bytes 589832 | tf_op jit(solution)/shard_map/ppermute | solution.py:323
  16.4 14.8 %collective-permute-start.4 = (bf16[96,1024]{1,0:T(8,128)(2,1)S(1)}, bf16[96,1024]{1,0:T(8,128)(2,1)S(1)}, u32[]{:S(2)}, u32[]{:S(2)}) collective-permute-start(bf16[96,1024]{1,0:T(8,128)(2,1)S(1)} %constant_dynamic-update-slice_fusion.refs_1_), channel_id=1, source_target_pairs={{0,1},{1,0},{2,3},{3,2},{4,5},{5,4},{6,7},{7,6},{8,9},{9,8},{10,11... | collective-permute-start | bytes 589832 | tf_op jit(solution)/shard_map/ppermute | solution.py:323
  17.0 9.9 %collective-permute-start.7 = (bf16[32,1024]{1,0:T(8,128)(2,1)S(1)}, bf16[32,1024]{1,0:T(8,128)(2,1)S(1)}, u32[]{:S(2)}, u32[]{:S(2)}) collective-permute-start(bf16[32,1024]{1,0:T(8,128)(2,1)S(1)} %pad_maximum_fusion.refs_0_), channel_id=1, source_target_pairs={{0,3},{1,2},{2,1},{3,0},{4,7},{5,6},{6,5},{7,4},{8,11},{9,10},{10,... | collective-permute-start | bytes 196616 | tf_op jit(solution)/shard_map/ppermute | solution.py:323
  19.4 9.0 %collective-permute-start.5 = (bf16[32,1024]{1,0:T(8,128)(2,1)S(1)}, bf16[32,1024]{1,0:T(8,128)(2,1)S(1)}, u32[]{:S(2)}, u32[]{:S(2)}) collective-permute-start(bf16[32,1024]{1,0:T(8,128)(2,1)S(1)} %pad_maximum_fusion.refs_0_), channel_id=1, source_target_pairs={{0,2},{1,3},{2,0},{3,1},{4,6},{5,7},{6,4},{7,5},{8,10},{9,11},{10,... | collective-permute-start | bytes 196616 | tf_op jit(solution)/shard_map/ppermute | solution.py:323
  26.9 4.3 %collective-permute-start.3 = (bf16[32,1024]{1,0:T(8,128)(2,1)S(1)}, bf16[32,1024]{1,0:T(8,128)(2,1)S(1)}, u32[]{:S(2)}, u32[]{:S(2)}) collective-permute-start(bf16[32,1024]{1,0:T(8,128)(2,1)S(1)} %pad_maximum_fusion.refs_0_), channel_id=1, source_target_pairs={{0,1},{1,0},{2,3},{3,2},{4,5},{5,4},{6,7},{7,6},{8,9},{9,8},{10,11... | collective-permute-start | bytes 196616 | tf_op jit(solution)/shard_map/ppermute | solution.py:323
  31.2 39.5 %copy-start = (bf16[1,2,16,5120]{3,2,1,0:T(8,128)(2,1)S(1)}, bf16[1,2,16,5120]{3,2,1,0:T(8,128)(2,1)}, u32[]{:S(2)}) copy-start(bf16[1,2,16,5120]{3,2,1,0:T(8,128)(2,1)} %param.12) | copy-start | bytes 983044
  31.2 45.9 %copy-start.1 = (s32[16]{0:T(128)S(1)}, s32[16]{0:T(128)}, u32[]{:S(2)}) copy-start(s32[16]{0:T(128)} %constant.11.clone) | copy-start | bytes 196
  53.4 8.7 %collective-permute-start.9 = (bf16[128,1024]{1,0:T(8,128)(2,1)S(1)}, bf16[128,1024]{1,0:T(8,128)(2,1)S(1)}, u32[]{:S(2)}, u32[]{:S(2)}) collective-permute-start(bf16[128,1024]{1,0:T(8,128)(2,1)S(1)} %get-tuple-element.15), channel_id=1, source_target_pairs={{0,1},{1,0},{2,3},{3,2},{4,5},{5,4},{6,7},{7,6},{8,9},{9,8},{10,11... | collective-permute-start | bytes 786440 | tf_op jit(solution)/shard_map/ppermute | solution.py:323
  54.9 11.1 %collective-permute-start.10 = (bf16[128,1024]{1,0:T(8,128)(2,1)S(1)}, bf16[128,1024]{1,0:T(8,128)(2,1)S(1)}, u32[]{:S(2)}, u32[]{:S(2)}) collective-permute-start(bf16[128,1024]{1,0:T(8,128)(2,1)S(1)} %get-tuple-element.16), channel_id=1, source_target_pairs={{0,2},{1,3},{2,0},{3,1},{4,6},{5,7},{6,4},{7,5},{8,10},{9,11},{10,... | collective-permute-start | bytes 786440 | tf_op jit(solution)/shard_map/ppermute | solution.py:323
  56.5 9.6 %collective-permute-start.11 = (bf16[128,1024]{1,0:T(8,128)(2,1)S(1)}, bf16[128,1024]{1,0:T(8,128)(2,1)S(1)}, u32[]{:S(2)}, u32[]{:S(2)}) collective-permute-start(bf16[128,1024]{1,0:T(8,128)(2,1)S(1)} %get-tuple-element.17), channel_id=1, source_target_pairs={{0,3},{1,2},{2,1},{3,0},{4,7},{5,6},{6,5},{7,4},{8,11},{9,10},{10,... | collective-permute-start | bytes 786440 | tf_op jit(solution)/shard_map/ppermute | solution.py:323
  66.2 8.9 %collective-permute-start.12 = (bf16[32,1024]{1,0:T(8,128)(2,1)S(1)}, bf16[32,1024]{1,0:T(8,128)(2,1)S(1)}, u32[]{:S(2)}, u32[]{:S(2)}) collective-permute-start(bf16[32,1024]{1,0:T(8,128)(2,1)S(1)} %get-tuple-element.19), channel_id=1, source_target_pairs={{0,4},{1,5},{2,6},{3,7},{4,0},{5,1},{6,2},{7,3},{8,12},{9,13},{10,... | collective-permute-start | bytes 196616 | tf_op jit(solution)/shard_map/ppermute | solution.py:323
  66.3 8.9 %collective-permute-start.13 = (bf16[32,1024]{1,0:T(8,128)(2,1)S(1)}, bf16[32,1024]{1,0:T(8,128)(2,1)S(1)}, u32[]{:S(2)}, u32[]{:S(2)}) collective-permute-start(bf16[32,1024]{1,0:T(8,128)(2,1)S(1)} %get-tuple-element.20), channel_id=1, source_target_pairs={{0,8},{1,9},{2,10},{3,11},{4,12},{5,13},{6,14},{7,15},{8,0},{9,1},... | collective-permute-start | bytes 196616 | tf_op jit(solution)/shard_map/ppermute | solution.py:323
  67.9 7.3 %collective-permute-start.14 = (bf16[32,1024]{1,0:T(8,128)(2,1)S(1)}, bf16[32,1024]{1,0:T(8,128)(2,1)S(1)}, u32[]{:S(2)}, u32[]{:S(2)}) collective-permute-start(bf16[32,1024]{1,0:T(8,128)(2,1)S(1)} %get-tuple-element.21), channel_id=1, source_target_pairs={{0,12},{1,13},{2,14},{3,15},{4,8},{5,9},{6,10},{7,11},{8,4},{9,5},... | collective-permute-start | bytes 196616 | tf_op jit(solution)/shard_map/ppermute | solution.py:323
  71.6 23.1 %all-to-all-start = ((bf16[16,32,320]{2,1,0:T(8,128)(2,1)}), bf16[16,32,320]{2,1,0:T(8,128)(2,1)S(1)}, u32[]{:S(2)}, u32[]{:S(2)}) async-start(bf16[16,32,320]{2,1,0:T(8,128)(2,1)} %by_target.1), calls=%async_computation | async-start | bytes 786432 | tf_op jit(solution)/shard_map/all_to_all | solution.py:345
  75.2 7.9 %collective-permute-start.15 = (bf16[32,1024]{1,0:T(8,128)(2,1)S(1)}, bf16[32,1024]{1,0:T(8,128)(2,1)S(1)}, u32[]{:S(2)}, u32[]{:S(2)}) collective-permute-start(bf16[32,1024]{1,0:T(8,128)(2,1)S(1)} %add_split.3.refs_0_), channel_id=1, source_target_pairs={{0,4},{1,5},{2,6},{3,7},{4,0},{5,1},{6,2},{7,3},{8,12},{9,13},{10,... | collective-permute-start | bytes 196616 | tf_op jit(solution)/shard_map/ppermute | solution.py:323
  77.1 16.0 %collective-permute-start.22 = (bf16[32,1024]{1,0:T(8,128)(2,1)S(1)}, bf16[32,1024]{1,0:T(8,128)(2,1)S(1)}, u32[]{:S(2)}, u32[]{:S(2)}) collective-permute-start(bf16[32,1024]{1,0:T(8,128)(2,1)S(1)} %add_split.3.refs_0_), channel_id=1, source_target_pairs={{0,3},{1,2},{2,1},{3,0},{4,7},{5,6},{6,5},{7,4},{8,11},{9,10},{10,... | collective-permute-start | bytes 196616 | tf_op jit(solution)/shard_map/ppermute | solution.py:323
  79.5 8.6 %collective-permute-start.17 = (bf16[32,1024]{1,0:T(8,128)(2,1)S(1)}, bf16[32,1024]{1,0:T(8,128)(2,1)S(1)}, u32[]{:S(2)}, u32[]{:S(2)}) collective-permute-start(bf16[32,1024]{1,0:T(8,128)(2,1)S(1)} %add_split.3.refs_0_), channel_id=1, source_target_pairs={{0,12},{1,13},{2,14},{3,15},{4,8},{5,9},{6,10},{7,11},{8,4},{9,5},... | collective-permute-start | bytes 196616 | tf_op jit(solution)/shard_map/ppermute | solution.py:323
  81.9 6.2 %collective-permute-start.16 = (bf16[32,1024]{1,0:T(8,128)(2,1)S(1)}, bf16[32,1024]{1,0:T(8,128)(2,1)S(1)}, u32[]{:S(2)}, u32[]{:S(2)}) collective-permute-start(bf16[32,1024]{1,0:T(8,128)(2,1)S(1)} %add_split.3.refs_0_), channel_id=1, source_target_pairs={{0,8},{1,9},{2,10},{3,11},{4,12},{5,13},{6,14},{7,15},{8,0},{9,1},... | collective-permute-start | bytes 196616 | tf_op jit(solution)/shard_map/ppermute | solution.py:323
  88.1 9.4 %collective-permute-start.23 = (bf16[96,1024]{1,0:T(8,128)(2,1)S(1)}, bf16[96,1024]{1,0:T(8,128)(2,1)S(1)}, u32[]{:S(2)}, u32[]{:S(2)}) collective-permute-start(bf16[96,1024]{1,0:T(8,128)(2,1)S(1)} %constant_dynamic-update-slice_fusion.3.refs_1_), channel_id=1, source_target_pairs={{0,3},{1,2},{2,1},{3,0},{4,7},{5,6},{6,5},{7,4},{8,11},{9,10},{10,... | collective-permute-start | bytes 589832 | tf_op jit(solution)/shard_map/ppermute | solution.py:323
  90.5 7.1 %collective-permute-start.21 = (bf16[96,1024]{1,0:T(8,128)(2,1)S(1)}, bf16[96,1024]{1,0:T(8,128)(2,1)S(1)}, u32[]{:S(2)}, u32[]{:S(2)}) collective-permute-start(bf16[96,1024]{1,0:T(8,128)(2,1)S(1)} %constant_dynamic-update-slice_fusion.3.refs_1_), channel_id=1, source_target_pairs={{0,2},{1,3},{2,0},{3,1},{4,6},{5,7},{6,4},{7,5},{8,10},{9,11},{10,... | collective-permute-start | bytes 589832 | tf_op jit(solution)/shard_map/ppermute | solution.py:323
  91.0 6.5 %collective-permute-start.19 = (bf16[96,1024]{1,0:T(8,128)(2,1)S(1)}, bf16[96,1024]{1,0:T(8,128)(2,1)S(1)}, u32[]{:S(2)}, u32[]{:S(2)}) collective-permute-start(bf16[96,1024]{1,0:T(8,128)(2,1)S(1)} %constant_dynamic-update-slice_fusion.3.refs_1_), channel_id=1, source_target_pairs={{0,1},{1,0},{2,3},{3,2},{4,5},{5,4},{6,7},{7,6},{8,9},{9,8},{10,11... | collective-permute-start | bytes 589832 | tf_op jit(solution)/shard_map/ppermute | solution.py:323
  91.7 5.9 %collective-permute-start.20 = (bf16[32,1024]{1,0:T(8,128)(2,1)S(1)}, bf16[32,1024]{1,0:T(8,128)(2,1)S(1)}, u32[]{:S(2)}, u32[]{:S(2)}) collective-permute-start(bf16[32,1024]{1,0:T(8,128)(2,1)S(1)} %add_split.3.refs_0_), channel_id=1, source_target_pairs={{0,2},{1,3},{2,0},{3,1},{4,6},{5,7},{6,4},{7,5},{8,10},{9,11},{10,... | collective-permute-start | bytes 196616 | tf_op jit(solution)/shard_map/ppermute | solution.py:323
  93.1 4.5 %collective-permute-start.18 = (bf16[32,1024]{1,0:T(8,128)(2,1)S(1)}, bf16[32,1024]{1,0:T(8,128)(2,1)S(1)}, u32[]{:S(2)}, u32[]{:S(2)}) collective-permute-start(bf16[32,1024]{1,0:T(8,128)(2,1)S(1)} %add_split.3.refs_0_), channel_id=1, source_target_pairs={{0,1},{1,0},{2,3},{3,2},{4,5},{5,4},{6,7},{7,6},{8,9},{9,8},{10,11... | collective-permute-start | bytes 196616 | tf_op jit(solution)/shard_map/ppermute | solution.py:323
  98.8 2.2 %collective-permute-start.24 = (f32[160,1024]{1,0:T(8,128)S(1)}, f32[160,1024]{1,0:T(8,128)S(1)}, u32[]{:S(2)}, u32[]{:S(2)}) collective-permute-start(f32[160,1024]{1,0:T(8,128)S(1)} %get-tuple-element.23), channel_id=1, source_target_pairs={{0,16},{16,0},{1,17},{17,1},{2,18},{18,2},{3,19},{19,3},{4,20},{20... | collective-permute-start | bytes 1966088 | tf_op jit(solution)/shard_map/ppermute | solution.py:323
